TPU v7x, 32 devices: a whole 2x2x4 slice. The times are simulated.
32 devices in a mesh: obj: 4 (over z), dp: 4 (over x, core), tp: 2 (over y).
Axes of the slice: x: 2, y: 2, z: 4, core: 2. Of those that a mesh axis runs over, the one named last changes fastest.
Arguments:
- hidden_in: bfloat16 [16, 1024, 2048], P(('obj', 'dp'), 'tp'), may hold values from -6 to 6
- cotangent: bfloat16 [16, 1024, 2048], P(('obj', 'dp'), 'tp'), may hold values from -6 to 6
- loss_mask: int32 [16, 1024], P(('obj', 'dp'), 'tp'), may hold values from 0 to 1, as said below
- prefix_len: int32 [16], P(('obj', 'dp')), may hold values from 256 to 1024, as said below
- w_qkv: bfloat16 [2048, 3, 2048], P(None, None, 'tp'), may hold values from -0.1875 to 0.1875
- w_out: bfloat16 [2048, 2048], P('tp'), may hold values from -1 to 1
- gain_one: float32 [2048], replicated, may hold values from 0.5 to 1.5
- bias_one: float32 [2048], replicated, may hold values from -3 to 3
- w_gate_up: bfloat16 [2048, 2, 5632], P(None, None, 'tp'), may hold values from -0.125 to 0.125
- w_down: bfloat16 [5632, 2048], P('tp'), may hold values from -0.625 to 0.625
- gain_two: float32 [2048], replicated, may hold values from 0.5 to 1.5
- bias_two: float32 [2048], replicated, may hold values from -3 to 3
Outputs:
- outputs: bfloat16 [16, 1024, 2048], P(('obj', 'dp'), 'tp')
- input_grad: float32 [16, 1024, 2048], P(('obj', 'dp'), 'tp')
- grad_qkv: float32 [2048, 3, 2048], P(None, None, 'tp')
- grad_out: float32 [2048, 2048], P('tp')
- grad_gain_one: float32 [2048], P('tp')
- grad_bias_one: float32 [2048], P('tp')
- grad_gate_up: float32 [2048, 2, 5632], P(None, None, 'tp')
- grad_down: float32 [5632, 2048], P('tp')
- grad_gain_two: float32 [2048], P('tp')
- grad_bias_two: float32 [2048], P('tp')
Inputs may be any that keep to these rules, and one draw needn't show every extreme that they name: `loss_mask`: group 0 holds MLM chains, whose ones are masked positions (always including the last token of a live chain); the other groups hold GLM chains, whose ones are the tokens at or after prefix_len. Padding chains, the last slots of groups 0 to 2, are all zero. Every group has a one. `prefix_len`: every chain of group 0 has prefix 1024 and attends both ways; GLM chains have prefixes from 256 to 768.
All inputs are finite; a program needn't handle non-finite values.
Results may differ from a plain program's by a relative error of at most 0.017.
The roundings to bfloat16 on the way count: a program that leaves them out, or rounds other values in their place, can miss the bound.
Values may be sent and summed in bfloat16 or wider, within the bound.
A program may use at most 448 MiB of HBM per device.

v0:
```python
import jax
import jax.numpy as jnp
from jax import lax
from jax.sharding import PartitionSpec as P

HEAD_DIM = 128


DEEP_ALPHA = 48.0**0.5
NORM_EPS = 1e-05
MASKED_SCORE = -1e30


def layer_norm(rows_in, norm_gain, norm_bias):
    row_mean = jnp.mean(rows_in, axis=-1, keepdims=True)
    centred = rows_in - row_mean
    variance = jnp.mean(centred * centred, axis=-1, keepdims=True)
    return centred * lax.rsqrt(variance + NORM_EPS) * norm_gain + norm_bias


def rotate(vectors, positions):
    half_dim = vectors.shape[-1] // 2
    frequency = 10000.0 ** (-jnp.arange(half_dim).astype(positions.dtype) / half_dim)
    angles = positions[:, None] * frequency[None, :]
    cos_vals = jnp.cos(angles)[:, None, :]
    sin_vals = jnp.sin(angles)[:, None, :]
    first_half = vectors[..., :half_dim]
    second_half = vectors[..., half_dim:]
    return jnp.concatenate(
        [
            first_half * cos_vals - second_half * sin_vals,
            second_half * cos_vals + first_half * sin_vals,
        ],
        axis=-1,
    )


def geglu(gate_up):
    return jax.nn.gelu(gate_up[:, 0], approximate=False) * gate_up[:, 1]


def allowed_mask(row_start, block_rows, seq_len, prefix_value):
    row_ids = row_start + jnp.arange(block_rows, dtype=jnp.int32)
    col_ids = jnp.arange(seq_len, dtype=jnp.int32)
    return (col_ids[None, :] < prefix_value) | (col_ids[None, :] <= row_ids[:, None])


def body(
    hidden_in,
    cotangent,
    loss_mask,
    prefix_len,
    w_qkv,
    w_out,
    gain_one,
    bias_one,
    w_gate_up,
    w_down,
    gain_two,
    bias_two,
):
    chains, share_len, feature_width = hidden_in.shape
    seq_len = share_len * lax.axis_size("tp")
    local_width = w_qkv.shape[2]
    head_dim = HEAD_DIM
    head_count = local_width // head_dim
    row_count = chains * seq_len
    block_rows = min(512, seq_len)
    block_count = seq_len // block_rows
    score_scale = head_dim ** (-0.5)
    positions = jnp.arange(seq_len, dtype=jnp.float32)
    split_shape = (chains, seq_len, head_count, head_dim)
    whole_x = lax.all_gather(hidden_in, "tp", axis=1, tiled=True).reshape(row_count, feature_width)
    proj_qkv = jnp.einsum("td,dke->tke", whole_x, w_qkv, preferred_element_type=jnp.float32)
    raw_queries = proj_qkv[:, 0].reshape(split_shape)
    queries = rotate(raw_queries, positions).astype(jnp.bfloat16)
    key_rows = rotate(proj_qkv[:, 1].reshape(split_shape), positions).astype(jnp.bfloat16)
    values = proj_qkv[:, 2].reshape(split_shape).astype(jnp.bfloat16)

    def block_scores(item_id):
        chain_id = item_id // block_count
        row_start = item_id % block_count * block_rows
        query_block = lax.dynamic_slice_in_dim(queries[chain_id], row_start, block_rows, 0)
        scores = (
            jnp.einsum(
                "qhe,khe->hqk", query_block, key_rows[chain_id], preferred_element_type=jnp.float32
            )
            * score_scale
        )
        allowed = allowed_mask(row_start, block_rows, seq_len, prefix_len[chain_id])
        return (jnp.where(allowed[None], scores, MASKED_SCORE), chain_id, row_start, query_block)

    def attend(item_id):
        scores, chain_id, row_start, query_block = block_scores(item_id)
        row_max = jnp.max(scores, axis=-1, keepdims=True)
        weights_exp = jnp.exp(scores - row_max)
        row_total = jnp.sum(weights_exp, axis=-1, keepdims=True)
        attn_probs = (weights_exp / row_total).astype(jnp.bfloat16)
        mixed_block = jnp.einsum(
            "hqk,khe->qhe", attn_probs, values[chain_id], preferred_element_type=jnp.float32
        )
        return (mixed_block.astype(jnp.bfloat16), (row_max + jnp.log(row_total))[..., 0])

    item_ids = jnp.arange(chains * block_count, dtype=jnp.int32)
    mixed_blocks, log_totals = lax.map(attend, item_ids)
    mixed_heads = mixed_blocks.reshape(row_count, local_width)
    attn_part = jnp.dot(mixed_heads, w_out, preferred_element_type=jnp.float32).reshape(
        chains, seq_len, feature_width
    )
    attn_here = lax.psum_scatter(attn_part, "tp", scatter_dimension=1, tiled=True)
    z_one = DEEP_ALPHA * hidden_in.astype(jnp.float32) + attn_here
    h_one = layer_norm(z_one, gain_one, bias_one)
    whole_h = lax.all_gather(h_one.astype(jnp.bfloat16), "tp", axis=1, tiled=True).reshape(
        row_count, feature_width
    )
    gate_up = jnp.einsum("td,dke->tke", whole_h, w_gate_up, preferred_element_type=jnp.float32)
    hidden = geglu(gate_up).astype(jnp.bfloat16)
    ffn_part = jnp.dot(hidden, w_down, preferred_element_type=jnp.float32).reshape(
        chains, seq_len, feature_width
    )
    ffn_here = lax.psum_scatter(ffn_part, "tp", scatter_dimension=1, tiled=True)
    z_two = DEEP_ALPHA * h_one + ffn_here
    outputs = layer_norm(z_two, gain_two, bias_two)
    mask_vals = loss_mask.astype(jnp.float32)
    total_count = lax.psum(jnp.sum(mask_vals), ("dp", "tp"))
    grad_y = cotangent.astype(jnp.float32) * (mask_vals * (seq_len / total_count))[..., None]
    norm_back_two = jax.vjp(layer_norm, z_two, gain_two, bias_two)[1]
    d_z_two, d_gain_two, d_bias_two = norm_back_two(grad_y)
    d_ffn = lax.all_gather(d_z_two.astype(jnp.bfloat16), "tp", axis=1, tiled=True).reshape(
        row_count, feature_width
    )
    grad_down = jnp.einsum("tf,td->fd", hidden, d_ffn, preferred_element_type=jnp.float32)
    d_hidden = jnp.einsum("td,fd->tf", d_ffn, w_down, preferred_element_type=jnp.float32)
    d_gate_up = jax.vjp(geglu, gate_up)[1](d_hidden)[0].astype(jnp.bfloat16)
    grad_gate_up = jnp.einsum("td,tke->dke", whole_h, d_gate_up, preferred_element_type=jnp.float32)
    d_h_part = jnp.einsum(
        "tke,dke->td", d_gate_up, w_gate_up, preferred_element_type=jnp.float32
    ).reshape(chains, seq_len, feature_width)
    d_h_here = lax.psum_scatter(d_h_part, "tp", scatter_dimension=1, tiled=True)
    norm_back_one = jax.vjp(layer_norm, z_one, gain_one, bias_one)[1]
    d_z_one, d_gain_one, d_bias_one = norm_back_one(DEEP_ALPHA * d_z_two + d_h_here)
    d_attn = lax.all_gather(d_z_one.astype(jnp.bfloat16), "tp", axis=1, tiled=True).reshape(
        row_count, feature_width
    )
    grad_out = jnp.einsum("tf,td->fd", mixed_heads, d_attn, preferred_element_type=jnp.float32)
    d_mixed = (
        jnp.einsum("td,fd->tf", d_attn, w_out, preferred_element_type=jnp.float32)
        .astype(jnp.bfloat16)
        .reshape(split_shape)
    )

    def attend_back(item_id):
        scores, chain_id, row_start, query_block = block_scores(item_id)
        probs_full = jnp.exp(scores - log_totals[item_id][..., None])
        grad_block = lax.dynamic_slice_in_dim(d_mixed[chain_id], row_start, block_rows, 0)
        d_probs = jnp.einsum(
            "qhe,khe->hqk", grad_block, values[chain_id], preferred_element_type=jnp.float32
        )
        delta_rows = jnp.sum(probs_full * d_probs, axis=-1, keepdims=True)
        d_scores = (probs_full * (d_probs - delta_rows)).astype(jnp.bfloat16)
        d_query = (
            jnp.einsum(
                "hqk,khe->qhe", d_scores, key_rows[chain_id], preferred_element_type=jnp.float32
            )
            * score_scale
        )
        d_key = (
            jnp.einsum("hqk,qhe->khe", d_scores, query_block, preferred_element_type=jnp.float32)
            * score_scale
        )
        d_value = jnp.einsum(
            "hqk,qhe->khe",
            probs_full.astype(jnp.bfloat16),
            grad_block,
            preferred_element_type=jnp.float32,
        )
        return (d_query, d_key, d_value)

    d_query_blocks, d_key_parts, d_value_parts = lax.map(attend_back, item_ids)
    d_queries = d_query_blocks.reshape(split_shape)
    part_shape = (chains, block_count, seq_len, head_count, head_dim)
    d_keys = d_key_parts.reshape(part_shape).sum(axis=1)
    d_values = d_value_parts.reshape(part_shape).sum(axis=1)

    def rotate_chains(vectors):
        return rotate(vectors, positions)

    rotate_back = jax.vjp(rotate_chains, raw_queries)[1]
    d_qkv = jnp.stack(
        [
            rotate_back(d_queries)[0].reshape(row_count, local_width),
            rotate_back(d_keys)[0].reshape(row_count, local_width),
            d_values.reshape(row_count, local_width),
        ],
        axis=1,
    ).astype(jnp.bfloat16)
    grad_qkv = jnp.einsum("td,tke->dke", whole_x, d_qkv, preferred_element_type=jnp.float32)
    d_x_part = jnp.einsum("tke,dke->td", d_qkv, w_qkv, preferred_element_type=jnp.float32).reshape(
        chains, seq_len, feature_width
    )
    norm_terms = jnp.stack([d_gain_one, d_bias_one, d_gain_two, d_bias_two])
    d_x_here, norm_here = (
        lax.psum_scatter(d_x_part, "tp", scatter_dimension=1, tiled=True),
        lax.psum_scatter(norm_terms, "tp", scatter_dimension=1, tiled=True),
    )
    input_grad = DEEP_ALPHA * d_z_one + d_x_here
    weight_grads = (grad_qkv, grad_out, grad_gate_up, grad_down, norm_here.T)
    weight_grads = lax.psum(
        (weight_grads[0], weight_grads[1], weight_grads[2], weight_grads[3], weight_grads[4]),
        ("obj", "dp"),
    )
    grad_qkv, grad_out, grad_gate_up, grad_down, norm_cols = weight_grads
    return (
        outputs.astype(jnp.bfloat16),
        input_grad,
        grad_qkv,
        grad_out,
        norm_cols[:, 0],
        norm_cols[:, 1],
        grad_gate_up,
        grad_down,
        norm_cols[:, 2],
        norm_cols[:, 3],
    )


def solution(mesh):
    return jax.shard_map(
        body,
        mesh=mesh,
        in_specs=(
            P(("obj", "dp"), "tp", None),
            P(("obj", "dp"), "tp", None),
            P(("obj", "dp"), "tp"),
            P(("obj", "dp")),
            P(None, None, "tp"),
            P("tp", None),
            P(),
            P(),
            P(None, None, "tp"),
            P("tp", None),
            P(),
            P(),
        ),
        out_specs=(
            P(("obj", "dp"), "tp", None),
            P(("obj", "dp"), "tp", None),
            P(None, None, "tp"),
            P("tp", None),
            P("tp"),
            P("tp"),
            P(None, None, "tp"),
            P("tp", None),
            P("tp"),
            P("tp"),
        ),
        check_vma=False,
    )
```

profile of v0, /device:TPU:0, one launch (start us, length us, event | category | flops | bytes accessed | tf_op | source)
XLA Modules:
  0.0 2938.4 jit_solution(17761213509327280699)
XLA Ops:
  9.0 60.0 %all-gather.5.cloned.1.call-done = bf16[1,1024,2048]{2,1,0:T(8,128)(2,1)} async-done(((bf16[1,512,2048]{2,1,0:T(8,128)(2,1)}), bf16[1,1024,2048]{2,1,0:T(8,128)(2,1)}) %all-gather.5.cloned.1.call-update) | async-done | bytes 4194320 | tf_op jit(solution)/shard_map/all_gather | solution.py:73
  69.0 17.9 fusion.128
  106.2 40.9 %while.30 = (s32[]{:T(128)}, bf16[2,512,8,128]{3,2,1,0:T(8,128)(2,1)}, f32[2,8,512]{2,1,0:T(8,128)S(1)}, s32[1]{0:T(128)}, s32[2]{0:T(128)S(1)}, /*index=5*/bf16...) while((s32[]{:T(128)}, ...), condition=%wide.region_3.4_spmd, body=%wide.region_0.3_spmd.sunk | while | flops 2199385600 | bytes 86120848 | solution.py:105
  147.1 11.5 convolution_bitcast_fusion.1
  158.7 99.4 %reduce-scatter.8.cloned.1.call-done = f32[1,512,2048]{2,1,0:T(8,128)} async-done(((f32[1,1024,2048]{2,1,0:T(8,128)}), f32[1,512,2048]{2,1,0:T(8,128)}) %reduce-scatter.8.cloned.1.call-update) | async-done | bytes 4194320 | tf_op jit(solution)/shard_map/reduce_scatter | solution.py:110
  265.1 56.8 %all-gather.7.cloned.1.call-done = bf16[1,1024,2048]{2,1,0:T(8,128)(2,1)} async-done(((bf16[1,512,2048]{2,1,0:T(8,128)(2,1)}), bf16[1,1024,2048]{2,1,0:T(8,128)(2,1)}) %all-gather.7.cloned.1.call-update) | async-done | bytes 4194320 | tf_op jit(solution)/shard_map/all_gather | solution.py:113
  321.9 34.8 %fusion.44 = f32[1024,2,2816]{2,0,1:T(8,128)} fusion(bf16[2048,2,2816]{2,1,0:T(2,128)(2,1)} %param.24, bf16[1,1024,2048]{2,1,0:T(8,128)(2,1)} %all-gather.7.cloned.1.call-done), kind=kOutput, calls=%fused_computation.56 | convolution fusion | flops 23622320128 | bytes 50331648 | tf_op jit(solution)/shard_map/td,dke->tke/dot_general | solution.py:116
  356.8 25.9 fusion.46
  382.6 27.2 fusion.111
  411.1 13.4 psum.42
  425.3 84.5 %reduce-scatter.10.cloned.1.call-done = f32[1,512,2048]{2,1,0:T(8,128)} async-done(((f32[1,1024,2048]{2,1,0:T(8,128)}), f32[1,512,2048]{2,1,0:T(8,128)}) %reduce-scatter.10.cloned.1.call-update) | async-done | bytes 4194320 | tf_op jit(solution)/shard_map/reduce_scatter | solution.py:121
  524.0 56.8 %all-gather.9.cloned.1.call-done = bf16[1,1024,2048]{2,1,0:T(8,128)(2,1)} async-done(((bf16[1,512,2048]{2,1,0:T(8,128)(2,1)}), bf16[1,1024,2048]{2,1,0:T(8,128)(2,1)}) %all-gather.9.cloned.1.call-update) | async-done | bytes 4194320 | tf_op jit(solution)/shard_map/all_gather | solution.py:129
  580.8 30.8 %multiply_bitcast_fusion.1 = (f32[1024,1,2816]{2,0,1:T(8,128)}, f32[1024,1,2816]{2,0,1:T(8,128)}) fusion(f32[1024,2816]{1,0:T(8,128)} %fusion.46, f32[1024,2,2816]{2,0,1:T(8,128)} %fusion.44, bf16[2816,2048]{1,0:T(8,128)(2,1)} %param.25, bf16[1,1024,2048]{2,1,0:T(8,128)(2,1)} %all-gather.9.cloned.1.call-done), kind=kOutput, calls=%fused_computation.93 | convolution fusion | flops 11857297408 | bytes 73400320 | tf_op jit(solution)/shard_map/td,fd->tf/dot_general | solution.py:133
  611.6 35.7 %fusion.114 = f32[1,1024,2048]{2,1,0:T(8,128)} fusion(bf16[2048,2,2816]{2,1,0:T(2,128)(2,1)} %param.24, f32[1024,1,2816]{2,0,1:T(8,128)} %get-tuple-element.407, f32[1024,1,2816]{2,0,1:T(8,128)} %get-tuple-element.406), kind=kOutput, calls=%fused_computation.147 | convolution fusion | flops 23633854464 | bytes 54525952 | tf_op jit(solution)/shard_map/tke,dke->td/dot_general | solution.py:136
  647.4 99.4 %reduce-scatter.12.cloned.1.call-done = f32[1,512,2048]{2,1,0:T(8,128)} async-done(((f32[1,1024,2048]{2,1,0:T(8,128)}), f32[1,512,2048]{2,1,0:T(8,128)}) %reduce-scatter.12.cloned.1.call-update) | async-done | bytes 4194320 | tf_op jit(solution)/shard_map/reduce_scatter | solution.py:139
  759.2 55.3 %all-gather.11.cloned.1.call-done = bf16[1,1024,2048]{2,1,0:T(8,128)(2,1)} async-done(((bf16[1,512,2048]{2,1,0:T(8,128)(2,1)}), bf16[1,1024,2048]{2,1,0:T(8,128)(2,1)}) %all-gather.11.cloned.1.call-update) | async-done | bytes 4194320 | tf_op jit(solution)/shard_map/all_gather | solution.py:142
  823.9 129.0 %while.31 = (s32[]{:T(128)}, f32[2,512,8,128]{3,2,1,0:T(8,128)}, f32[2,1024,8,128]{1,3,2,0:T(8,128)}, f32[2,1024,8,128]{1,3,2,0:T(8,128)}, s32[1]{0:T(128)}, /*i...) while((s32[]{:T(128)}, f32[2,512,8,128]{3,2,1,0:T(8,128)}, ...), condition=%wide.region_19.20_spmd, body=%wide.region_17.19_spmd.sunk | while | flops 5409076736 | bytes 294738496 | solution.py:179
  839.6 12.7 multiply_reduce_fusion.8
  852.2 15.0 multiply_convert_fusion.2
  893.3 10.6 fusion.224
  903.9 12.7 multiply_reduce_fusion.8
  916.6 15.0 multiply_convert_fusion.2
  1000.6 19.9 convolution_bitcast_fusion.2
  1020.6 38.0 %fusion.124 = f32[2048,2,2816]{2,0,1:T(8,128)} fusion(bf16[1,1024,2048]{2,1,0:T(8,128)(2,1)} %all-gather.7.cloned.1.call-done, f32[1024,1,2816]{2,0,1:T(8,128)} %get-tuple-element.407, f32[1024,1,2816]{2,0,1:T(8,128)} %get-tuple-element.406), kind=kOutput, calls=%fused_computation.157 | convolution fusion | flops 23633854464 | bytes 73400320 | tf_op jit(solution)/shard_map/td,tke->dke/dot_general | solution.py:135
  1058.6 46.2 %fusion.79 = f32[2816,2048]{1,0:T(8,128)} fusion(f32[1024,2,2816]{2,0,1:T(8,128)} %fusion.44, bf16[1,1024,2048]{2,1,0:T(8,128)(2,1)} %all-gather.9.cloned.1.call-done), kind=kOutput, calls=%fused_computation.114 | convolution fusion | flops 12001476608 | bytes 50331648 | tf_op jit(solution)/shard_map/tf,td->fd/dot_general | solution.py:132
  1104.9 10.9 fusion.117
  1115.8 17.0 convolution_bitcast_fusion
  1134.2 64.4 %psum.45 = f32[1024,4]{0,1:T(4,128)S(1)} all-reduce(f32[1024,4]{0,1:T(4,128)S(1)} %bitcast.292), channel_id=1, replica_groups=mesh['obj'=4,'dp'=4,'tp'=2] {'obj','dp'}, use_global_device_ids=true, to_apply=%region_30.31 | all-reduce | flops 4096 | bytes 32768 | tf_op jit(solution)/shard_map/psum | solution.py:208
  1205.4 1605.9 %all-reduce.9.cloned.1.call-done = (f32[2048,3,1024]{0,2,1:T(8,128)}, f32[1024,2048]{1,0:T(8,128)}, f32[2048,2,2816]{2,0,1:T(8,128)}, f32[2816,2048]{1,0:T(8,128)}) async-done(((f32[2048,3,1024]{0,2,1:T(8,128)}, f32[1024,2048]{1,0:T(8,128)}, f32[2048,2,2816]{2,0,1:T(8,128)}, f32[2816,2048]{1,0:T(8,128)}), (f32[2048,3,1024]{0,2,1:T(8,128)}, f32[1024,2048]{1,0:T(8,128)}, f32[2048,2,2816]{2,0,1:T(8,128)}, ...) | async-done | bytes 102760464 | tf_op jit(solution)/shard_map/psum | solution.py:208
  2811.3 24.7 copy.83
  2836.0 75.2 %copy.84 = f32[2048,2,2816]{2,1,0:T(2,128)} copy(f32[2048,2,2816]{2,0,1:T(8,128)} %get-tuple-element.391) | data formatting | bytes 92274688
  2914.6 16.6 copy.176
  (210 shorter events, 217.0 us)
Async XLA Ops:
  7.2 61.8 %all-gather.5.cloned.1.call-start = ((), (), s32[]{:S(2)}) async-start(), calls=%async_computation.5 | async-start | bytes 6291456 | tf_op jit(solution)/shard_map/all_gather | solution.py:73
  7.9 250.2 %reduce-scatter.8.cloned.1.call-start = ((), (), s32[]{:S(2)}) async-start(), calls=%async_computation.6 | async-start | bytes 12582912 | tf_op jit(solution)/shard_map/reduce_scatter | solution.py:110
  9.0 84.9 %copy-start.15 = (f32[1024,64]{0,1:T(8,128)}, f32[1024,64]{0,1:T(8,128)S(1)}, u32[]{:S(2)}) copy-start(f32[1024,64]{0,1:T(8,128)S(1)} %get-tuple-element.429) | copy-start | bytes 786436
  9.0 84.9 %copy-start.17 = (f32[1024,64]{0,1:T(8,128)}, f32[1024,64]{0,1:T(8,128)S(1)}, u32[]{:S(2)}) copy-start(f32[1024,64]{0,1:T(8,128)S(1)} %get-tuple-element.430) | copy-start | bytes 786436
  147.1 11.5 copy-start.1
  147.1 11.5 copy-start.21
  158.6 99.5 %copy-start.14 = (bf16[1,512,2048]{2,1,0:T(8,128)(2,1)S(1)}, bf16[1,512,2048]{2,1,0:T(8,128)(2,1)}, u32[]{:S(2)}) copy-start(bf16[1,512,2048]{2,1,0:T(8,128)(2,1)} %param.16) | copy-start | bytes 6291460
  158.6 104.3 %copy-start.23 = (f32[2048]{0:T(1024)S(1)}, f32[2048]{0:T(1024)}, u32[]{:S(2)}) copy-start(f32[2048]{0:T(1024)} %param.22) | copy-start | bytes 24580
  158.6 104.3 %copy-start.24 = (f32[2048]{0:T(1024)S(1)}, f32[2048]{0:T(1024)}, u32[]{:S(2)}) copy-start(f32[2048]{0:T(1024)} %param.23) | copy-start | bytes 24580
  158.6 163.3 %all-gather.7.cloned.1.call-start = ((), (), s32[]{:S(2)}) async-start(), calls=%async_computation.7 | async-start | bytes 6291456 | tf_op jit(solution)/shard_map/all_gather | solution.py:113
  265.0 244.7 %reduce-scatter.10.cloned.1.call-start = ((), (), s32[]{:S(2)}) async-start(), calls=%async_computation.8 | async-start | bytes 12582912 | tf_op jit(solution)/shard_map/reduce_scatter | solution.py:121
  409.9 171.0 %all-gather.9.cloned.1.call-start = ((), (), s32[]{:S(2)}) async-start(), calls=%async_computation.9 | async-start | bytes 6291456 | tf_op jit(solution)/shard_map/all_gather | solution.py:129
  425.3 89.7 %copy-start.13 = (bf16[1,512,2048]{2,1,0:T(8,128)(2,1)S(1)}, bf16[1,512,2048]{2,1,0:T(8,128)(2,1)}, u32[]{:S(2)}) copy-start(bf16[1,512,2048]{2,1,0:T(8,128)(2,1)} %param.17) | copy-start | bytes 6291460
  425.3 89.7 %copy-start.25 = (f32[2048]{0:T(1024)S(1)}, f32[2048]{0:T(1024)}, u32[]{:S(2)}) copy-start(f32[2048]{0:T(1024)} %param.26) | copy-start | bytes 24580
  524.0 222.8 %reduce-scatter.12.cloned.1.call-start = ((), (), s32[]{:S(2)}) async-start(), calls=%async_computation.10 | async-start | bytes 12582912 | tf_op jit(solution)/shard_map/reduce_scatter | solution.py:139
  647.3 105.5 %copy-start.27 = (f32[512]{0:T(512)S(1)}, f32[512]{0:T(512)}, u32[]{:S(2)}) copy-start(f32[512]{0:T(512)} %copy-done.26) | copy-start | bytes 6148
  647.3 167.2 %all-gather.11.cloned.1.call-start = ((), (), s32[]{:S(2)}) async-start(), calls=%async_computation.11 | async-start | bytes 6291456 | tf_op jit(solution)/shard_map/all_gather | solution.py:142
  754.1 69.8 %copy-start.28 = (f32[512]{0:T(512)}, f32[512]{0:T(512)S(1)}, u32[]{:S(2)}) copy-start(f32[512]{0:T(512)S(1)} %negate_multiply_fusion.1) | copy-start | bytes 6148
  757.6 375.3 %reduce-scatter.16.cloned.1.call-start = ((), (), s32[]{:S(2)}) async-start(), calls=%async_computation.13 | async-start | bytes 1572864
  759.1 64.7 %copy-start.2 = (bf16[1,1024,8,128]{3,1,2,0:T(8,128)(2,1)S(1)}, bf16[1,1024,8,128]{3,1,2,0:T(8,128)(2,1)}, u32[]{:S(2)}) copy-start(bf16[1,1024,8,128]{3,1,2,0:T(8,128)(2,1)} %copy-done.1) | copy-start | bytes 6291460
  759.1 64.7 %copy-start.22 = (f32[2,8,512]{2,1,0:T(8,128)S(1)}, f32[2,8,512]{2,1,0:T(8,128)}, u32[]{:S(2)}) copy-start(f32[2,8,512]{2,1,0:T(8,128)} %copy-done.21) | copy-start | bytes 98308
  759.1 440.1 %reduce-scatter.14.cloned.1.call-start = ((), (), s32[]{:S(2)}) async-start(), calls=%async_computation.12 | async-start | bytes 12582912 | tf_op jit(solution)/shard_map/reduce_scatter | solution.py:203
  852.2 18.4 copy-start
  870.7 10.7 slice-start
  916.6 18.4 copy-start
  935.0 10.8 slice-start
  1020.6 1790.7 %all-reduce.9.cloned.1.call-start = ((), (), s32[]{:S(2)}) async-start(), calls=%async_computation.14 | async-start | bytes 205520896 | tf_op jit(solution)/shard_map/psum | solution.py:208
  1104.9 11.0 copy-start.19
  1104.9 11.0 copy-start.20
  1104.9 11.0 copy-start.32
  1132.9 66.3 %copy-start.29 = (f32[512]{0:T(512)S(1)}, f32[512]{0:T(512)}, u32[]{:S(2)}) copy-start(f32[512]{0:T(512)} %copy-done.28) | copy-start | bytes 6148
  2836.0 75.2 %copy-start.12 = (f32[1024,2048]{1,0:T(8,128)S(1)}, f32[1024,2048]{1,0:T(8,128)}, u32[]{:S(2)}) copy-start(f32[1024,2048]{1,0:T(8,128)} %get-tuple-element.647) | copy-start | bytes 25165828
  (25 other events, 111.0 us)
Sparse Core Ops, SparseCore 0:
  9.5 59.4 all-gather.4
  158.7 99.2 reduce-scatter.7
  265.1 56.7 all-gather.6
  410.0 99.7 reduce-scatter.9
  524.1 56.6 all-gather.8
  647.4 99.3 reduce-scatter.11
  757.8 56.7 all-gather.10
  816.8 20.3 reduce-scatter.15
  1020.7 99.3 reduce-scatter.13
  1133.0 1678.2 all-reduce.8
where the time goes:
time: 2950 us; the launch traced here: 2940 us
  waiting for transfers between devices  2120 us (72%)
  matrix products  395 us (13%)
  local copies, waits for them, and re-layouts  187 us (6%)
  other arithmetic  133 us (5%)
  blocking collectives  77.9 us (3%)
    psum x1, waiting for transfers between devices, body(): lax.psum((weight_grads[0], weight_grads[1], weight_grads[2], weight_grads...  1610 us
    unnamed x62, local copies, waits for them, and re-layouts  136 us
    reduce_scatter x1, waiting for transfers between devices, body(): d_h_here = lax.psum_scatter(d_h_part, 'tp', scatter_dimension=1, tiled=True)  99.4 us
    reduce_scatter x1, waiting for transfers between devices, body(): lax.psum_scatter(attn_part, 'tp', scatter_dimension=1, tiled=True)  99.4 us
    reduce_scatter x1, waiting for transfers between devices, body(): ffn_here = lax.psum_scatter(ffn_part, 'tp', scatter_dimension=1, tiled=True)  84.5 us
    psum x1, blocking collectives, body(): lax.psum((weight_grads[0], weight_grads[1], weight_grads[2], weight_grads...  64.4 us
    all_gather x1, waiting for transfers between devices, body(): lax.all_gather(hidden_in, 'tp', axis=1, tiled=True)  60 us
  transfers between devices with their start and end apart: 10, of which 8 were waited for; matrix products, arithmetic and copies ran while one was open for 11% of the time, Pallas kernels for 0%

commit v1 on v0

v1 whole, which is shorter than its diff:
```python
import functools

import jax
import jax.numpy as jnp
from jax import lax
from jax.experimental import pallas as pl
from jax.experimental.pallas import tpu as pltpu
from jax.sharding import PartitionSpec as P

HEAD_DIM = 128
DEEP_ALPHA = 48.0**0.5
NORM_EPS = 1e-05
MASKED_SCORE = -1e30
F32 = jnp.float32
BF16 = jnp.bfloat16
VMEM_BYTES = 60 * 1024 * 1024


def rotated(block, cos_ref, sin_ref, sign):
    half = block.shape[-1] // 2
    return block * cos_ref[...] + sign * (pltpu.roll(block, half, 1) * sin_ref[...])


def row_limits(info_ref, start, rows, seq_len):
    row_ids = lax.broadcasted_iota(jnp.int32, (1, rows), 1) + start + info_ref[0]
    row_ids = jnp.where(row_ids >= seq_len, row_ids - seq_len, row_ids)
    return jnp.maximum(row_ids, info_ref[1] - 1)


def key_ids(info_ref, seq_len):
    ids = lax.broadcasted_iota(jnp.int32, (seq_len, 1), 0) + info_ref[0]
    return jnp.where(ids >= seq_len, ids - seq_len, ids)


def attend_kernel(
    block_rows, info_ref, own_ref, other_ref, cos_ref, sin_ref, mixed_ref, qkv_ref
):
    share_len = own_ref.shape[1]
    seq_len = mixed_ref.shape[0]
    scale = HEAD_DIM**-0.5
    for part in range(3):
        block = jnp.concatenate([own_ref[part], other_ref[part]], axis=0)
        if part < 2:
            block = rotated(block, cos_ref, sin_ref, 1.0)
        qkv_ref[part] = block.astype(BF16)
    keys = qkv_ref[1]
    values = qkv_ref[2]
    ids = key_ids(info_ref, seq_len)
    for start in range(0, seq_len, block_rows):
        queries = qkv_ref[0, start : start + block_rows, :]
        scores = (
            lax.dot_general(keys, queries, (((1,), (1,)), ((), ())), preferred_element_type=F32)
            * scale
        )
        limits = row_limits(info_ref, start, block_rows, seq_len)
        scores = jnp.where(ids <= limits, scores, MASKED_SCORE)
        row_max = jnp.max(scores, axis=0, keepdims=True)
        weights = jnp.exp(scores - row_max)
        total = jnp.sum(weights, axis=0, keepdims=True)
        probs = (weights * (1.0 / total)).astype(BF16)
        mixed = lax.dot_general(
            probs, values, (((0,), (0,)), ((), ())), preferred_element_type=F32
        )
        mixed_ref[start : start + block_rows, :] = mixed.astype(BF16)


def attend_back_kernel(
    block_rows, info_ref, qkv_ref, grad_ref, cos_ref, sin_ref, out_ref, d_key_ref, d_value_ref
):
    seq_len = grad_ref.shape[0]
    scale = HEAD_DIM**-0.5
    keys = qkv_ref[1]
    values = qkv_ref[2]
    ids = key_ids(info_ref, seq_len)
    for start in range(0, seq_len, block_rows):
        rows = slice(start, start + block_rows)
        queries = qkv_ref[0, rows, :]
        grads = grad_ref[rows, :]
        scores = (
            lax.dot_general(keys, queries, (((1,), (1,)), ((), ())), preferred_element_type=F32)
            * scale
        )
        limits = row_limits(info_ref, start, block_rows, seq_len)
        scores = jnp.where(ids <= limits, scores, MASKED_SCORE)
        row_max = jnp.max(scores, axis=0, keepdims=True)
        weights = jnp.exp(scores - row_max)
        total = jnp.sum(weights, axis=0, keepdims=True)
        probs = weights * (1.0 / total)
        d_probs = lax.dot_general(
            values, grads, (((1,), (1,)), ((), ())), preferred_element_type=F32
        )
        delta = jnp.sum(probs * d_probs, axis=0, keepdims=True)
        d_scores = (probs * (d_probs - delta)).astype(BF16)
        d_value = jnp.dot(probs.astype(BF16), grads, preferred_element_type=F32)
        d_key = jnp.dot(d_scores, queries, preferred_element_type=F32)
        if start == 0:
            d_value_ref[...] = d_value
            d_key_ref[...] = d_key
        else:
            d_value_ref[...] += d_value
            d_key_ref[...] += d_key
        d_query = (
            lax.dot_general(d_scores, keys, (((0,), (0,)), ((), ())), preferred_element_type=F32)
            * scale
        )
        d_query = d_query * cos_ref[rows, :] - (
            pltpu.roll(d_query, HEAD_DIM // 2, 1) * sin_ref[rows, :]
        )
        out_ref[0, rows, :] = d_query.astype(BF16)
    d_key = d_key_ref[...] * scale
    out_ref[1] = rotated(d_key, cos_ref, sin_ref, -1.0).astype(BF16)
    out_ref[2] = d_value_ref[...].astype(BF16)


def attend(info, own, other, cos_vals, sin_vals):
    share_len, local_width = own.shape[1:]
    seq_len = share_len + other.shape[1]
    heads = local_width // HEAD_DIM
    table = pl.BlockSpec((seq_len, HEAD_DIM), lambda h, info: (0, 0))
    return pl.pallas_call(
        functools.partial(attend_kernel, min(256, seq_len)),
        grid_spec=pltpu.PrefetchScalarGridSpec(
            num_scalar_prefetch=1,
            grid=(heads,),
            in_specs=[
                pl.BlockSpec((3, share_len, HEAD_DIM), lambda h, info: (0, 0, h)),
                pl.BlockSpec((3, seq_len - share_len, HEAD_DIM), lambda h, info: (0, 0, h)),
                table,
                table,
            ],
            out_specs=[
                pl.BlockSpec((seq_len, HEAD_DIM), lambda h, info: (0, h)),
                pl.BlockSpec((3, seq_len, HEAD_DIM), lambda h, info: (0, 0, h)),
            ],
        ),
        out_shape=[
            jax.ShapeDtypeStruct((seq_len, local_width), BF16),
            jax.ShapeDtypeStruct((3, seq_len, local_width), BF16),
        ],
        compiler_params=pltpu.CompilerParams(vmem_limit_bytes=VMEM_BYTES),
        cost_estimate=pl.CostEstimate(
            flops=8 * seq_len * seq_len * local_width,
            bytes_accessed=seq_len * local_width * 20,
            transcendentals=seq_len * seq_len * heads,
        ),
        name="attend",
    )(info, own, other, cos_vals, sin_vals)


def attend_back(info, qkv, grads, cos_vals, sin_vals):
    seq_len, local_width = grads.shape
    heads = local_width // HEAD_DIM
    table = pl.BlockSpec((seq_len, HEAD_DIM), lambda h, info: (0, 0))
    return pl.pallas_call(
        functools.partial(attend_back_kernel, min(256, seq_len)),
        grid_spec=pltpu.PrefetchScalarGridSpec(
            num_scalar_prefetch=1,
            grid=(heads,),
            in_specs=[
                pl.BlockSpec((3, seq_len, HEAD_DIM), lambda h, info: (0, 0, h)),
                pl.BlockSpec((seq_len, HEAD_DIM), lambda h, info: (0, h)),
                table,
                table,
            ],
            out_specs=pl.BlockSpec((3, seq_len, HEAD_DIM), lambda h, info: (0, 0, h)),
            scratch_shapes=[
                pltpu.VMEM((seq_len, HEAD_DIM), F32),
                pltpu.VMEM((seq_len, HEAD_DIM), F32),
            ],
        ),
        out_shape=jax.ShapeDtypeStruct((3, seq_len, local_width), BF16),
        compiler_params=pltpu.CompilerParams(vmem_limit_bytes=VMEM_BYTES),
        cost_estimate=pl.CostEstimate(
            flops=20 * seq_len * seq_len * local_width,
            bytes_accessed=seq_len * local_width * 14,
            transcendentals=seq_len * seq_len * heads,
        ),
        name="attend_back",
    )(info, qkv, grads, cos_vals, sin_vals)


def gather_rows(own):
    size = lax.axis_size("tp")
    if size == 2:
        return lax.ppermute(own, "tp", [(0, 1), (1, 0)])
    share = own.shape[0]
    whole = lax.all_gather(own, "tp", axis=0, tiled=True)
    start = (lax.axis_index("tp") + 1) * share
    return lax.dynamic_slice_in_dim(
        jnp.concatenate([whole, whole], axis=0), start, (size - 1) * share, 0
    )


def scatter_rows(own_part, send_part):
    size = lax.axis_size("tp")
    if size == 2:
        return own_part + lax.ppermute(send_part, "tp", [(0, 1), (1, 0)]).astype(F32)
    share = own_part.shape[0]
    ring = jnp.concatenate([own_part.astype(BF16), send_part] * 2, axis=0)
    start = (size - lax.axis_index("tp")) * share
    whole = lax.dynamic_slice_in_dim(ring, start, size * share, 0)
    return lax.psum_scatter(whole.astype(F32), "tp", scatter_dimension=0, tiled=True)


def all_sum(value, axes):
    for axis in axes:
        size = lax.axis_size(axis)
        step = 1
        while step < size:
            value = value + lax.ppermute(value, axis, [(i, i ^ step) for i in range(size)])
            step *= 2
    return value


CORE_SWAP = [(0, 1), (1, 0), (2, 3), (3, 2)]
X_SWAP = [(0, 2), (2, 0), (1, 3), (3, 1)]
INWARD = [(0, 1), (3, 2)]
MIDDLE = [(1, 2), (2, 1)]
OUTWARD = [(1, 0), (2, 3)]


def reduce_quarters(make):
    dp_index = lax.axis_index("dp")
    obj_index = lax.axis_index("obj")
    x_bit, core_bit = dp_index // 2, dp_index % 2

    def quarter(x_same, core_same):
        x_at = x_bit if x_same else 1 - x_bit
        core_at = core_bit if core_same else 1 - core_bit
        return 2 * x_at + core_at

    give_far = make(quarter(False, False)).astype(BF16)
    give_near = make(quarter(True, False)).astype(BF16)
    got_far = lax.ppermute(give_far, "dp", CORE_SWAP)
    got_near = lax.ppermute(give_near, "dp", CORE_SWAP)
    far = (make(quarter(False, True)) + got_far.astype(F32)).astype(BF16)
    near = make(quarter(True, True)) + got_near.astype(F32)
    near = near + lax.ppermute(far, "dp", X_SWAP).astype(F32)
    near_low = near.astype(BF16)
    side = (near + lax.ppermute(near_low, "obj", INWARD).astype(F32)).astype(BF16)
    both = side + lax.ppermute(side, "obj", MIDDLE)
    in_middle = (obj_index == 1) | (obj_index == 2)
    mine = jnp.where(in_middle, both, lax.ppermute(both, "obj", OUTWARD))
    across = lax.ppermute(mine, "dp", X_SWAP)
    return (
        mine,
        across,
        lax.ppermute(mine, "dp", CORE_SWAP),
        lax.ppermute(across, "dp", CORE_SWAP),
    )


def in_order(quarters, axis):
    mine, across, mine_c, across_c = quarters
    dp_index = lax.axis_index("dp")
    x_is0 = dp_index // 2 == 0
    core_is0 = dp_index % 2 == 0
    c0_near, c1_near = jnp.where(core_is0, mine, mine_c), jnp.where(core_is0, mine_c, mine)
    c0_far, c1_far = jnp.where(core_is0, across, across_c), jnp.where(core_is0, across_c, across)
    return jnp.concatenate(
        [
            jnp.where(x_is0, c0_near, c0_far),
            jnp.where(x_is0, c1_near, c1_far),
            jnp.where(x_is0, c0_far, c0_near),
            jnp.where(x_is0, c1_far, c1_near),
        ],
        axis=axis,
    ).astype(F32)


def columns(array, index, count=4):
    width = array.shape[-1] // count
    return lax.dynamic_slice_in_dim(array, index * width, width, array.ndim - 1)


def token_sum(left, right):
    return lax.dot_general(left, right, (((0,), (0,)), ((), ())), preferred_element_type=F32)


def norm_stats(rows):
    mean = jnp.mean(rows, axis=-1, keepdims=True)
    centred = rows - mean
    scale = lax.rsqrt(jnp.mean(centred * centred, axis=-1, keepdims=True) + NORM_EPS)
    return centred * scale, scale


def norm_back(grads, zhat, scale, gain):
    q = grads * gain
    d_rows = scale * (
        q - jnp.mean(q, axis=-1, keepdims=True) - zhat * jnp.mean(q * zhat, axis=-1, keepdims=True)
    )
    return d_rows, jnp.sum(grads * zhat, axis=0), jnp.sum(grads, axis=0)


def body(
    hidden_in,
    cotangent,
    loss_mask,
    prefix_len,
    w_qkv,
    w_out,
    gain_one,
    bias_one,
    w_gate_up,
    w_down,
    gain_two,
    bias_two,
):
    tp_index = lax.axis_index("tp")
    share_len, width = hidden_in.shape[1:]
    seq_len = share_len * lax.axis_size("tp")
    local_ff = w_down.shape[0]
    mask_vals = loss_mask[0].astype(F32)
    total_count = all_sum(jnp.full((8, 128), jnp.sum(mask_vals)), ("dp", "tp"))[0, 0]

    positions = (tp_index * share_len + jnp.arange(seq_len, dtype=jnp.int32)) % seq_len
    half = HEAD_DIM // 2
    frequency = 10000.0 ** (-jnp.arange(half).astype(F32) / half)
    angles = positions.astype(F32)[:, None] * frequency[None, :]
    cos_half, sin_half = jnp.cos(angles), jnp.sin(angles)
    cos_vals = jnp.concatenate([cos_half, cos_half], axis=1)
    sin_vals = jnp.concatenate([-sin_half, sin_half], axis=1)
    info = jnp.stack([tp_index * share_len, prefix_len[0]]).astype(jnp.int32)

    def project(rows):
        return jnp.einsum("td,dke->kte", rows, w_qkv, preferred_element_type=F32)

    x_own = hidden_in[0]
    x_other = gather_rows(x_own)
    mixed, qkv = attend(info, project(x_own), project(x_other), cos_vals, sin_vals)
    mixed_own, mixed_other = mixed[:share_len], mixed[share_len:]
    out_send = jnp.dot(mixed_other, w_out, preferred_element_type=F32).astype(BF16)
    out_own = jnp.dot(mixed_own, w_out, preferred_element_type=F32)
    z_one = DEEP_ALPHA * x_own.astype(F32) + scatter_rows(out_own, out_send)
    zhat_one, scale_one = norm_stats(z_one)
    h_one = zhat_one * gain_one + bias_one
    h_own = h_one.astype(BF16)
    h_other = gather_rows(h_own)

    def feed(rows):
        gate_up = jnp.einsum("td,dke->tke", rows, w_gate_up, preferred_element_type=F32)
        gate, up = gate_up[:, 0], gate_up[:, 1]
        phi = 0.5 * (1.0 + lax.erf(gate * (0.5**0.5)))
        density = jnp.exp(-0.5 * gate * gate) * (0.5 / jnp.pi) ** 0.5
        act = gate * phi
        return lax.optimization_barrier(
            ((act * up).astype(BF16), up * (phi + gate * density), act)
        )

    hidden_own, slope_own, act_own = feed(h_own)
    hidden_other, slope_other, act_other = feed(h_other)
    ffn_send = jnp.dot(hidden_other, w_down, preferred_element_type=F32).astype(BF16)
    ffn_own = jnp.dot(hidden_own, w_down, preferred_element_type=F32)
    z_two = DEEP_ALPHA * h_one + scatter_rows(ffn_own, ffn_send)
    zhat_two, scale_two = norm_stats(z_two)
    outputs = (zhat_two * gain_two + bias_two).astype(BF16)
    grad_y = cotangent[0].astype(F32) * (mask_vals * (seq_len / total_count))[:, None]
    d_z_two, d_gain_two, d_bias_two = norm_back(grad_y, zhat_two, scale_two, gain_two)

    d_ffn_own = d_z_two.astype(BF16)
    d_ffn_other = gather_rows(d_ffn_own)
    hidden = jnp.concatenate([hidden_own, hidden_other], axis=0)
    d_ffn = jnp.concatenate([d_ffn_own, d_ffn_other], axis=0)

    def feed_back(d_rows, slope, act):
        d_hidden = lax.dot_general(
            d_rows, w_down, (((1,), (1,)), ((), ())), preferred_element_type=F32
        )
        return jnp.stack([d_hidden * slope, d_hidden * act], axis=0).astype(BF16)

    grad_down = reduce_quarters(lambda q: token_sum(hidden, columns(d_ffn, q)))
    d_gu_own = feed_back(d_ffn_own, slope_own, act_own)
    d_gu_other = feed_back(d_ffn_other, slope_other, act_other)
    d_gu = jnp.concatenate([d_gu_own, d_gu_other], axis=1)
    h_rows = jnp.concatenate([h_own, h_other], axis=0)
    grad_gate_up = [
        reduce_quarters(lambda q, k=k: token_sum(columns(h_rows, q), d_gu[k])) for k in range(2)
    ]

    def feed_rows(d_gate_up):
        return jnp.einsum("kte,dke->td", d_gate_up, w_gate_up, preferred_element_type=F32)

    d_h_send = feed_rows(d_gu_other).astype(BF16)
    d_h = scatter_rows(feed_rows(d_gu_own), d_h_send)
    d_z_one, d_gain_one, d_bias_one = norm_back(
        DEEP_ALPHA * d_z_two + d_h, zhat_one, scale_one, gain_one
    )
    d_attn_own = d_z_one.astype(BF16)
    d_attn_other = gather_rows(d_attn_own)
    d_attn = jnp.concatenate([d_attn_own, d_attn_other], axis=0)
    grad_out = reduce_quarters(lambda q: token_sum(mixed, columns(d_attn, q)))

    def unmix(d_rows):
        return lax.dot_general(
            d_rows, w_out, (((1,), (1,)), ((), ())), preferred_element_type=F32
        ).astype(BF16)

    d_mixed = jnp.concatenate([unmix(d_attn_own), unmix(d_attn_other)], axis=0)
    d_qkv = attend_back(info, qkv, d_mixed, cos_vals, sin_vals)
    x_rows = jnp.concatenate([x_own, x_other], axis=0)
    grad_qkv = [
        reduce_quarters(lambda q, k=k: token_sum(columns(x_rows, q), d_qkv[k])) for k in range(3)
    ]

    def unproject(d_rows):
        return jnp.einsum("kte,dke->td", d_rows, w_qkv, preferred_element_type=F32)

    d_x_send = unproject(d_qkv[:, share_len:]).astype(BF16)
    d_x = scatter_rows(unproject(d_qkv[:, :share_len]), d_x_send)
    input_grad = DEEP_ALPHA * d_z_one + d_x

    norm_terms = all_sum(
        jnp.stack([d_gain_one, d_bias_one, d_gain_two, d_bias_two]), ("dp", "obj", "tp")
    )
    local = width // lax.axis_size("tp")
    norm_terms = lax.dynamic_slice_in_dim(norm_terms, tp_index * local, local, 1)
    return (
        outputs[None],
        input_grad[None],
        jnp.stack([in_order(g, 0) for g in grad_qkv], axis=1),
        in_order(grad_out, 1),
        norm_terms[0],
        norm_terms[1],
        jnp.stack([in_order(g, 0) for g in grad_gate_up], axis=1),
        in_order(grad_down, 1),
        norm_terms[2],
        norm_terms[3],
    )


def solution(mesh):
    return jax.shard_map(
        body,
        mesh=mesh,
        in_specs=(
            P(("obj", "dp"), "tp", None),
            P(("obj", "dp"), "tp", None),
            P(("obj", "dp"), "tp"),
            P(("obj", "dp")),
            P(None, None, "tp"),
            P("tp", None),
            P(),
            P(),
            P(None, None, "tp"),
            P("tp", None),
            P(),
            P(),
        ),
        out_specs=(
            P(("obj", "dp"), "tp", None),
            P(("obj", "dp"), "tp", None),
            P(None, None, "tp"),
            P("tp", None),
            P("tp"),
            P("tp"),
            P(None, None, "tp"),
            P("tp", None),
            P("tp"),
            P("tp"),
        ),
        check_vma=False,
    )
```

time: 2950 us -> 1820 us (0.62)
  waiting for transfers between devices: 2120 us -> 983 us
  other arithmetic: 133 us -> 220 us
  starting transfers between devices: 0.41 us -> 85 us
  blocking collectives: 77.9 us -> 0 us
  Pallas kernels: 0 us -> 70.5 us
  local copies, waits for them, and re-layouts: 187 us -> 118 us
  matrix products: 395 us -> 332 us
    psum x1 -> x0, waiting for transfers between devices: 1610 us -> none  [body(): lax.psum((weight_grads[0], weight_grads[1], weight_grads[2], weight_grads...]
    ppermute x0 -> x79, waiting for transfers between devices: none -> 983 us  [the longest x7 374 us: reduce_quarters(): mine = jnp.where(in_middle, both, lax.ppermute(both, 'obj', OUTWARD))]
    reduce_scatter x4 -> x0, waiting for transfers between devices: 283 us -> none  [the longest x1 99.4 us: body(): d_h_here = lax.psum_scatter(d_h_part, 'tp', scatter_dimension=1, tiled=True)]
    all_gather x4 -> x0, waiting for transfers between devices: 229 us -> none  [the longest x1 60 us: body(): lax.all_gather(hidden_in, 'tp', axis=1, tiled=True)]
    ppermute x0 -> x79, starting transfers between devices: none -> 85 us  [the longest x7 23.4 us: reduce_quarters(): lax.ppermute(near_low, 'obj', INWARD).astype(F32)]
    psum x2 -> x0, blocking collectives: 77.9 us -> none  [the longest x1 64.4 us: body(): lax.psum((weight_grads[0], weight_grads[1], weight_grads[2], weight_grads...]
    pallas_call x0 -> x2, Pallas kernels: none -> 70.5 us  [the longest x1 43.2 us: attend_back(): pl.pallas_call(functools.partial(attend_back_kernel, min(256, seq_len)),...]
    dot_general x26 -> x44, matrix products: 395 us -> 332 us  [the longest x28 132 us: token_sum(): lax.dot_general(left, right, (((0,), (0,)), ((), ())), preferred_element_...]
  transfers between devices with their start and end apart: 10 -> 79, of which waited for: 8 -> 32; matrix products, arithmetic and copies ran while one was open for 11% -> 27% of each run, Pallas kernels for 0% -> 2%
where the time goes in v1:
time: 1820 us; the launch traced here: 1810 us
  waiting for transfers between devices  983 us (54%)
  matrix products  332 us (18%)
  other arithmetic  220 us (12%)
  local copies, waits for them, and re-layouts  118 us (6%)
  starting transfers between devices  85 us (5%)
  Pallas kernels  70.5 us (4%)
    ppermute x7, waiting for transfers between devices, reduce_quarters(): mine = jnp.where(in_middle, both, lax.ppermute(both, 'obj', OUTWARD))  374 us
    ppermute x7, waiting for transfers between devices, reduce_quarters(): lax.ppermute(near_low, 'obj', INWARD).astype(F32)  146 us
    ppermute x7, waiting for transfers between devices, reduce_quarters(): near = near + lax.ppermute(far, 'dp', X_SWAP).astype(F32)  145 us
    dot_general x28, matrix products, token_sum(): lax.dot_general(left, right, (((0,), (0,)), ((), ())), preferred_element_...  132 us
    ppermute x7, waiting for transfers between devices, reduce_quarters(): across = lax.ppermute(mine, 'dp', X_SWAP)  130 us
    unnamed x162, local copies, waits for them, and re-layouts  116 us
    ppermute x4, waiting for transfers between devices, gather_rows(): return lax.ppermute(own, 'tp', [(0, 1), (1, 0)])  84.6 us
    ppermute x4, waiting for transfers between devices, scatter_rows(): lax.ppermute(send_part, 'tp', [(0, 1), (1, 0)]).astype(F32)  59.7 us
  transfers between devices with their start and end apart: 79, of which 32 were waited for; matrix products, arithmetic and copies ran while one was open for 27% of the time, Pallas kernels for 2%

profile of v1, /device:TPU:0, one launch (start us, length us, event | category | flops | bytes accessed | tf_op | source)
XLA Modules:
  0.0 1812.7 jit_solution(16100927748077110053)
XLA Ops:
  19.8 29.8 %collective-permute-done = bf16[512,2048]{1,0:T(8,128)(2,1)} collective-permute-done((bf16[512,2048]{1,0:T(8,128)(2,1)}, bf16[512,2048]{1,0:T(8,128)(2,1)}, u32[]{:S(2)}, u32[]{:S(2)}) %collective-permute-start) | collective-permute-done | bytes 2097184 | tf_op jit(solution)/shard_map/ppermute | solution.py:185
  59.7 27.2 %attend.1 = (bf16[1024,1024]{1,0:T(8,128)(2,1)}, bf16[3,1024,1024]{2,1,0:T(8,128)(2,1)}) custom-call(s32[2]{0:T(128)} %pad_add_fusion.info_ref, f32[3,512,1024]{2,1,0:T(8,128)} %convolution_bitcast_fusion.1.own_ref, f32[3,512,1024]{2,1,0:T(8,128)} %convolution_bitcast_fusion.other_ref, f32[1024,128]{1,0:T(8,128)} %get-tuple-element.116.cos_ref, ...), custom_call_target="tpu_custom_call" | custom-call | flops 8589934592 | bytes 20971520 | tf_op jit(solution)/shard_map/attend/pallas_call | solution.py:120
  93.7 45.1 %collective-permute-done.1 = bf16[512,2048]{1,0:T(8,128)(2,1)S(1)} collective-permute-done((bf16[512,2048]{1,0:T(8,128)(2,1)S(1)}, bf16[512,2048]{1,0:T(8,128)(2,1)S(1)}, u32[]{:S(2)}, u32[]{:S(2)}) %collective-permute-start.1) | collective-permute-done | bytes 2097184 | tf_op jit(solution)/shard_map/ppermute | solution.py:197
  153.1 36.5 %collective-permute-done.6 = f32[8,128]{1,0:T(8,128)S(1)} collective-permute-done((f32[8,128]{1,0:T(8,128)S(1)}, f32[8,128]{1,0:T(8,128)S(1)}, u32[]{:S(2)}, u32[]{:S(2)}) %collective-permute-start.6) | collective-permute-done | bytes 4128 | tf_op jit(solution)/shard_map/ppermute | solution.py:210
  195.0 21.8 %fusion.4 = f32[512,2,2816]{2,0,1:T(8,128)} fusion(bf16[2048,2,2816]{2,1,0:T(2,128)(2,1)} %param.20, bf16[512,2048]{1,0:T(8,128)(2,1)} %collective-permute-done.2), kind=kOutput, calls=%fused_computation.5 | convolution fusion | flops 11811160064 | bytes 36700160 | tf_op jit(solution)/shard_map/td,dke->tke/dot_general | solution.py:341
  236.4 20.9 %fusion.6 = f32[512,2,2816]{2,0,1:T(8,128)} fusion(bf16[2048,2,2816]{2,1,0:T(2,128)(2,1)} %param.20, bf16[512,2048]{1,0:T(8,128)(2,1)S(1)} %fusion.41), kind=kOutput, calls=%fused_computation.7 | convolution fusion | flops 11811160064 | bytes 36700160 | tf_op jit(solution)/shard_map/td,dke->tke/dot_general | solution.py:341
  266.1 14.6 collective-permute-done.3
  300.6 15.2 fusion.52
  315.9 28.5 %collective-permute-done.7 = bf16[512,2048]{1,0:T(8,128)(2,1)} collective-permute-done((bf16[512,2048]{1,0:T(8,128)(2,1)}, bf16[512,2048]{1,0:T(8,128)(2,1)}, u32[]{:S(2)}, u32[]{:S(2)}) %collective-permute-start.7) | collective-permute-done | bytes 2097184 | tf_op jit(solution)/shard_map/ppermute | solution.py:185
  344.3 15.2 fusion.54
  359.5 21.8 %bitcast_convert_fusion.1 = bf16[512,2048]{1,0:T(8,128)(2,1)} fusion(bf16[2048,2,2816]{2,1,0:T(2,128)(2,1)} %param.20, bf16[1,512,2816]{2,1,0:T(8,128)(2,1)} %get-tuple-element.69, bf16[1,512,2816]{2,1,0:T(8,128)(2,1)} %get-tuple-element.68), kind=kOutput, calls=%fused_computation.109 | convolution fusion | flops 11815092224 | bytes 30932992 | tf_op jit(solution)/shard_map/kte,dke->td/dot_general | solution.py:381
  426.2 26.9 %multiply_reduce_fusion = (f32[2048]{0:T(1024)S(1)}, f32[512]{0:T(512)S(1)}, f32[512]{0:T(512)S(1)}, f32[2048]{0:T(1024)S(1)}, f32[512,2048]{1,0:T(8,128)}) fusion(f32[512,2048]{1,0:T(8,128)} %copy-done.2, f32[512]{0:T(512)S(1)} %add_rsqrt_fusion.1, f32[512]{0:T(512)S(1)} %broadcast_multiply_fusion.5, f32[2048]{0:T(1024)S(1)} %copy-done.47, ...), kind=kOutput, calls=%fused_computation.112 | convolution fusion | flops 11837108224 | bytes 45664256 | tf_op jit(solution)/shard_map/kte,dke->td/dot_general | solution.py:381
  492.9 26.3 %collective-permute-done.9 = bf16[512,2048]{1,0:T(8,128)(2,1)S(1)} collective-permute-done((bf16[512,2048]{1,0:T(8,128)(2,1)S(1)}, bf16[512,2048]{1,0:T(8,128)(2,1)S(1)}, u32[]{:S(2)}, u32[]{:S(2)}) %collective-permute-start.9) | collective-permute-done | bytes 2097184 | tf_op jit(solution)/shard_map/ppermute | solution.py:185
  523.2 43.2 %attend_back.1 = bf16[3,1024,1024]{2,1,0:T(8,128)(2,1)} custom-call(s32[2]{0:T(128)} %pad_add_fusion.info_ref, bf16[3,1024,1024]{2,1,0:T(8,128)(2,1)} %get-tuple-element.25.qkv_ref, bf16[1024,1024]{1,0:T(8,128)(2,1)} %pad_maximum_fusion.grad_ref, f32[1024,128]{1,0:T(8,128)} %get-tuple-element.116.cos_ref, f32[1024,128]{1,0:T(8,128)} %get-tuple-element.117.sin_ref), custom_call_target="tpu_custom_call" | custom-call | flops 21474836480 | bytes 14680064 | tf_op jit(solution)/shard_map/attend_back/pallas_call | solution.py:154
  623.0 41.7 %collective-permute-done.54 = bf16[512,2816]{1,0:T(8,128)(2,1)S(1)} collective-permute-done((bf16[512,2816]{1,0:T(8,128)(2,1)}, bf16[512,2816]{1,0:T(8,128)(2,1)S(1)}, u32[]{:S(2)}, u32[]{:S(2)}) %collective-permute-start.54) | collective-permute-done | bytes 2883616 | tf_op jit(solution)/shard_map/ppermute | solution.py:238
  677.4 49.2 %collective-permute-done.72 = bf16[2816,512]{0,1:T(8,128)(2,1)} collective-permute-done((bf16[2816,512]{0,1:T(8,128)(2,1)}, bf16[2816,512]{0,1:T(8,128)(2,1)}, u32[]{:S(2)}, u32[]{:S(2)}) %collective-permute-start.72) | collective-permute-done | bytes 2883616 | tf_op jit(solution)/shard_map/ppermute | solution.py:238
  753.7 17.8 collective-permute-done.22
  775.4 18.5 %collective-permute-done.40 = bf16[1024,512]{0,1:T(8,128)(2,1)S(1)} collective-permute-done((bf16[1024,512]{0,1:T(8,128)(2,1)}, bf16[1024,512]{0,1:T(8,128)(2,1)S(1)}, u32[]{:S(2)}, u32[]{:S(2)}) %collective-permute-start.40) | collective-permute-done | bytes 1048608 | tf_op jit(solution)/shard_map/ppermute | solution.py:238
  822.5 54.2 %collective-permute-done.32 = bf16[512,1024]{1,0:T(8,128)(2,1)S(1)} collective-permute-done((bf16[512,1024]{1,0:T(8,128)(2,1)S(1)}, bf16[512,1024]{1,0:T(8,128)(2,1)S(1)}, u32[]{:S(2)}, u32[]{:S(2)}) %collective-permute-start.32) | collective-permute-done | bytes 1048608 | tf_op jit(solution)/shard_map/ppermute | solution.py:240
  899.9 61.2 %collective-permute-done.23 = bf16[512,1024]{1,0:T(8,128)(2,1)} collective-permute-done((bf16[512,1024]{1,0:T(8,128)(2,1)}, bf16[512,1024]{1,0:T(8,128)(2,1)}, u32[]{:S(2)}, u32[]{:S(2)}) %collective-permute-start.23) | collective-permute-done | bytes 1048608 | tf_op jit(solution)/shard_map/ppermute | solution.py:240
  963.3 20.3 %collective-permute-done.14 = bf16[512,1024]{1,0:T(8,128)(2,1)} collective-permute-done((bf16[512,1024]{1,0:T(8,128)(2,1)}, bf16[512,1024]{1,0:T(8,128)(2,1)}, u32[]{:S(2)}, u32[]{:S(2)}) %collective-permute-start.14) | collective-permute-done | bytes 1048608 | tf_op jit(solution)/shard_map/ppermute | solution.py:240
  1039.3 129.6 %collective-permute-done.34 = bf16[512,1024]{1,0:T(8,128)(2,1)S(1)} collective-permute-done((bf16[512,1024]{1,0:T(8,128)(2,1)S(1)}, bf16[512,1024]{1,0:T(8,128)(2,1)S(1)}, u32[]{:S(2)}, u32[]{:S(2)}) %collective-permute-start.34) | collective-permute-done | bytes 1048608 | tf_op jit(solution)/shard_map/ppermute | solution.py:243
  1187.0 183.0 %collective-permute-done.16 = bf16[512,1024]{1,0:T(8,128)(2,1)} collective-permute-done((bf16[512,1024]{1,0:T(8,128)(2,1)}, bf16[512,1024]{1,0:T(8,128)(2,1)}, u32[]{:S(2)}, u32[]{:S(2)}) %collective-permute-start.16) | collective-permute-done | bytes 1048608 | tf_op jit(solution)/shard_map/ppermute | solution.py:243
  1407.2 19.2 %collective-permute-done.27 = bf16[512,1024]{1,0:T(8,128)(2,1)} collective-permute-done((bf16[512,1024]{1,0:T(8,128)(2,1)}, bf16[512,1024]{1,0:T(8,128)(2,1)}, u32[]{:S(2)}, u32[]{:S(2)}) %collective-permute-start.27) | collective-permute-done | bytes 1048608 | tf_op jit(solution)/shard_map/ppermute | solution.py:244
  1471.9 40.1 %collective-permute-done.75 = bf16[2816,512]{0,1:T(8,128)(2,1)S(1)} collective-permute-done((bf16[2816,512]{0,1:T(8,128)(2,1)}, bf16[2816,512]{0,1:T(8,128)(2,1)S(1)}, u32[]{:S(2)}, u32[]{:S(2)}) %collective-permute-start.75) | collective-permute-done | bytes 2883616 | tf_op jit(solution)/shard_map/ppermute | solution.py:243
  1528.2 61.8 %collective-permute-done.59 = bf16[512,2816]{1,0:T(8,128)(2,1)} collective-permute-done((bf16[512,2816]{1,0:T(8,128)(2,1)}, bf16[512,2816]{1,0:T(8,128)(2,1)}, u32[]{:S(2)}, u32[]{:S(2)}) %collective-permute-start.59) | collective-permute-done | bytes 2883616 | tf_op jit(solution)/shard_map/ppermute | solution.py:244
  1590.0 27.8 %maximum_convert_fusion.1 = f32[2048,3,1024]{2,0,1:T(8,128)} fusion(bf16[512,1,1024]{2,0,1:T(8,128)(2,1)S(1)} %get-tuple-element.87, bf16[512,1,1024]{2,0,1:T(8,128)(2,1)S(1)} %get-tuple-element.86, bf16[512,1,1024]{2,0,1:T(8,128)(2,1)S(1)} %get-tuple-element.85, bf16[512,1,1024]{2,0,1:T(8,128)(2,1)S(1)} %get-tuple-element.84, ...), kind=kLoop, calls=%fused_computation.9 | loop fusion | flops 150994944 | bytes 37748736 | tf_op jit(solution)/shard_map/stack | solution.py:420
  1633.2 16.0 collective-permute-done.77
  1664.1 21.1 %maximum_convert_fusion = f32[2048,2,2816]{2,0,1:T(8,128)} fusion(bf16[512,1,2816]{2,0,1:T(8,128)(2,1)} %get-tuple-element.63, bf16[512,1,2816]{2,0,1:T(8,128)(2,1)} %get-tuple-element.62, bf16[512,1,2816]{2,0,1:T(8,128)(2,1)} %get-tuple-element.61, bf16[512,1,2816]{2,0,1:T(8,128)(2,1)S(1)} %get-tuple-element.60, bf16[512,1,2816]{2,0,1:T(8,128)(2,1)} %get-tuple-element.59, ...), kind=kLoop, calls=%fused_computation | loop fusion | flops 184549376 | bytes 69206016 | tf_op jit(solution)/shard_map/stack | solution.py:424
  1685.2 75.3 %copy.37 = f32[2048,2,2816]{2,1,0:T(2,128)} copy(f32[2048,2,2816]{2,0,1:T(8,128)} %maximum_convert_fusion) | data formatting | bytes 92274688
  1765.4 23.6 %maximum_convert_fusion.2 = f32[2816,2048]{0,1:T(8,128)} fusion(bf16[2816,512]{0,1:T(8,128)(2,1)S(1)} %get-tuple-element.55, bf16[2816,512]{0,1:T(8,128)(2,1)S(1)} %get-tuple-element.54, bf16[2816,512]{0,1:T(8,128)(2,1)S(1)} %get-tuple-element.53, bf16[2816,512]{0,1:T(8,128)(2,1)S(1)} %get-tuple-element.52), kind=kLoop, calls=%fused_computation.11 | loop fusion | flops 46137344 | bytes 34603008 | tf_op jit(solution)/shard_map/convert_element_type | solution.py:268
  1789.0 23.3 %copy.38 = f32[2816,2048]{1,0:T(8,128)} copy(f32[2816,2048]{0,1:T(8,128)} %maximum_convert_fusion.2) | data formatting | bytes 46137344
  (414 shorter events, 552.5 us)
Async XLA Ops:
  394.7 76.4 %collective-permute-start.62 = (bf16[512,2816]{1,0:T(8,128)(2,1)}, bf16[512,2816]{1,0:T(8,128)(2,1)}, u32[]{:S(2)}, u32[]{:S(2)}) collective-permute-start(bf16[512,2816]{1,0:T(8,128)(2,1)} %convolution_convert_fusion.2), channel_id=1, source_target_pairs={{0,2},{2,0},{4,6},{6,4},{1,3},{3,1},{5,7},{7,5},{8,10},{10,8},{12,... | collective-permute-start | bytes 8650760 | tf_op jit(solution)/shard_map/ppermute | solution.py:234
  400.8 186.7 %collective-permute-start.61 = (bf16[512,2816]{1,0:T(8,128)(2,1)}, bf16[512,2816]{1,0:T(8,128)(2,1)}, u32[]{:S(2)}, u32[]{:S(2)}) collective-permute-start(bf16[512,2816]{1,0:T(8,128)(2,1)} %convolution_convert_fusion.3), channel_id=1, source_target_pairs={{0,2},{2,0},{4,6},{6,4},{1,3},{3,1},{5,7},{7,5},{8,10},{10,8},{12,... | collective-permute-start | bytes 8650760 | tf_op jit(solution)/shard_map/ppermute | solution.py:235
  471.1 143.9 %collective-permute-start.52 = (bf16[512,2816]{1,0:T(8,128)(2,1)}, bf16[512,2816]{1,0:T(8,128)(2,1)}, u32[]{:S(2)}, u32[]{:S(2)}) collective-permute-start(bf16[512,2816]{1,0:T(8,128)(2,1)} %convolution_convert_fusion.5), channel_id=1, source_target_pairs={{0,2},{2,0},{4,6},{6,4},{1,3},{3,1},{5,7},{7,5},{8,10},{10,8},{12,... | collective-permute-start | bytes 8650760 | tf_op jit(solution)/shard_map/ppermute | solution.py:235
  478.3 137.0 %collective-permute-start.63 = (bf16[512,2816]{1,0:T(8,128)(2,1)}, bf16[512,2816]{1,0:T(8,128)(2,1)}, u32[]{:S(2)}, u32[]{:S(2)}) collective-permute-start(bf16[512,2816]{1,0:T(8,128)(2,1)} %add_convert_fusion.3), channel_id=1, source_target_pairs={{0,4},{4,0},{2,6},{6,2},{1,5},{5,1},{3,7},{7,3},{8,12},{12,8},{10,... | collective-permute-start | bytes 8650760 | tf_op jit(solution)/shard_map/ppermute | solution.py:238
  609.9 116.7 %collective-permute-start.72 = (bf16[2816,512]{0,1:T(8,128)(2,1)}, bf16[2816,512]{0,1:T(8,128)(2,1)}, u32[]{:S(2)}, u32[]{:S(2)}) collective-permute-start(bf16[2816,512]{0,1:T(8,128)(2,1)} %add_convert_fusion.1), channel_id=1, source_target_pairs={{0,4},{4,0},{2,6},{6,2},{1,5},{5,1},{3,7},{7,3},{8,12},{12,8},{10,... | collective-permute-start | bytes 8650760 | tf_op jit(solution)/shard_map/ppermute | solution.py:238
  622.9 118.5 %collective-permute-start.38 = (bf16[1024,512]{0,1:T(8,128)(2,1)}, bf16[1024,512]{0,1:T(8,128)(2,1)S(1)}, u32[]{:S(2)}, u32[]{:S(2)}) collective-permute-start(bf16[1024,512]{0,1:T(8,128)(2,1)} %convolution_convert_fusion.9), channel_id=1, source_target_pairs={{0,2},{2,0},{4,6},{6,4},{1,3},{3,1},{5,7},{7,5},{8,10},{10,8},{12,... | collective-permute-start | bytes 3145736 | tf_op jit(solution)/shard_map/ppermute | solution.py:235
  666.3 82.8 %collective-permute-start.31 = (bf16[512,1024]{1,0:T(8,128)(2,1)}, bf16[512,1024]{1,0:T(8,128)(2,1)}, u32[]{:S(2)}, u32[]{:S(2)}) collective-permute-start(bf16[512,1024]{1,0:T(8,128)(2,1)} %add_convert_fusion.10), channel_id=1, source_target_pairs={{0,4},{4,0},{2,6},{6,2},{1,5},{5,1},{3,7},{7,3},{8,12},{12,8},{10,... | collective-permute-start | bytes 3145736 | tf_op jit(solution)/shard_map/ppermute | solution.py:238
  675.3 96.1 %collective-permute-start.22 = (bf16[512,1024]{1,0:T(8,128)(2,1)}, bf16[512,1024]{1,0:T(8,128)(2,1)S(1)}, u32[]{:S(2)}, u32[]{:S(2)}) collective-permute-start(bf16[512,1024]{1,0:T(8,128)(2,1)} %add_convert_fusion.12), channel_id=1, source_target_pairs={{0,4},{4,0},{2,6},{6,2},{1,5},{5,1},{3,7},{7,3},{8,12},{12,8},{10,... | collective-permute-start | bytes 3145736 | tf_op jit(solution)/shard_map/ppermute | solution.py:238
  675.9 118.0 %collective-permute-start.40 = (bf16[1024,512]{0,1:T(8,128)(2,1)}, bf16[1024,512]{0,1:T(8,128)(2,1)S(1)}, u32[]{:S(2)}, u32[]{:S(2)}) collective-permute-start(bf16[1024,512]{0,1:T(8,128)(2,1)} %add_convert_fusion.8), channel_id=1, source_target_pairs={{0,4},{4,0},{2,6},{6,2},{1,5},{5,1},{3,7},{7,3},{8,12},{12,8},{10,... | collective-permute-start | bytes 3145736 | tf_op jit(solution)/shard_map/ppermute | solution.py:238
  726.6 158.8 %collective-permute-start.64 = (bf16[512,2816]{1,0:T(8,128)(2,1)}, bf16[512,2816]{1,0:T(8,128)(2,1)S(1)}, u32[]{:S(2)}, u32[]{:S(2)}) collective-permute-start(bf16[512,2816]{1,0:T(8,128)(2,1)} %get-tuple-element.110), channel_id=1, source_target_pairs={{0,8},{24,16},{1,9},{25,17},{2,10},{26,18},{3,11},{27,19},{4,12},{... | collective-permute-start | bytes 8650760 | tf_op jit(solution)/shard_map/ppermute | solution.py:240
  771.4 121.2 %collective-permute-start.55 = (bf16[512,2816]{1,0:T(8,128)(2,1)}, bf16[512,2816]{1,0:T(8,128)(2,1)}, u32[]{:S(2)}, u32[]{:S(2)}) collective-permute-start(bf16[512,2816]{1,0:T(8,128)(2,1)} %get-tuple-element.112), channel_id=1, source_target_pairs={{0,8},{24,16},{1,9},{25,17},{2,10},{26,18},{3,11},{27,19},{4,12},{... | collective-permute-start | bytes 8650760 | tf_op jit(solution)/shard_map/ppermute | solution.py:240
  793.9 82.8 %collective-permute-start.32 = (bf16[512,1024]{1,0:T(8,128)(2,1)S(1)}, bf16[512,1024]{1,0:T(8,128)(2,1)S(1)}, u32[]{:S(2)}, u32[]{:S(2)}) collective-permute-start(bf16[512,1024]{1,0:T(8,128)(2,1)S(1)} %get-tuple-element.102), channel_id=1, source_target_pairs={{0,8},{24,16},{1,9},{25,17},{2,10},{26,18},{3,11},{27,19},{4,12},{... | collective-permute-start | bytes 3145736 | tf_op jit(solution)/shard_map/ppermute | solution.py:240
  803.7 211.9 %collective-permute-start.10 = (bf16[512,2048]{1,0:T(8,128)(2,1)}, bf16[512,2048]{1,0:T(8,128)(2,1)}, u32[]{:S(2)}, u32[]{:S(2)}) collective-permute-start(bf16[512,2048]{1,0:T(8,128)(2,1)} %bitcast_convert_fusion), channel_id=1, source_target_pairs={{0,1},{1,0},{2,3},{3,2},{4,5},{5,4},{6,7},{7,6},{8,9},{9,8},{10,11... | collective-permute-start | bytes 6291464 | tf_op jit(solution)/shard_map/ppermute | solution.py:197
  815.5 192.8 %collective-permute-start.73 = (bf16[2816,512]{0,1:T(8,128)(2,1)}, bf16[2816,512]{0,1:T(8,128)(2,1)}, u32[]{:S(2)}, u32[]{:S(2)}) collective-permute-start(bf16[2816,512]{0,1:T(8,128)(2,1)} %get-tuple-element.114), channel_id=1, source_target_pairs={{0,8},{24,16},{1,9},{25,17},{2,10},{26,18},{3,11},{27,19},{4,12},{... | collective-permute-start | bytes 8650760 | tf_op jit(solution)/shard_map/ppermute | solution.py:240
  876.7 84.4 %collective-permute-start.23 = (bf16[512,1024]{1,0:T(8,128)(2,1)}, bf16[512,1024]{1,0:T(8,128)(2,1)}, u32[]{:S(2)}, u32[]{:S(2)}) collective-permute-start(bf16[512,1024]{1,0:T(8,128)(2,1)} %get-tuple-element.104), channel_id=1, source_target_pairs={{0,8},{24,16},{1,9},{25,17},{2,10},{26,18},{3,11},{27,19},{4,12},{... | collective-permute-start | bytes 3145736 | tf_op jit(solution)/shard_map/ppermute | solution.py:240
  885.4 98.1 %collective-permute-start.14 = (bf16[512,1024]{1,0:T(8,128)(2,1)}, bf16[512,1024]{1,0:T(8,128)(2,1)}, u32[]{:S(2)}, u32[]{:S(2)}) collective-permute-start(bf16[512,1024]{1,0:T(8,128)(2,1)} %get-tuple-element.106), channel_id=1, source_target_pairs={{0,8},{24,16},{1,9},{25,17},{2,10},{26,18},{3,11},{27,19},{4,12},{... | collective-permute-start | bytes 3145736 | tf_op jit(solution)/shard_map/ppermute | solution.py:240
  892.7 110.7 %collective-permute-start.41 = (bf16[1024,512]{0,1:T(8,128)(2,1)}, bf16[1024,512]{0,1:T(8,128)(2,1)}, u32[]{:S(2)}, u32[]{:S(2)}) collective-permute-start(bf16[1024,512]{0,1:T(8,128)(2,1)} %get-tuple-element.108), channel_id=1, source_target_pairs={{0,8},{24,16},{1,9},{25,17},{2,10},{26,18},{3,11},{27,19},{4,12},{... | collective-permute-start | bytes 3145736 | tf_op jit(solution)/shard_map/ppermute | solution.py:240
  1015.7 367.1 %collective-permute-start.74 = (bf16[2816,512]{0,1:T(8,128)(2,1)}, bf16[2816,512]{0,1:T(8,128)(2,1)}, u32[]{:S(2)}, u32[]{:S(2)}) collective-permute-start(bf16[2816,512]{0,1:T(8,128)(2,1)} %add_convert_fusion), channel_id=1, source_target_pairs={{8,16},{16,8},{9,17},{17,9},{10,18},{18,10},{11,19},{19,11},{12,20... | collective-permute-start | bytes 8650760 | tf_op jit(solution)/shard_map/ppermute | solution.py:241
  1023.3 145.6 %collective-permute-start.34 = (bf16[512,1024]{1,0:T(8,128)(2,1)S(1)}, bf16[512,1024]{1,0:T(8,128)(2,1)S(1)}, u32[]{:S(2)}, u32[]{:S(2)}) collective-permute-start(bf16[512,1024]{1,0:T(8,128)(2,1)S(1)} %add.357), channel_id=1, source_target_pairs={{8,0},{16,24},{9,1},{17,25},{10,2},{18,26},{11,3},{19,27},{12,4},{... | collective-permute-start | bytes 3145736 | tf_op jit(solution)/shard_map/ppermute | solution.py:243
  1024.6 155.5 %collective-permute-start.25 = (bf16[512,1024]{1,0:T(8,128)(2,1)S(1)}, bf16[512,1024]{1,0:T(8,128)(2,1)S(1)}, u32[]{:S(2)}, u32[]{:S(2)}) collective-permute-start(bf16[512,1024]{1,0:T(8,128)(2,1)S(1)} %add.352), channel_id=1, source_target_pairs={{8,0},{16,24},{9,1},{17,25},{10,2},{18,26},{11,3},{19,27},{12,4},{... | collective-permute-start | bytes 3145736 | tf_op jit(solution)/shard_map/ppermute | solution.py:243
  1032.7 395.2 %collective-permute-start.66 = (bf16[512,2816]{1,0:T(8,128)(2,1)S(1)}, bf16[512,2816]{1,0:T(8,128)(2,1)}, u32[]{:S(2)}, u32[]{:S(2)}) collective-permute-start(bf16[512,2816]{1,0:T(8,128)(2,1)S(1)} %add.378), channel_id=1, source_target_pairs={{8,0},{16,24},{9,1},{17,25},{10,2},{18,26},{11,3},{19,27},{12,4},{... | collective-permute-start | bytes 8650760 | tf_op jit(solution)/shard_map/ppermute | solution.py:243
  1034.0 393.9 %collective-permute-start.57 = (bf16[512,2816]{1,0:T(8,128)(2,1)}, bf16[512,2816]{1,0:T(8,128)(2,1)}, u32[]{:S(2)}, u32[]{:S(2)}) collective-permute-start(bf16[512,2816]{1,0:T(8,128)(2,1)} %add.373), channel_id=1, source_target_pairs={{8,0},{16,24},{9,1},{17,25},{10,2},{18,26},{11,3},{19,27},{12,4},{... | collective-permute-start | bytes 8650760 | tf_op jit(solution)/shard_map/ppermute | solution.py:243
  1168.9 201.2 %collective-permute-start.16 = (bf16[512,1024]{1,0:T(8,128)(2,1)}, bf16[512,1024]{1,0:T(8,128)(2,1)}, u32[]{:S(2)}, u32[]{:S(2)}) collective-permute-start(bf16[512,1024]{1,0:T(8,128)(2,1)} %add.347), channel_id=1, source_target_pairs={{8,0},{16,24},{9,1},{17,25},{10,2},{18,26},{11,3},{19,27},{12,4},{... | collective-permute-start | bytes 3145736 | tf_op jit(solution)/shard_map/ppermute | solution.py:243
  1181.1 200.2 %collective-permute-start.43 = (bf16[1024,512]{0,1:T(8,128)(2,1)}, bf16[1024,512]{0,1:T(8,128)(2,1)}, u32[]{:S(2)}, u32[]{:S(2)}) collective-permute-start(bf16[1024,512]{0,1:T(8,128)(2,1)} %add.362), channel_id=1, source_target_pairs={{8,0},{16,24},{9,1},{17,25},{10,2},{18,26},{11,3},{19,27},{12,4},{... | collective-permute-start | bytes 3145736 | tf_op jit(solution)/shard_map/ppermute | solution.py:243
  1447.5 80.7 %collective-permute-start.68 = (bf16[512,2816]{1,0:T(8,128)(2,1)}, bf16[512,2816]{1,0:T(8,128)(2,1)}, u32[]{:S(2)}, u32[]{:S(2)}) collective-permute-start(bf16[512,2816]{1,0:T(8,128)(2,1)} %broadcast_select_fusion.9), channel_id=1, source_target_pairs={{0,4},{4,0},{2,6},{6,2},{1,5},{5,1},{3,7},{7,3},{8,12},{12,8},{10,... | collective-permute-start | bytes 8650760 | tf_op jit(solution)/shard_map/ppermute | solution.py:244
  1449.9 140.0 %collective-permute-start.59 = (bf16[512,2816]{1,0:T(8,128)(2,1)}, bf16[512,2816]{1,0:T(8,128)(2,1)}, u32[]{:S(2)}, u32[]{:S(2)}) collective-permute-start(bf16[512,2816]{1,0:T(8,128)(2,1)} %broadcast_select_fusion.10), channel_id=1, source_target_pairs={{0,4},{4,0},{2,6},{6,2},{1,5},{5,1},{3,7},{7,3},{8,12},{12,8},{10,... | collective-permute-start | bytes 8650760 | tf_op jit(solution)/shard_map/ppermute | solution.py:244
  1512.0 120.8 %collective-permute-start.67 = (bf16[512,2816]{1,0:T(8,128)(2,1)}, bf16[512,2816]{1,0:T(8,128)(2,1)}, u32[]{:S(2)}, u32[]{:S(2)}) collective-permute-start(bf16[512,2816]{1,0:T(8,128)(2,1)} %broadcast_select_fusion.9), channel_id=1, source_target_pairs={{0,2},{2,0},{4,6},{6,4},{1,3},{3,1},{5,7},{7,5},{8,10},{10,8},{12,... | collective-permute-start | bytes 8650760 | tf_op jit(solution)/shard_map/ppermute | solution.py:248
  1513.9 142.4 %collective-permute-start.58 = (bf16[512,2816]{1,0:T(8,128)(2,1)}, bf16[512,2816]{1,0:T(8,128)(2,1)}, u32[]{:S(2)}, u32[]{:S(2)}) collective-permute-start(bf16[512,2816]{1,0:T(8,128)(2,1)} %broadcast_select_fusion.10), channel_id=1, source_target_pairs={{0,2},{2,0},{4,6},{6,4},{1,3},{3,1},{5,7},{7,5},{8,10},{10,8},{12,... | collective-permute-start | bytes 8650760 | tf_op jit(solution)/shard_map/ppermute | solution.py:248
  1514.4 134.8 %collective-permute-start.77 = (bf16[2816,512]{0,1:T(8,128)(2,1)}, bf16[2816,512]{0,1:T(8,128)(2,1)}, u32[]{:S(2)}, u32[]{:S(2)}) collective-permute-start(bf16[2816,512]{0,1:T(8,128)(2,1)} %broadcast_select_fusion), channel_id=1, source_target_pairs={{0,4},{4,0},{2,6},{6,2},{1,5},{5,1},{3,7},{7,3},{8,12},{12,8},{10,... | collective-permute-start | bytes 8650760 | tf_op jit(solution)/shard_map/ppermute | solution.py:244
  1528.2 121.0 %collective-permute-start.69 = (bf16[512,2816]{1,0:T(8,128)(2,1)}, bf16[512,2816]{1,0:T(8,128)(2,1)}, u32[]{:S(2)}, u32[]{:S(2)}) collective-permute-start(bf16[512,2816]{1,0:T(8,128)(2,1)} %collective-permute-done.68), channel_id=1, source_target_pairs={{0,2},{2,0},{4,6},{6,4},{1,3},{3,1},{5,7},{7,5},{8,10},{10,8},{12,... | collective-permute-start | bytes 8650760 | tf_op jit(solution)/shard_map/ppermute | solution.py:249
  1632.7 127.8 %collective-permute-start.76 = (bf16[2816,512]{0,1:T(8,128)(2,1)}, bf16[2816,512]{0,1:T(8,128)(2,1)}, u32[]{:S(2)}, u32[]{:S(2)}) collective-permute-start(bf16[2816,512]{0,1:T(8,128)(2,1)} %broadcast_select_fusion), channel_id=1, source_target_pairs={{0,2},{2,0},{4,6},{6,4},{1,3},{3,1},{5,7},{7,5},{8,10},{10,8},{12,... | collective-permute-start | bytes 8650760 | tf_op jit(solution)/shard_map/ppermute | solution.py:248
  1649.2 111.3 %collective-permute-start.78 = (bf16[2816,512]{0,1:T(8,128)(2,1)}, bf16[2816,512]{0,1:T(8,128)(2,1)}, u32[]{:S(2)}, u32[]{:S(2)}) collective-permute-start(bf16[2816,512]{0,1:T(8,128)(2,1)} %collective-permute-done.77), channel_id=1, source_target_pairs={{0,2},{2,0},{4,6},{6,4},{1,3},{3,1},{5,7},{7,5},{8,10},{10,8},{12,... | collective-permute-start | bytes 8650760 | tf_op jit(solution)/shard_map/ppermute | solution.py:249
  (126 other events, 3114.2 us)

commit v2 on v1

--- a/solution.py
+++ b/solution.py
@@ -212,65 +212,20 @@
     return value
 
 
-CORE_SWAP = [(0, 1), (1, 0), (2, 3), (3, 2)]
-X_SWAP = [(0, 2), (2, 0), (1, 3), (3, 1)]
-INWARD = [(0, 1), (3, 2)]
-MIDDLE = [(1, 2), (2, 1)]
-OUTWARD = [(1, 0), (2, 3)]
-
-
-def reduce_quarters(make):
-    dp_index = lax.axis_index("dp")
-    obj_index = lax.axis_index("obj")
-    x_bit, core_bit = dp_index // 2, dp_index % 2
-
-    def quarter(x_same, core_same):
-        x_at = x_bit if x_same else 1 - x_bit
-        core_at = core_bit if core_same else 1 - core_bit
-        return 2 * x_at + core_at
-
-    give_far = make(quarter(False, False)).astype(BF16)
-    give_near = make(quarter(True, False)).astype(BF16)
-    got_far = lax.ppermute(give_far, "dp", CORE_SWAP)
-    got_near = lax.ppermute(give_near, "dp", CORE_SWAP)
-    far = (make(quarter(False, True)) + got_far.astype(F32)).astype(BF16)
-    near = make(quarter(True, True)) + got_near.astype(F32)
-    near = near + lax.ppermute(far, "dp", X_SWAP).astype(F32)
-    near_low = near.astype(BF16)
-    side = (near + lax.ppermute(near_low, "obj", INWARD).astype(F32)).astype(BF16)
-    both = side + lax.ppermute(side, "obj", MIDDLE)
-    in_middle = (obj_index == 1) | (obj_index == 2)
-    mine = jnp.where(in_middle, both, lax.ppermute(both, "obj", OUTWARD))
-    across = lax.ppermute(mine, "dp", X_SWAP)
-    return (
-        mine,
-        across,
-        lax.ppermute(mine, "dp", CORE_SWAP),
-        lax.ppermute(across, "dp", CORE_SWAP),
-    )
-
-
-def in_order(quarters, axis):
-    mine, across, mine_c, across_c = quarters
-    dp_index = lax.axis_index("dp")
-    x_is0 = dp_index // 2 == 0
-    core_is0 = dp_index % 2 == 0
-    c0_near, c1_near = jnp.where(core_is0, mine, mine_c), jnp.where(core_is0, mine_c, mine)
-    c0_far, c1_far = jnp.where(core_is0, across, across_c), jnp.where(core_is0, across_c, across)
-    return jnp.concatenate(
-        [
-            jnp.where(x_is0, c0_near, c0_far),
-            jnp.where(x_is0, c1_near, c1_far),
-            jnp.where(x_is0, c0_far, c0_near),
-            jnp.where(x_is0, c1_far, c1_near),
-        ],
-        axis=axis,
-    ).astype(F32)
-
-
-def columns(array, index, count=4):
-    width = array.shape[-1] // count
-    return lax.dynamic_slice_in_dim(array, index * width, width, array.ndim - 1)
+GROUP = ("obj", "dp")
+
+
+def reduce_share(partial):
+    return lax.psum_scatter(partial.astype(BF16), GROUP, scatter_dimension=0, tiled=True)
+
+
+def gather_shares(share):
+    return lax.all_gather(share, GROUP, axis=0, tiled=True)
+
+
+def gather_after(share, earlier):
+    share, earlier = lax.optimization_barrier((share, earlier))
+    return gather_shares(share), earlier
 
 
 def token_sum(left, right):
@@ -368,27 +323,35 @@
         )
         return jnp.stack([d_hidden * slope, d_hidden * act], axis=0).astype(BF16)
 
-    grad_down = reduce_quarters(lambda q: token_sum(hidden, columns(d_ffn, q)))
+    partial_down, d_ffn_own, d_ffn_other = lax.optimization_barrier(
+        (token_sum(hidden, d_ffn).astype(BF16), d_ffn_own, d_ffn_other)
+    )
+    share_down = reduce_share(partial_down)
     d_gu_own = feed_back(d_ffn_own, slope_own, act_own)
     d_gu_other = feed_back(d_ffn_other, slope_other, act_other)
     d_gu = jnp.concatenate([d_gu_own, d_gu_other], axis=1)
     h_rows = jnp.concatenate([h_own, h_other], axis=0)
-    grad_gate_up = [
-        reduce_quarters(lambda q, k=k: token_sum(columns(h_rows, q), d_gu[k])) for k in range(2)
-    ]
+    partial_gate_up = [token_sum(h_rows, d_gu[k]).astype(BF16) for k in range(2)]
 
     def feed_rows(d_gate_up):
         return jnp.einsum("kte,dke->td", d_gate_up, w_gate_up, preferred_element_type=F32)
 
     d_h_send = feed_rows(d_gu_other).astype(BF16)
     d_h = scatter_rows(feed_rows(d_gu_own), d_h_send)
+    d_h, partial_gate_up[0] = lax.optimization_barrier((d_h, partial_gate_up[0]))
     d_z_one, d_gain_one, d_bias_one = norm_back(
         DEEP_ALPHA * d_z_two + d_h, zhat_one, scale_one, gain_one
     )
     d_attn_own = d_z_one.astype(BF16)
-    d_attn_other = gather_rows(d_attn_own)
+    d_attn_other, partial_gate_up[1] = lax.optimization_barrier(
+        (gather_rows(d_attn_own), partial_gate_up[1])
+    )
+    share_gate_up = [reduce_share(partial) for partial in partial_gate_up]
     d_attn = jnp.concatenate([d_attn_own, d_attn_other], axis=0)
-    grad_out = reduce_quarters(lambda q: token_sum(mixed, columns(d_attn, q)))
+    partial_out, d_attn_own, d_attn_other = lax.optimization_barrier(
+        (token_sum(mixed, d_attn).astype(BF16), d_attn_own, d_attn_other)
+    )
+    share_out = reduce_share(partial_out)
 
     def unmix(d_rows):
         return lax.dot_general(
@@ -396,16 +359,20 @@
         ).astype(BF16)
 
     d_mixed = jnp.concatenate([unmix(d_attn_own), unmix(d_attn_other)], axis=0)
+    d_mixed, share_down = lax.optimization_barrier((d_mixed, share_down))
     d_qkv = attend_back(info, qkv, d_mixed, cos_vals, sin_vals)
+    d_qkv, share_gate_up[0] = lax.optimization_barrier((d_qkv, share_gate_up[0]))
     x_rows = jnp.concatenate([x_own, x_other], axis=0)
-    grad_qkv = [
-        reduce_quarters(lambda q, k=k: token_sum(columns(x_rows, q), d_qkv[k])) for k in range(3)
-    ]
+    partial_qkv = [token_sum(x_rows, d_qkv[k]).astype(BF16) for k in range(3)]
 
     def unproject(d_rows):
         return jnp.einsum("kte,dke->td", d_rows, w_qkv, preferred_element_type=F32)
 
     d_x_send = unproject(d_qkv[:, share_len:]).astype(BF16)
+    d_x_send, share_gate_up[1], share_out, partial_qkv = lax.optimization_barrier(
+        (d_x_send, share_gate_up[1], share_out, partial_qkv)
+    )
+    share_qkv = [reduce_share(partial) for partial in partial_qkv]
     d_x = scatter_rows(unproject(d_qkv[:, :share_len]), d_x_send)
     input_grad = DEEP_ALPHA * d_z_one + d_x
 
@@ -414,15 +381,32 @@
     )
     local = width // lax.axis_size("tp")
     norm_terms = lax.dynamic_slice_in_dim(norm_terms, tp_index * local, local, 1)
+
+    share_gate_up = jnp.stack(share_gate_up, axis=1)
+    share_qkv = jnp.concatenate(share_qkv, axis=1)
+    share_rows = jnp.concatenate([share_down, share_out], axis=0)
+    input_grad, share_gate_up, share_qkv, share_rows = lax.optimization_barrier(
+        (input_grad, share_gate_up, share_qkv, share_rows)
+    )
+    grad_gate_up = gather_shares(share_gate_up)
+    grad_qkv, grad_gate_up = gather_after(share_qkv, grad_gate_up)
+    grad_rows, grad_qkv = gather_after(share_rows, grad_qkv)
+    grad_gate_up = grad_gate_up.astype(F32)
+    grad_qkv = jnp.stack(jnp.split(grad_qkv, 3, axis=1), axis=1).astype(F32)
+    group_size = lax.axis_size(GROUP)
+    grad_rows = grad_rows.reshape(group_size, -1, width).astype(F32)
+    down_rows = local_ff // group_size
+    grad_down = grad_rows[:, :down_rows].reshape(-1, width)
+    grad_out = grad_rows[:, down_rows:].reshape(-1, width)
     return (
         outputs[None],
         input_grad[None],
-        jnp.stack([in_order(g, 0) for g in grad_qkv], axis=1),
-        in_order(grad_out, 1),
+        grad_qkv,
+        grad_out,
         norm_terms[0],
         norm_terms[1],
-        jnp.stack([in_order(g, 0) for g in grad_gate_up], axis=1),
-        in_order(grad_down, 1),
+        grad_gate_up,
+        grad_down,
         norm_terms[2],
         norm_terms[3],
     )

time: 1820 us -> 1430 us (0.79)
  other arithmetic: 220 us -> 67.4 us
  waiting for transfers between devices: 983 us -> 878 us
  starting transfers between devices: 85 us -> 19.6 us
  local copies, waits for them, and re-layouts: 118 us -> 70.1 us
  matrix products: 332 us -> 304 us
    ppermute x63 -> x0, waiting for transfers between devices: 796 us -> none  [the longest x7 374 us: reduce_quarters(): mine = jnp.where(in_middle, both, lax.ppermute(both, 'obj', OUTWARD))]
    reduce_scatter x0 -> x7, waiting for transfers between devices: none -> 364 us  [reduce_share(): lax.psum_scatter(partial.astype(BF16), GROUP, scatter_dimension=0, tiled=...]
    all_gather x0 -> x3, waiting for transfers between devices: none -> 265 us  [gather_shares(): return lax.all_gather(share, GROUP, axis=0, tiled=True)]
    unnamed x162 -> x81, local copies, waits for them, and re-layouts: 116 us -> 50.9 us
    ppermute x63 -> x0, starting transfers between devices: 64.9 us -> none  [the longest x7 23.4 us: reduce_quarters(): lax.ppermute(near_low, 'obj', INWARD).astype(F32)]
    convert_element_type x9 -> x1, other arithmetic: 57 us -> 8.8 us  [body(): grad_qkv = jnp.stack(jnp.split(grad_qkv, 3, axis=1), axis=1).astype(F32)]
    another operation x2 -> x1, other arithmetic: 49 us -> 1.23 us  [body(): share_gate_up = jnp.stack(share_gate_up, axis=1)]
    dot_general x28 -> x7, matrix products: 132 us -> 89.7 us  [token_sum(): lax.dot_general(left, right, (((0,), (0,)), ((), ())), preferred_element_...]
  transfers between devices with their start and end apart: 79 -> 26, of which waited for: 32 -> 23; matrix products, arithmetic and copies ran while one was open for 27% -> 23% of each run, Pallas kernels for 2% -> 3%
where the time goes in v2:
time: 1430 us
  waiting for transfers between devices  878 us (61%)
  matrix products  304 us (21%)
  Pallas kernels  70.3 us (5%)
  local copies, waits for them, and re-layouts  70.1 us (5%)
  other arithmetic  67.4 us (5%)
  starting transfers between devices  19.6 us (1%)
  between operations  16.2 us (1%)
    reduce_scatter x7, waiting for transfers between devices, reduce_share(): lax.psum_scatter(partial.astype(BF16), GROUP, scatter_dimension=0, tiled=...  364 us
    all_gather x3, waiting for transfers between devices, gather_shares(): return lax.all_gather(share, GROUP, axis=0, tiled=True)  265 us
    ppermute x4, waiting for transfers between devices, gather_rows(): return lax.ppermute(own, 'tp', [(0, 1), (1, 0)])  96.7 us
    ppermute x4, waiting for transfers between devices, scatter_rows(): lax.ppermute(send_part, 'tp', [(0, 1), (1, 0)]).astype(F32)  94.8 us
    dot_general x7, matrix products, token_sum(): lax.dot_general(left, right, (((0,), (0,)), ((), ())), preferred_element_...  89.7 us
    ppermute x8, waiting for transfers between devices, all_sum(): lax.ppermute(value, axis, [(i, i ^ step) for i in range(size)])  55.5 us
    unnamed x81, local copies, waits for them, and re-layouts  50.9 us
    dot_general x2, matrix products, feed(): jnp.einsum('td,dke->tke', rows, w_gate_up, preferred_element_type=F32)  50.8 us
  transfers between devices with their start and end apart: 26, of which 23 were waited for; matrix products, arithmetic and copies ran while one was open for 23% of the time, Pallas kernels for 3%

profile of v2, /device:TPU:0, one launch (start us, length us, event | category | flops | bytes accessed | tf_op | source)
XLA Modules:
  0.0 1425.5 jit_solution(3394190721205359772)
XLA Ops:
  14.8 11.6 convolution_bitcast_fusion.1.own_ref
  26.4 29.8 %collective-permute-done = bf16[512,2048]{1,0:T(8,128)(2,1)} collective-permute-done((bf16[512,2048]{1,0:T(8,128)(2,1)}, bf16[512,2048]{1,0:T(8,128)(2,1)}, u32[]{:S(2)}, u32[]{:S(2)}) %collective-permute-start) | collective-permute-done | bytes 2097184 | tf_op jit(solution)/shard_map/ppermute | solution.py:185
  66.3 27.3 %attend.1 = (bf16[1024,1024]{1,0:T(8,128)(2,1)}, bf16[3,1024,1024]{2,1,0:T(8,128)(2,1)}) custom-call(s32[2]{0:T(128)} %pad_add_fusion.info_ref, f32[3,512,1024]{2,1,0:T(8,128)} %convolution_bitcast_fusion.1.own_ref, f32[3,512,1024]{2,1,0:T(8,128)} %convolution_bitcast_fusion.other_ref, f32[1024,128]{1,0:T(8,128)} %get-tuple-element.128.cos_ref, ...), custom_call_target="tpu_custom_call" | custom-call | flops 8589934592 | bytes 20971520 | tf_op jit(solution)/shard_map/attend/pallas_call | solution.py:120
  100.4 45.1 %collective-permute-done.1 = bf16[512,2048]{1,0:T(8,128)(2,1)S(1)} collective-permute-done((bf16[512,2048]{1,0:T(8,128)(2,1)S(1)}, bf16[512,2048]{1,0:T(8,128)(2,1)S(1)}, u32[]{:S(2)}, u32[]{:S(2)}) %collective-permute-start.1) | collective-permute-done | bytes 2097184 | tf_op jit(solution)/shard_map/ppermute | solution.py:197
  159.4 36.5 %collective-permute-done.6 = f32[8,128]{1,0:T(8,128)S(1)} collective-permute-done((f32[8,128]{1,0:T(8,128)S(1)}, f32[8,128]{1,0:T(8,128)S(1)}, u32[]{:S(2)}, u32[]{:S(2)}) %collective-permute-start.6) | collective-permute-done | bytes 4128 | tf_op jit(solution)/shard_map/ppermute | solution.py:210
  197.1 21.4 %fusion.4 = f32[512,2,2816]{2,0,1:T(8,128)} fusion(bf16[2048,2,2816]{2,1,0:T(2,128)(2,1)} %param.20, bf16[512,2048]{1,0:T(8,128)(2,1)} %collective-permute-done.2), kind=kOutput, calls=%fused_computation.4 | convolution fusion | flops 11811160064 | bytes 36700160 | tf_op jit(solution)/shard_map/td,dke->tke/dot_general | solution.py:296
  226.9 11.0 convolution_convert_fusion.7
  239.1 29.4 %fusion.6 = f32[512,2,2816]{2,0,1:T(8,128)} fusion(bf16[2048,2,2816]{2,1,0:T(2,128)(2,1)} %param.20, bf16[512,2048]{1,0:T(8,128)(2,1)S(1)} %fusion.50), kind=kOutput, calls=%fused_computation.6 | convolution fusion | flops 11811160064 | bytes 36700160 | tf_op jit(solution)/shard_map/td,dke->tke/dot_general | solution.py:296
  302.5 43.5 %collective-permute-done.7 = bf16[512,2048]{1,0:T(8,128)(2,1)} collective-permute-done((bf16[512,2048]{1,0:T(8,128)(2,1)S(1)}, bf16[512,2048]{1,0:T(8,128)(2,1)}, u32[]{:S(2)}, u32[]{:S(2)}) %collective-permute-start.7) | collective-permute-done | bytes 2097184 | tf_op jit(solution)/shard_map/ppermute | solution.py:185
  346.1 16.7 %convolution_convert_fusion.2 = bf16[2816,2048]{1,0:T(8,128)(2,1)} fusion(bf16[512,2816]{1,0:T(8,128)(2,1)S(1)} %copy-done.7, bf16[512,2816]{1,0:T(8,128)(2,1)S(1)} %copy-done.9, bf16[512,2048]{1,0:T(8,128)(2,1)} %collective-permute-done.7, bf16[512,2048]{1,0:T(8,128)(2,1)S(1)} %fusion.97), kind=kOutput, calls=%fused_computation.12 | convolution fusion | flops 11836850176 | bytes 21495808 | tf_op jit(solution)/shard_map/dot_general | solution.py:232
  362.8 16.2 %fusion.63 = (bf16[1,512,2816]{2,1,0:T(8,128)(2,1)}, bf16[1,512,2816]{2,1,0:T(8,128)(2,1)}) fusion(f32[512,2816]{1,0:T(8,128)} %get-tuple-element.53, f32[512,2816]{1,0:T(8,128)} %get-tuple-element.54, bf16[512,2048]{1,0:T(8,128)(2,1)} %collective-permute-done.7, bf16[2816,2048]{1,0:T(8,128)(2,1)} %param.21), kind=kOutput, calls=%fused_computation.102 | convolution fusion | flops 5911347200 | bytes 30932992 | tf_op jit(solution)/shard_map/dot_general | solution.py:321
  379.0 23.6 %bitcast_convert_fusion.1 = bf16[512,2048]{1,0:T(8,128)(2,1)} fusion(bf16[2048,2,2816]{2,1,0:T(2,128)(2,1)} %param.20, bf16[1,512,2816]{2,1,0:T(8,128)(2,1)} %get-tuple-element.117, bf16[1,512,2816]{2,1,0:T(8,128)(2,1)} %get-tuple-element.116), kind=kOutput, calls=%fused_computation.73 | convolution fusion | flops 11815092224 | bytes 30932992 | tf_op jit(solution)/shard_map/kte,dke->td/dot_general | solution.py:337
  403.0 15.4 %fusion.61 = (bf16[1,512,2816]{2,1,0:T(8,128)(2,1)}, bf16[1,512,2816]{2,1,0:T(8,128)(2,1)}) fusion(f32[512,2816]{1,0:T(8,128)} %get-tuple-element.50, f32[512,2816]{1,0:T(8,128)} %get-tuple-element.51, bf16[512,2048]{1,0:T(8,128)(2,1)} %copy-done.12, bf16[2816,2048]{1,0:T(8,128)(2,1)} %param.21), kind=kOutput, calls=%fused_computation.100 | convolution fusion | flops 5911347200 | bytes 30932992 | tf_op jit(solution)/shard_map/dot_general | solution.py:321
  418.4 10.9 maximum_maximum_fusion
  429.3 18.0 %convolution_convert_fusion.1 = bf16[2048,2816]{1,0:T(8,128)(2,1)} fusion(bf16[2,1024,2816]{2,1,0:T(8,128)(2,1)} %maximum_maximum_fusion, bf16[512,2048]{1,0:T(8,128)(2,1)} %collective-permute-done.2, bf16[512,2048]{1,0:T(8,128)(2,1)S(1)} %copy-done.14), kind=kOutput, calls=%fused_computation.11 | convolution fusion | flops 11825315840 | bytes 21495808 | tf_op jit(solution)/shard_map/dot_general | solution.py:232
  447.3 22.5 %bitcast_add_fusion.1 = f32[512,2048]{1,0:T(8,128)} fusion(bf16[512,2048]{1,0:T(8,128)(2,1)} %collective-permute-done.8, bf16[2048,2,2816]{2,1,0:T(2,128)(2,1)} %param.20, bf16[1,512,2816]{2,1,0:T(8,128)(2,1)} %get-tuple-element.115, bf16[1,512,2816]{2,1,0:T(8,128)(2,1)} %get-tuple-element.114), kind=kOutput, calls=%fused_computation.74 | convolution fusion | flops 11816140800 | bytes 35127296 | tf_op jit(solution)/shard_map/kte,dke->td/dot_general | solution.py:337
  484.6 17.8 %convolution_convert_fusion = bf16[2048,2816]{1,0:T(8,128)(2,1)} fusion(bf16[2,1024,2816]{2,1,0:T(8,128)(2,1)S(1)} %bitcast.152, bf16[512,2048]{1,0:T(8,128)(2,1)} %collective-permute-done.2, bf16[512,2048]{1,0:T(8,128)(2,1)} %copy-done.13), kind=kOutput, calls=%fused_computation.10 | convolution fusion | flops 11825315840 | bytes 21495808 | tf_op jit(solution)/shard_map/dot_general | solution.py:232
  502.4 23.3 %collective-permute-done.9 = bf16[512,2048]{1,0:T(8,128)(2,1)} collective-permute-done((bf16[512,2048]{1,0:T(8,128)(2,1)}, bf16[512,2048]{1,0:T(8,128)(2,1)}, u32[]{:S(2)}, u32[]{:S(2)}) %collective-permute-start.9) | collective-permute-done | bytes 2097184 | tf_op jit(solution)/shard_map/ppermute | solution.py:185
  547.9 43.0 %attend_back.1 = bf16[3,1024,1024]{2,1,0:T(8,128)(2,1)} custom-call(s32[2]{0:T(128)} %pad_add_fusion.info_ref, bf16[3,1024,1024]{2,1,0:T(8,128)(2,1)} %get-tuple-element.56.qkv_ref, bf16[1024,1024]{1,0:T(8,128)(2,1)} %pad_maximum_fusion.4.grad_ref, f32[1024,128]{1,0:T(8,128)} %get-tuple-element.128.cos_ref, f32[1024,128]{1,0:T(8,128)} %get-tuple-element.129.sin_ref), custom_call_target="tpu_custom_call" | custom-call | flops 21474836480 | bytes 14680064 | tf_op jit(solution)/shard_map/attend_back/pallas_call | solution.py:154
  590.9 30.5 %reduce-scatter.10.cloned.1.call-done = bf16[128,2816]{1,0:T(8,128)(2,1)} async-done(((bf16[2048,2816]{1,0:T(8,128)(2,1)}), bf16[128,2816]{1,0:T(8,128)(2,1)}) %reduce-scatter.10.cloned.1.call-update) | async-done | bytes 720912 | tf_op jit(solution)/shard_map/reduce_scatter | solution.py:219
  648.4 11.6 bitcast_convert_fusion
  660.0 37.4 %reduce-scatter.14.cloned.1.call-done = bf16[64,2048]{1,0:T(8,128)(2,1)} async-done(((bf16[1024,2048]{1,0:T(8,128)(2,1)}), bf16[64,2048]{1,0:T(8,128)(2,1)}) %reduce-scatter.14.cloned.1.call-update) | async-done | bytes 262160 | tf_op jit(solution)/shard_map/reduce_scatter | solution.py:219
  697.4 130.6 %reduce-scatter.12.cloned.1.call-done = bf16[128,2816]{1,0:T(8,128)(2,1)} async-done(((bf16[2048,2816]{1,0:T(8,128)(2,1)}), bf16[128,2816]{1,0:T(8,128)(2,1)}) %reduce-scatter.12.cloned.1.call-update) | async-done | bytes 720912 | tf_op jit(solution)/shard_map/reduce_scatter | solution.py:219
  833.3 43.3 %collective-permute-done.10 = bf16[512,2048]{1,0:T(8,128)(2,1)} collective-permute-done((bf16[512,2048]{1,0:T(8,128)(2,1)}, bf16[512,2048]{1,0:T(8,128)(2,1)}, u32[]{:S(2)}, u32[]{:S(2)}) %collective-permute-start.10) | collective-permute-done | bytes 2097184 | tf_op jit(solution)/shard_map/ppermute | solution.py:197
  876.5 14.6 %fusion.46 = f32[512,2048]{1,0:T(8,128)} fusion(bf16[512,2048]{1,0:T(8,128)(2,1)} %collective-permute-done.10, f32[512,2048]{1,0:T(8,128)} %get-tuple-element.101, bf16[2048,3,1024]{2,0,1:T(8,128)(2,1)} %param.16, bf16[3,1024,1024]{2,1,0:T(8,128)(2,1)} %attend_back.1), kind=kOutput, calls=%fused_computation.72 | convolution fusion | flops 6446645248 | bytes 26214400 | tf_op jit(solution)/shard_map/kte,dke->td/dot_general | solution.py:369
  891.1 13.4 reduce-scatter.20.cloned.1.call-done
  904.5 76.1 %reduce-scatter.18.cloned.1.call-done = bf16[128,1024]{1,0:T(8,128)(2,1)} async-done(((bf16[2048,1024]{1,0:T(8,128)(2,1)}), bf16[128,1024]{1,0:T(8,128)(2,1)}) %reduce-scatter.18.cloned.1.call-update) | async-done | bytes 262160 | tf_op jit(solution)/shard_map/reduce_scatter | solution.py:219
  980.6 75.7 %reduce-scatter.16.cloned.1.call-done = bf16[128,1024]{1,0:T(8,128)(2,1)} async-done(((bf16[2048,1024]{1,0:T(8,128)(2,1)}), bf16[128,1024]{1,0:T(8,128)(2,1)}) %reduce-scatter.16.cloned.1.call-update) | async-done | bytes 262160 | tf_op jit(solution)/shard_map/reduce_scatter | solution.py:219
  1058.4 117.8 %all-gather.4.cloned.1.call-done = bf16[2048,2,2816]{2,0,1:T(8,128)(2,1)} async-done(((bf16[128,2,2816]{2,0,1:T(8,128)(2,1)}), bf16[2048,2,2816]{2,0,1:T(8,128)(2,1)}) %all-gather.4.cloned.1.call-update) | async-done | bytes 23068688 | tf_op jit(solution)/shard_map/all_gather | solution.py:223
  1176.3 103.2 %all-gather.6.cloned.1.call-done = bf16[2048,3072]{1,0:T(8,128)(2,1)} async-done(((bf16[128,3072]{1,0:T(8,128)(2,1)}), bf16[2048,3072]{1,0:T(8,128)(2,1)}) %all-gather.6.cloned.1.call-update) | async-done | bytes 12582928 | tf_op jit(solution)/shard_map/all_gather | solution.py:223
  1300.7 45.3 %copy.30 = f32[2048,2,2816]{2,1,0:T(2,128)} copy(bf16[2048,2,2816]{2,0,1:T(8,128)(2,1)} %all-gather.4.cloned.1.call-done) | data formatting | bytes 69206016
  1356.3 44.1 %all-gather.8.cloned.1.call-done = bf16[3840,2048]{1,0:T(8,128)(2,1)} async-done(((bf16[240,2048]{1,0:T(8,128)(2,1)}), bf16[3840,2048]{1,0:T(8,128)(2,1)}) %all-gather.8.cloned.1.call-update) | async-done | bytes 15728656 | tf_op jit(solution)/shard_map/all_gather | solution.py:223
  (183 shorter events, 202.5 us)
Async XLA Ops:
  7.2 540.7 %reduce-scatter.8.cloned.1.call-start = ((), (), s32[]{:S(2)}) async-start(), calls=%async_computation.7 | async-start | bytes 12255232 | tf_op jit(solution)/shard_map/reduce_scatter | solution.py:219
  7.2 49.0 %collective-permute-start = (bf16[512,2048]{1,0:T(8,128)(2,1)}, bf16[512,2048]{1,0:T(8,128)(2,1)}, u32[]{:S(2)}, u32[]{:S(2)}) collective-permute-start(bf16[512,2048]{1,0:T(8,128)(2,1)} %bitcast.154), channel_id=1, source_target_pairs={{0,1},{1,0},{2,3},{3,2},{4,5},{5,4},{6,7},{7,6},{8,9},{9,8},{10,11... | collective-permute-start | bytes 6291464 | tf_op jit(solution)/shard_map/ppermute | solution.py:185
  98.6 46.9 %collective-permute-start.1 = (bf16[512,2048]{1,0:T(8,128)(2,1)S(1)}, bf16[512,2048]{1,0:T(8,128)(2,1)S(1)}, u32[]{:S(2)}, u32[]{:S(2)}) collective-permute-start(bf16[512,2048]{1,0:T(8,128)(2,1)S(1)} %convolution_convert_fusion.6), channel_id=1, source_target_pairs={{0,1},{1,0},{2,3},{3,2},{4,5},{5,4},{6,7},{7,6},{8,9},{9,8},{10,11... | collective-permute-start | bytes 6291464 | tf_op jit(solution)/shard_map/ppermute | solution.py:197
  148.2 135.2 %copy-start.1 = (f32[512,2048]{1,0:T(8,128)}, f32[512,2048]{1,0:T(8,128)S(1)}, u32[]{:S(2)}) copy-start(f32[512,2048]{1,0:T(8,128)S(1)} %get-tuple-element.127) | copy-start | bytes 12582916
  148.2 135.2 %copy-start.24 = (f32[512]{0:T(512)}, f32[512]{0:T(512)S(1)}, u32[]{:S(2)}) copy-start(f32[512]{0:T(512)S(1)} %broadcast_multiply_fusion.5) | copy-start | bytes 6148
  149.0 134.4 %copy-start.26 = (f32[512]{0:T(512)}, f32[512]{0:T(512)S(1)}, u32[]{:S(2)}) copy-start(f32[512]{0:T(512)S(1)} %add_rsqrt_fusion.1) | copy-start | bytes 6148
  149.7 89.4 %copy-start.13 = (bf16[512,2048]{1,0:T(8,128)(2,1)}, bf16[512,2048]{1,0:T(8,128)(2,1)S(1)}, u32[]{:S(2)}) copy-start(bf16[512,2048]{1,0:T(8,128)(2,1)S(1)} %fusion.50) | copy-start | bytes 6291460
  149.8 47.4 %collective-permute-start.2 = (bf16[512,2048]{1,0:T(8,128)(2,1)S(1)}, bf16[512,2048]{1,0:T(8,128)(2,1)}, u32[]{:S(2)}, u32[]{:S(2)}) collective-permute-start(bf16[512,2048]{1,0:T(8,128)(2,1)S(1)} %fusion.50), channel_id=1, source_target_pairs={{0,1},{1,0},{2,3},{3,2},{4,5},{5,4},{6,7},{7,6},{8,9},{9,8},{10,11... | collective-permute-start | bytes 6291464 | tf_op jit(solution)/shard_map/ppermute | solution.py:185
  152.5 1.2 collective-permute-start.4
  154.4 3.7 collective-permute-start.5
  158.8 37.2 %collective-permute-start.6 = (f32[8,128]{1,0:T(8,128)S(1)}, f32[8,128]{1,0:T(8,128)S(1)}, u32[]{:S(2)}, u32[]{:S(2)}) collective-permute-start(f32[8,128]{1,0:T(8,128)S(1)} %fusion.124), channel_id=1, source_target_pairs={{0,1},{1,0},{2,3},{3,2},{4,5},{5,4},{6,7},{7,6},{8,9},{9,8},{10,11... | collective-permute-start | bytes 12296 | tf_op jit(solution)/shard_map/ppermute | solution.py:210
  237.9 45.5 %collective-permute-start.3 = (bf16[512,2048]{1,0:T(8,128)(2,1)}, bf16[512,2048]{1,0:T(8,128)(2,1)}, u32[]{:S(2)}, u32[]{:S(2)}) collective-permute-start(bf16[512,2048]{1,0:T(8,128)(2,1)} %convolution_convert_fusion.7), channel_id=1, source_target_pairs={{0,1},{1,0},{2,3},{3,2},{4,5},{5,4},{6,7},{7,6},{8,9},{9,8},{10,11... | collective-permute-start | bytes 6291464 | tf_op jit(solution)/shard_map/ppermute | solution.py:197
  301.6 44.5 %collective-permute-start.7 = (bf16[512,2048]{1,0:T(8,128)(2,1)S(1)}, bf16[512,2048]{1,0:T(8,128)(2,1)}, u32[]{:S(2)}, u32[]{:S(2)}) collective-permute-start(bf16[512,2048]{1,0:T(8,128)(2,1)S(1)} %fusion.97), channel_id=1, source_target_pairs={{0,1},{1,0},{2,3},{3,2},{4,5},{5,4},{6,7},{7,6},{8,9},{9,8},{10,11... | collective-permute-start | bytes 6291464 | tf_op jit(solution)/shard_map/ppermute | solution.py:185
  362.8 258.6 %reduce-scatter.10.cloned.1.call-start = ((), (), s32[]{:S(2)}) async-start(), calls=%async_computation.8 | async-start | bytes 12255232 | tf_op jit(solution)/shard_map/reduce_scatter | solution.py:219
  402.6 44.7 %collective-permute-start.8 = (bf16[512,2048]{1,0:T(8,128)(2,1)}, bf16[512,2048]{1,0:T(8,128)(2,1)}, u32[]{:S(2)}, u32[]{:S(2)}) collective-permute-start(bf16[512,2048]{1,0:T(8,128)(2,1)} %bitcast_convert_fusion.1), channel_id=1, source_target_pairs={{0,1},{1,0},{2,3},{3,2},{4,5},{5,4},{6,7},{7,6},{8,9},{9,8},{10,11... | collective-permute-start | bytes 6291464 | tf_op jit(solution)/shard_map/ppermute | solution.py:197
  469.8 227.6 %reduce-scatter.14.cloned.1.call-start = ((), (), s32[]{:S(2)}) async-start(), calls=%async_computation.10 | async-start | bytes 4456448 | tf_op jit(solution)/shard_map/reduce_scatter | solution.py:219
  483.0 42.7 %collective-permute-start.9 = (bf16[512,2048]{1,0:T(8,128)(2,1)}, bf16[512,2048]{1,0:T(8,128)(2,1)}, u32[]{:S(2)}, u32[]{:S(2)}) collective-permute-start(bf16[512,2048]{1,0:T(8,128)(2,1)} %get-tuple-element.58), channel_id=1, source_target_pairs={{0,1},{1,0},{2,3},{3,2},{4,5},{5,4},{6,7},{7,6},{8,9},{9,8},{10,11... | collective-permute-start | bytes 6291464 | tf_op jit(solution)/shard_map/ppermute | solution.py:185
  536.0 292.1 %reduce-scatter.12.cloned.1.call-start = ((), (), s32[]{:S(2)}) async-start(), calls=%async_computation.9 | async-start | bytes 12255232 | tf_op jit(solution)/shard_map/reduce_scatter | solution.py:219
  536.6 367.9 %reduce-scatter.20.cloned.1.call-start = ((), (), s32[]{:S(2)}) async-start(), calls=%async_computation.13 | async-start | bytes 4456448 | tf_op jit(solution)/shard_map/reduce_scatter | solution.py:219
  828.1 152.5 %reduce-scatter.18.cloned.1.call-start = ((), (), s32[]{:S(2)}) async-start(), calls=%async_computation.12 | async-start | bytes 4456448 | tf_op jit(solution)/shard_map/reduce_scatter | solution.py:219
  828.7 227.6 %reduce-scatter.16.cloned.1.call-start = ((), (), s32[]{:S(2)}) async-start(), calls=%async_computation.11 | async-start | bytes 4456448 | tf_op jit(solution)/shard_map/reduce_scatter | solution.py:219
  829.4 346.8 %all-gather.4.cloned.1.call-start = ((), (), s32[]{:S(2)}) async-start(), calls=%async_computation.14 | async-start | bytes 24510464 | tf_op jit(solution)/shard_map/all_gather | solution.py:223
  829.5 47.0 %collective-permute-start.10 = (bf16[512,2048]{1,0:T(8,128)(2,1)}, bf16[512,2048]{1,0:T(8,128)(2,1)}, u32[]{:S(2)}, u32[]{:S(2)}) collective-permute-start(bf16[512,2048]{1,0:T(8,128)(2,1)} %bitcast_convert_fusion), channel_id=1, source_target_pairs={{0,1},{1,0},{2,3},{3,2},{4,5},{5,4},{6,7},{7,6},{8,9},{9,8},{10,11... | collective-permute-start | bytes 6291464 | tf_op jit(solution)/shard_map/ppermute | solution.py:197
  891.1 388.5 %copy-start.19 = (f32[2048]{0:T(1024)S(1)}, f32[2048]{0:T(1024)}, u32[]{:S(2)}) copy-start(f32[2048]{0:T(1024)} %get-tuple-element.94) | copy-start | bytes 24580
  891.1 388.5 %copy-start.20 = (f32[2048]{0:T(1024)S(1)}, f32[2048]{0:T(1024)}, u32[]{:S(2)}) copy-start(f32[2048]{0:T(1024)} %get-tuple-element.99) | copy-start | bytes 24580
  1058.4 221.2 %all-gather.6.cloned.1.call-start = ((), (), s32[]{:S(2)}) async-start(), calls=%async_computation.15 | async-start | bytes 13369344 | tf_op jit(solution)/shard_map/all_gather | solution.py:223
  1176.3 224.1 %all-gather.8.cloned.1.call-start = ((), (), s32[]{:S(2)}) async-start(), calls=%async_computation.16 | async-start | bytes 16711680 | tf_op jit(solution)/shard_map/all_gather | solution.py:223
  1279.6 1.3 collective-permute-start.11
  1280.9 4.0 collective-permute-start.12
  1285.0 4.0 collective-permute-start.13
  1289.0 7.1 collective-permute-start.14
  1296.1 4.0 collective-permute-start.15
  (34 other events, 621.7 us)
Sparse Core Ops, SparseCore 0:
  362.9 127.3 reduce-scatter.7
  494.9 126.3 reduce-scatter.9
  625.2 72.1 reduce-scatter.13
  701.9 126.0 reduce-scatter.11
  832.3 72.1 reduce-scatter.19
  908.8 71.7 reduce-scatter.17
  984.4 71.8 reduce-scatter.15
  1058.5 117.6 all-gather.3
  1179.1 100.3 all-gather.5
  1281.7 118.6 all-gather.7

commit v3 on v2

--- a/solution.py
+++ b/solution.py
@@ -212,20 +212,67 @@
     return value
 
 
-GROUP = ("obj", "dp")
-
-
-def reduce_share(partial):
-    return lax.psum_scatter(partial.astype(BF16), GROUP, scatter_dimension=0, tiled=True)
-
-
-def gather_shares(share):
+CORE_SWAP = [(0, 1), (1, 0), (2, 3), (3, 2)]
+X_SWAP = [(0, 2), (2, 0), (1, 3), (3, 1)]
+Z_NEAR = [(0, 1), (1, 0), (2, 3), (3, 2)]
+Z_FAR = [(0, 2), (2, 0), (1, 3), (3, 1)]
+GROUP = ("dp", "obj")
+tie = lax.optimization_barrier
+
+
+def columns(array, index, count=4):
+    width = array.shape[-1] // count
+    return lax.dynamic_slice_in_dim(array, index * width, width, array.ndim - 1)
+
+
+def give_quarters(make):
+    dp_index = lax.axis_index("dp")
+    return make(3 - dp_index).astype(BF16), make(dp_index ^ 1).astype(BF16)
+
+
+def core_stage(make, gives):
+    dp_index = lax.axis_index("dp")
+    got_far = lax.ppermute(gives[0], "dp", CORE_SWAP)
+    got_near = lax.ppermute(gives[1], "dp", CORE_SWAP)
+    far = (make(dp_index ^ 2) + got_far.astype(F32)).astype(BF16)
+    return far, make(dp_index) + got_near.astype(F32)
+
+
+def x_stage(far, near):
+    return near + lax.ppermute(far, "dp", X_SWAP).astype(F32)
+
+
+def z_near_stage(near, axis):
+    obj_index = lax.axis_index("obj")
+    width = near.shape[axis] // lax.axis_size("obj")
+
+    def pieces(first):
+        return jnp.stack(
+            [
+                lax.dynamic_slice_in_dim(near, index * width, width, axis)
+                for index in (first, first ^ 2)
+            ]
+        )
+
+    got = lax.ppermute(pieces(obj_index ^ 1).astype(BF16), "obj", Z_NEAR)
+    return pieces(obj_index) + got.astype(F32)
+
+
+def z_far_stage(pair):
+    got = lax.ppermute(pair[1].astype(BF16), "obj", Z_FAR)
+    return (pair[0] + got.astype(F32)).astype(BF16)
+
+
+def gather_rows_of(share):
     return lax.all_gather(share, GROUP, axis=0, tiled=True)
 
 
-def gather_after(share, earlier):
-    share, earlier = lax.optimization_barrier((share, earlier))
-    return gather_shares(share), earlier
+def gather_columns_of(share):
+    return lax.all_gather(share, GROUP, axis=0, tiled=False)
+
+
+def widen(stacked):
+    return jnp.concatenate([stacked[i] for i in range(stacked.shape[0])], axis=1).astype(F32)
 
 
 def token_sum(left, right):
@@ -323,35 +370,47 @@
         )
         return jnp.stack([d_hidden * slope, d_hidden * act], axis=0).astype(BF16)
 
-    partial_down, d_ffn_own, d_ffn_other = lax.optimization_barrier(
-        (token_sum(hidden, d_ffn).astype(BF16), d_ffn_own, d_ffn_other)
-    )
-    share_down = reduce_share(partial_down)
+    def make_down(q):
+        return token_sum(hidden, columns(d_ffn, q))
+
+    gives_down, d_ffn_own, d_ffn_other = tie((give_quarters(make_down), d_ffn_own, d_ffn_other))
+    d_gu_other = feed_back(d_ffn_other, slope_other, act_other)
+    (far_down, near_down), d_gu_other = tie((core_stage(make_down, gives_down), d_gu_other))
+    near_down = x_stage(far_down, near_down)
+
+    def feed_rows(d_gate_up):
+        return jnp.einsum("kte,dke->td", d_gate_up, w_gate_up, preferred_element_type=F32)
+
+    d_h_send = feed_rows(d_gu_other).astype(BF16)
     d_gu_own = feed_back(d_ffn_own, slope_own, act_own)
-    d_gu_other = feed_back(d_ffn_other, slope_other, act_other)
     d_gu = jnp.concatenate([d_gu_own, d_gu_other], axis=1)
     h_rows = jnp.concatenate([h_own, h_other], axis=0)
-    partial_gate_up = [token_sum(h_rows, d_gu[k]).astype(BF16) for k in range(2)]
-
-    def feed_rows(d_gate_up):
-        return jnp.einsum("kte,dke->td", d_gate_up, w_gate_up, preferred_element_type=F32)
-
-    d_h_send = feed_rows(d_gu_other).astype(BF16)
+
+    def make_gate(q):
+        return token_sum(columns(h_rows, q), d_gu[0])
+
+    def make_up(q):
+        return token_sum(columns(h_rows, q), d_gu[1])
+
     d_h = scatter_rows(feed_rows(d_gu_own), d_h_send)
-    d_h, partial_gate_up[0] = lax.optimization_barrier((d_h, partial_gate_up[0]))
+    d_h, (far_gate, near_gate) = tie((d_h, core_stage(make_gate, give_quarters(make_gate))))
+    near_gate = x_stage(far_gate, near_gate)
     d_z_one, d_gain_one, d_bias_one = norm_back(
         DEEP_ALPHA * d_z_two + d_h, zhat_one, scale_one, gain_one
     )
     d_attn_own = d_z_one.astype(BF16)
-    d_attn_other, partial_gate_up[1] = lax.optimization_barrier(
-        (gather_rows(d_attn_own), partial_gate_up[1])
-    )
-    share_gate_up = [reduce_share(partial) for partial in partial_gate_up]
+    d_attn_other = gather_rows(d_attn_own)
+    d_attn_other, (far_up, near_up), near_down = tie(
+        (d_attn_other, core_stage(make_up, give_quarters(make_up)), near_down)
+    )
+    near_up = x_stage(far_up, near_up)
+    pair_down = z_near_stage(near_down, 1)
     d_attn = jnp.concatenate([d_attn_own, d_attn_other], axis=0)
-    partial_out, d_attn_own, d_attn_other = lax.optimization_barrier(
-        (token_sum(mixed, d_attn).astype(BF16), d_attn_own, d_attn_other)
-    )
-    share_out = reduce_share(partial_out)
+
+    def make_out(q):
+        return token_sum(mixed, columns(d_attn, q))
+
+    gives_out, d_attn_own, d_attn_other = tie((give_quarters(make_out), d_attn_own, d_attn_other))
 
     def unmix(d_rows):
         return lax.dot_general(
@@ -359,20 +418,35 @@
         ).astype(BF16)
 
     d_mixed = jnp.concatenate([unmix(d_attn_own), unmix(d_attn_other)], axis=0)
-    d_mixed, share_down = lax.optimization_barrier((d_mixed, share_down))
+    d_mixed, (far_out, near_out), near_gate, pair_down = tie(
+        (d_mixed, core_stage(make_out, gives_out), near_gate, pair_down)
+    )
+    near_out = x_stage(far_out, near_out)
+    pair_gate = z_near_stage(near_gate, 0)
+    share_down = z_far_stage(pair_down)
     d_qkv = attend_back(info, qkv, d_mixed, cos_vals, sin_vals)
-    d_qkv, share_gate_up[0] = lax.optimization_barrier((d_qkv, share_gate_up[0]))
+    d_qkv, near_up, pair_gate, share_down = tie((d_qkv, near_up, pair_gate, share_down))
+    pair_up = z_near_stage(near_up, 0)
+    share_gate = z_far_stage(pair_gate)
     x_rows = jnp.concatenate([x_own, x_other], axis=0)
-    partial_qkv = [token_sum(x_rows, d_qkv[k]).astype(BF16) for k in range(3)]
+
+    def make_qkv(k):
+        return lambda q: token_sum(columns(x_rows, q), d_qkv[k])
+
+    gives_qkv = [give_quarters(make_qkv(k)) for k in range(3)]
 
     def unproject(d_rows):
         return jnp.einsum("kte,dke->td", d_rows, w_qkv, preferred_element_type=F32)
 
+    parts_qkv = [core_stage(make_qkv(k), gives_qkv[k]) for k in range(3)]
+    parts_qkv, near_out = tie((parts_qkv, near_out))
+    pair_out = z_near_stage(near_out, 1)
+    near_qkv = [x_stage(far, near) for far, near in parts_qkv]
     d_x_send = unproject(d_qkv[:, share_len:]).astype(BF16)
-    d_x_send, share_gate_up[1], share_out, partial_qkv = lax.optimization_barrier(
-        (d_x_send, share_gate_up[1], share_out, partial_qkv)
-    )
-    share_qkv = [reduce_share(partial) for partial in partial_qkv]
+    d_x_send, pair_up, share_gate = tie((d_x_send, pair_up, share_gate))
+    near_qkv, pair_up, pair_out = tie((near_qkv, pair_up, pair_out))
+    share_up = z_far_stage(pair_up)
+    share_out = z_far_stage(pair_out)
     d_x = scatter_rows(unproject(d_qkv[:, :share_len]), d_x_send)
     input_grad = DEEP_ALPHA * d_z_one + d_x
 
@@ -382,22 +456,16 @@
     local = width // lax.axis_size("tp")
     norm_terms = lax.dynamic_slice_in_dim(norm_terms, tp_index * local, local, 1)
 
-    share_gate_up = jnp.stack(share_gate_up, axis=1)
-    share_qkv = jnp.concatenate(share_qkv, axis=1)
-    share_rows = jnp.concatenate([share_down, share_out], axis=0)
-    input_grad, share_gate_up, share_qkv, share_rows = lax.optimization_barrier(
-        (input_grad, share_gate_up, share_qkv, share_rows)
-    )
-    grad_gate_up = gather_shares(share_gate_up)
-    grad_qkv, grad_gate_up = gather_after(share_qkv, grad_gate_up)
-    grad_rows, grad_qkv = gather_after(share_rows, grad_qkv)
+    share_lanes = jnp.concatenate([share_down, share_out], axis=0)
+    share_gate_up = jnp.stack([share_gate, share_up], axis=1)
+    grad_lanes = gather_columns_of(share_lanes)
+    grad_gate_up = gather_rows_of(share_gate_up)
+    share_qkv = [z_far_stage(z_near_stage(near, 0)) for near in near_qkv]
+    share_qkv, grad_lanes = tie((share_qkv, grad_lanes))
+    grad_qkv = gather_rows_of(jnp.stack(share_qkv, axis=1)).astype(F32)
     grad_gate_up = grad_gate_up.astype(F32)
-    grad_qkv = jnp.stack(jnp.split(grad_qkv, 3, axis=1), axis=1).astype(F32)
-    group_size = lax.axis_size(GROUP)
-    grad_rows = grad_rows.reshape(group_size, -1, width).astype(F32)
-    down_rows = local_ff // group_size
-    grad_down = grad_rows[:, :down_rows].reshape(-1, width)
-    grad_out = grad_rows[:, down_rows:].reshape(-1, width)
+    grad_down = widen(grad_lanes[:, :local_ff])
+    grad_out = widen(grad_lanes[:, local_ff:])
     return (
         outputs[None],
         input_grad[None],

time: 1430 us -> 1320 us (0.923)
  waiting for transfers between devices: 878 us -> 639 us
  other arithmetic: 67.4 us -> 119 us
  local copies, waits for them, and re-layouts: 70.1 us -> 104 us
  starting transfers between devices: 19.6 us -> 45.2 us
    reduce_scatter x7 -> x0, waiting for transfers between devices: 364 us -> none  [reduce_share(): lax.psum_scatter(partial.astype(BF16), GROUP, scatter_dimension=0, tiled=...]
    ppermute x0 -> x35, waiting for transfers between devices: none -> 328 us  [the longest x7 127 us: z_far_stage(): got = lax.ppermute(pair[1].astype(BF16), 'obj', Z_FAR)]
    all_gather x3, waiting for transfers between devices: 265 us -> 58.6 us  [the longest x2 58.6 us: gather_rows_of(): return lax.all_gather(share, GROUP, axis=0, tiled=True)]
    unnamed x81 -> x166, local copies, waits for them, and re-layouts: 50.9 us -> 86.1 us
    ppermute x8, waiting for transfers between devices: 55.5 us -> 83.7 us  [all_sum(): lax.ppermute(value, axis, [(i, i ^ step) for i in range(size)])]
    ppermute x0 -> x35, starting transfers between devices: none -> 28 us  [the longest x7 9.92 us: z_near_stage(): got = lax.ppermute(pieces(obj_index ^ 1).astype(BF16), 'obj', Z_NEAR)]
    convert_element_type x1 -> x9, other arithmetic: 8.8 us -> 30.6 us  [the longest x1 14.2 us: body(): grad_qkv = gather_rows_of(jnp.stack(share_qkv, axis=1)).astype(F32)]
    add x0 -> x14, other arithmetic: none -> 21.7 us  [the longest x7 15.8 us: x_stage(): return near + lax.ppermute(far, 'dp', X_SWAP).astype(F32)]
  transfers between devices with their start and end apart: 26 -> 54, of which waited for: 23 -> 30; matrix products, arithmetic and copies ran while one was open for 23% -> 27% of each run, Pallas kernels for 3% -> 3%
where the time goes in v3:
time: 1320 us; the launch traced here: 1310 us
  waiting for transfers between devices  639 us (48%)
  matrix products  307 us (23%)
  other arithmetic  119 us (9%)
  local copies, waits for them, and re-layouts  104 us (8%)
  Pallas kernels  80.6 us (6%)
  starting transfers between devices  45.2 us (3%)
  between operations  17 us (1%)
    ppermute x7, waiting for transfers between devices, z_far_stage(): got = lax.ppermute(pair[1].astype(BF16), 'obj', Z_FAR)  127 us
    ppermute x7, waiting for transfers between devices, z_near_stage(): got = lax.ppermute(pieces(obj_index ^ 1).astype(BF16), 'obj', Z_NEAR)  116 us
    dot_general x28, matrix products, token_sum(): lax.dot_general(left, right, (((0,), (0,)), ((), ())), preferred_element_...  110 us
    ppermute x4, waiting for transfers between devices, gather_rows(): return lax.ppermute(own, 'tp', [(0, 1), (1, 0)])  93.1 us
    unnamed x166, local copies, waits for them, and re-layouts  86.1 us
    ppermute x7, waiting for transfers between devices, x_stage(): return near + lax.ppermute(far, 'dp', X_SWAP).astype(F32)  85.2 us
    ppermute x8, waiting for transfers between devices, all_sum(): lax.ppermute(value, axis, [(i, i ^ step) for i in range(size)])  83.7 us
    ppermute x4, waiting for transfers between devices, scatter_rows(): lax.ppermute(send_part, 'tp', [(0, 1), (1, 0)]).astype(F32)  75.2 us
  transfers between devices with their start and end apart: 54, of which 30 were waited for; matrix products, arithmetic and copies ran while one was open for 27% of the time, Pallas kernels for 3%

profile of v3, /device:TPU:0, one launch (start us, length us, event | category | flops | bytes accessed | tf_op | source)
XLA Modules:
  0.0 1312.0 jit_solution(3540524752183819099)
XLA Ops:
  14.9 11.6 convolution_bitcast_fusion.1.own_ref
  26.4 29.8 %collective-permute-done = bf16[512,2048]{1,0:T(8,128)(2,1)} collective-permute-done((bf16[512,2048]{1,0:T(8,128)(2,1)}, bf16[512,2048]{1,0:T(8,128)(2,1)}, u32[]{:S(2)}, u32[]{:S(2)}) %collective-permute-start) | collective-permute-done | bytes 2097184 | tf_op jit(solution)/shard_map/ppermute | solution.py:185
  66.3 37.8 %attend.1 = (bf16[1024,1024]{1,0:T(8,128)(2,1)}, bf16[3,1024,1024]{2,1,0:T(8,128)(2,1)}) custom-call(s32[2]{0:T(128)} %pad_add_fusion.info_ref, f32[3,512,1024]{2,1,0:T(8,128)} %convolution_bitcast_fusion.1.own_ref, f32[3,512,1024]{2,1,0:T(8,128)} %convolution_bitcast_fusion.other_ref, f32[1024,128]{1,0:T(8,128)} %get-tuple-element.193.cos_ref, ...), custom_call_target="tpu_custom_call" | custom-call | flops 8589934592 | bytes 20971520 | tf_op jit(solution)/shard_map/attend/pallas_call | solution.py:120
  110.9 45.1 %collective-permute-done.1 = bf16[512,2048]{1,0:T(8,128)(2,1)S(1)} collective-permute-done((bf16[512,2048]{1,0:T(8,128)(2,1)S(1)}, bf16[512,2048]{1,0:T(8,128)(2,1)S(1)}, u32[]{:S(2)}, u32[]{:S(2)}) %collective-permute-start.1) | collective-permute-done | bytes 2097184 | tf_op jit(solution)/shard_map/ppermute | solution.py:197
  169.8 36.5 %collective-permute-done.6 = f32[8,128]{1,0:T(8,128)S(1)} collective-permute-done((f32[8,128]{1,0:T(8,128)S(1)}, f32[8,128]{1,0:T(8,128)S(1)}, u32[]{:S(2)}, u32[]{:S(2)}) %collective-permute-start.6) | collective-permute-done | bytes 4128 | tf_op jit(solution)/shard_map/ppermute | solution.py:210
  207.6 21.4 %fusion.4 = f32[512,2,2816]{2,0,1:T(8,128)} fusion(bf16[2048,2,2816]{2,1,0:T(2,128)(2,1)} %param.20, bf16[512,2048]{1,0:T(8,128)(2,1)} %collective-permute-done.2), kind=kOutput, calls=%fused_computation.4 | convolution fusion | flops 11811160064 | bytes 36700160 | tf_op jit(solution)/shard_map/td,dke->tke/dot_general | solution.py:343
  249.6 21.2 %fusion.6 = f32[512,2,2816]{2,0,1:T(8,128)} fusion(bf16[2048,2,2816]{2,1,0:T(2,128)(2,1)} %param.20, bf16[512,2048]{1,0:T(8,128)(2,1)S(1)} %fusion.35), kind=kOutput, calls=%fused_computation.6 | convolution fusion | flops 11811160064 | bytes 36700160 | tf_op jit(solution)/shard_map/td,dke->tke/dot_general | solution.py:343
  279.0 14.8 %collective-permute-done.3 = bf16[512,2048]{1,0:T(8,128)(2,1)} collective-permute-done((bf16[512,2048]{1,0:T(8,128)(2,1)}, bf16[512,2048]{1,0:T(8,128)(2,1)}, u32[]{:S(2)}, u32[]{:S(2)}) %collective-permute-start.3) | collective-permute-done | bytes 2097184 | tf_op jit(solution)/shard_map/ppermute | solution.py:197
  320.3 37.3 %collective-permute-done.7 = bf16[512,2048]{1,0:T(8,128)(2,1)} collective-permute-done((bf16[512,2048]{1,0:T(8,128)(2,1)}, bf16[512,2048]{1,0:T(8,128)(2,1)}, u32[]{:S(2)}, u32[]{:S(2)}) %collective-permute-start.7) | collective-permute-done | bytes 2097184 | tf_op jit(solution)/shard_map/ppermute | solution.py:185
  369.7 15.2 %fusion.46 = (bf16[1,512,2816]{2,1,0:T(8,128)(2,1)}, bf16[1,512,2816]{2,1,0:T(8,128)(2,1)}) fusion(f32[512,2816]{1,0:T(8,128)} %get-tuple-element.73, f32[512,2816]{1,0:T(8,128)} %get-tuple-element.74, bf16[512,2048]{1,0:T(8,128)(2,1)} %collective-permute-done.7, bf16[2816,2048]{1,0:T(8,128)(2,1)} %param.21), kind=kOutput, calls=%fused_computation.125 | convolution fusion | flops 5911347200 | bytes 30932992 | tf_op jit(solution)/shard_map/dot_general | solution.py:368
  390.7 15.2 %fusion.44 = (bf16[1,512,2816]{2,1,0:T(8,128)(2,1)}, bf16[1,512,2816]{2,1,0:T(8,128)(2,1)}) fusion(f32[512,2816]{1,0:T(8,128)} %get-tuple-element.68, f32[512,2816]{1,0:T(8,128)} %get-tuple-element.69, bf16[512,2048]{1,0:T(8,128)(2,1)} %fusion.218, bf16[2816,2048]{1,0:T(8,128)(2,1)} %param.21), kind=kOutput, calls=%fused_computation.123 | convolution fusion | flops 5911347200 | bytes 30932992 | tf_op jit(solution)/shard_map/dot_general | solution.py:368
  424.1 22.3 %bitcast_convert_fusion.1 = bf16[512,2048]{1,0:T(8,128)(2,1)} fusion(bf16[2,512,2816]{2,1,0:T(8,128)(2,1)} %pad_maximum_fusion.1, bf16[2048,2,2816]{2,1,0:T(2,128)(2,1)} %param.20), kind=kOutput, calls=%fused_computation.103 | convolution fusion | flops 11812208640 | bytes 30932992 | tf_op jit(solution)/shard_map/kte,dke->td/dot_general | solution.py:382
  479.0 15.3 %collective-permute-done.10 = bf16[512,2048]{1,0:T(8,128)(2,1)} collective-permute-done((bf16[512,2048]{1,0:T(8,128)(2,1)}, bf16[512,2048]{1,0:T(8,128)(2,1)}, u32[]{:S(2)}, u32[]{:S(2)}) %collective-permute-start.10) | collective-permute-done | bytes 2097184 | tf_op jit(solution)/shard_map/ppermute | solution.py:197
  494.9 22.3 %bitcast_add_fusion.1 = f32[512,2048]{1,0:T(8,128)} fusion(bf16[512,2048]{1,0:T(8,128)(2,1)} %collective-permute-done.10, bf16[2048,2,2816]{2,1,0:T(2,128)(2,1)} %param.20, bf16[1,512,2816]{2,1,0:T(8,128)(2,1)} %get-tuple-element.160, bf16[1,512,2816]{2,1,0:T(8,128)(2,1)} %get-tuple-element.159), kind=kOutput, calls=%fused_computation.104 | convolution fusion | flops 11816140800 | bytes 35127296 | tf_op jit(solution)/shard_map/kte,dke->td/dot_general | solution.py:382
  564.5 26.0 %collective-permute-done.13 = bf16[512,2048]{1,0:T(8,128)(2,1)S(1)} collective-permute-done((bf16[512,2048]{1,0:T(8,128)(2,1)S(1)}, bf16[512,2048]{1,0:T(8,128)(2,1)S(1)}, u32[]{:S(2)}, u32[]{:S(2)}) %collective-permute-start.13) | collective-permute-done | bytes 2097184 | tf_op jit(solution)/shard_map/ppermute | solution.py:185
  603.9 17.8 %collective-permute-done.19 = bf16[512,2816]{1,0:T(8,128)(2,1)} collective-permute-done((bf16[512,2816]{1,0:T(8,128)(2,1)}, bf16[512,2816]{1,0:T(8,128)(2,1)}, u32[]{:S(2)}, u32[]{:S(2)}) %collective-permute-start.19) | collective-permute-done | bytes 2883616 | tf_op jit(solution)/shard_map/ppermute | solution.py:242
  636.1 42.9 %attend_back.1 = bf16[3,1024,1024]{2,1,0:T(8,128)(2,1)} custom-call(s32[2]{0:T(128)} %pad_add_fusion.info_ref, bf16[3,1024,1024]{2,1,0:T(8,128)(2,1)} %get-tuple-element.77.qkv_ref, bf16[1024,1024]{1,0:T(8,128)(2,1)} %pad_maximum_fusion.2.grad_ref, f32[1024,128]{1,0:T(8,128)} %get-tuple-element.193.cos_ref, f32[1024,128]{1,0:T(8,128)} %get-tuple-element.194.sin_ref), custom_call_target="tpu_custom_call" | custom-call | flops 21474836480 | bytes 14680064 | tf_op jit(solution)/shard_map/attend_back/pallas_call | solution.py:154
  685.0 19.3 %collective-permute-done.33 = bf16[1024,512]{1,0:T(8,128)(2,1)} collective-permute-done((bf16[1024,512]{1,0:T(8,128)(2,1)S(1)}, bf16[1024,512]{1,0:T(8,128)(2,1)}, u32[]{:S(2)}, u32[]{:S(2)}) %collective-permute-start.33) | collective-permute-done | bytes 1048608 | tf_op jit(solution)/shard_map/ppermute | solution.py:242
  743.1 38.9 %collective-permute-done.25 = bf16[128,2816]{1,0:T(8,128)(2,1)S(1)} collective-permute-done((bf16[128,2816]{1,0:T(8,128)(2,1)S(1)}, bf16[128,2816]{1,0:T(8,128)(2,1)S(1)}, u32[]{:S(2)}, u32[]{:S(2)}) %collective-permute-start.25) | collective-permute-done | bytes 720928 | tf_op jit(solution)/shard_map/ppermute | solution.py:262
  819.1 20.8 %collective-permute-done.35 = bf16[512,1024]{1,0:T(8,128)(2,1)S(1)} collective-permute-done((bf16[512,1024]{1,0:T(8,128)(2,1)S(1)}, bf16[512,1024]{1,0:T(8,128)(2,1)S(1)}, u32[]{:S(2)}, u32[]{:S(2)}) %collective-permute-start.35) | collective-permute-done | bytes 1048608 | tf_op jit(solution)/shard_map/ppermute | solution.py:242
  841.6 20.4 %collective-permute-done.36 = bf16[512,1024]{1,0:T(8,128)(2,1)S(1)} collective-permute-done((bf16[512,1024]{1,0:T(8,128)(2,1)S(1)}, bf16[512,1024]{1,0:T(8,128)(2,1)S(1)}, u32[]{:S(2)}, u32[]{:S(2)}) %collective-permute-start.36) | collective-permute-done | bytes 1048608 | tf_op jit(solution)/shard_map/ppermute | solution.py:242
  867.0 11.7 collective-permute-done.44
  880.2 64.8 %collective-permute-done.50 = bf16[128,2816]{1,0:T(8,128)(2,1)S(1)} collective-permute-done((bf16[128,2816]{1,0:T(8,128)(2,1)S(1)}, bf16[128,2816]{1,0:T(8,128)(2,1)S(1)}, u32[]{:S(2)}, u32[]{:S(2)}) %collective-permute-start.50) | collective-permute-done | bytes 720928 | tf_op jit(solution)/shard_map/ppermute | solution.py:262
  953.4 41.3 %collective-permute-done.38 = bf16[2,128,1024]{2,1,0:T(8,128)(2,1)S(1)} collective-permute-done((bf16[2,128,1024]{2,1,0:T(8,128)(2,1)S(1)}, bf16[2,128,1024]{2,1,0:T(8,128)(2,1)S(1)}, u32[]{:S(2)}, u32[]{:S(2)}) %collective-permute-start.38) | collective-permute-done | bytes 524320 | tf_op jit(solution)/shard_map/ppermute | solution.py:257
  995.0 32.9 %collective-permute-done.40 = bf16[2,128,1024]{2,1,0:T(8,128)(2,1)S(1)} collective-permute-done((bf16[2,128,1024]{2,1,0:T(8,128)(2,1)S(1)}, bf16[2,128,1024]{2,1,0:T(8,128)(2,1)S(1)}, u32[]{:S(2)}, u32[]{:S(2)}) %collective-permute-start.40) | collective-permute-done | bytes 524320 | tf_op jit(solution)/shard_map/ppermute | solution.py:257
  1028.2 30.4 %collective-permute-done.42 = bf16[2,128,1024]{2,1,0:T(8,128)(2,1)S(1)} collective-permute-done((bf16[2,128,1024]{2,1,0:T(8,128)(2,1)S(1)}, bf16[2,128,1024]{2,1,0:T(8,128)(2,1)S(1)}, u32[]{:S(2)}, u32[]{:S(2)}) %collective-permute-start.42) | collective-permute-done | bytes 524320 | tf_op jit(solution)/shard_map/ppermute | solution.py:257
  1059.1 11.7 collective-permute-done.43
  1089.7 30.4 %collective-permute-done.49 = f32[4,2048]{1,0:T(4,128)S(1)} collective-permute-done((f32[4,2048]{1,0:T(4,128)S(1)}, f32[4,2048]{1,0:T(4,128)S(1)}, u32[]{:S(2)}, u32[]{:S(2)}) %collective-permute-start.49) | collective-permute-done | bytes 32800 | tf_op jit(solution)/shard_map/ppermute | solution.py:210
  1120.8 14.8 %fusion.34 = f32[1,512,2048]{2,1,0:T(8,128)} fusion(bf16[512,2048]{1,0:T(8,128)(2,1)} %collective-permute-done.26, f32[512,2048]{1,0:T(8,128)} %get-tuple-element.137, bf16[2048,3,1024]{2,0,1:T(8,128)(2,1)} %param.16, bf16[3,1024,1024]{2,1,0:T(8,128)(2,1)} %attend_back.1), kind=kOutput, calls=%fused_computation.102 | convolution fusion | flops 6446645248 | bytes 26214400 | tf_op jit(solution)/shard_map/kte,dke->td/dot_general | solution.py:439
  1188.8 45.2 %copy.30 = f32[2048,2,2816]{2,1,0:T(2,128)} copy(bf16[2048,2,2816]{2,0,1:T(8,128)(2,1)} %all-gather.7.cloned.1.call-done) | data formatting | bytes 69206016
  1234.0 57.0 %all-gather.5.cloned.1.call-done = bf16[2048,3,1024]{2,0,1:T(8,128)(2,1)} async-done(((bf16[128,3,1024]{2,0,1:T(8,128)(2,1)}), bf16[2048,3,1024]{2,0,1:T(8,128)(2,1)}) %all-gather.5.cloned.1.call-update) | async-done | bytes 12582928 | tf_op jit(solution)/shard_map/all_gather | solution.py:267
  1291.1 14.2 %convert_element_type.406 = f32[2048,3,1024]{2,0,1:T(8,128)} convert(bf16[2048,3,1024]{2,0,1:T(8,128)(2,1)} %all-gather.5.cloned.1.call-done) | non-fusion elementwise | flops 6291456 | bytes 37748736 | tf_op jit(solution)/shard_map/convert_element_type | solution.py:465
  (393 shorter events, 408.6 us)
Async XLA Ops:
  7.2 1063.7 %all-gather.9.cloned.1.call-start = ((), (), s32[]{:S(2)}) async-start(), calls=%async_computation.2 | async-start | bytes 16711680 | tf_op jit(solution)/shard_map/all_gather | solution.py:271
  7.2 49.0 %collective-permute-start = (bf16[512,2048]{1,0:T(8,128)(2,1)}, bf16[512,2048]{1,0:T(8,128)(2,1)}, u32[]{:S(2)}, u32[]{:S(2)}) collective-permute-start(bf16[512,2048]{1,0:T(8,128)(2,1)} %bitcast.420), channel_id=1, source_target_pairs={{0,1},{1,0},{2,3},{3,2},{4,5},{5,4},{6,7},{7,6},{8,9},{9,8},{10,11... | collective-permute-start | bytes 6291464 | tf_op jit(solution)/shard_map/ppermute | solution.py:185
  109.1 46.9 %collective-permute-start.1 = (bf16[512,2048]{1,0:T(8,128)(2,1)S(1)}, bf16[512,2048]{1,0:T(8,128)(2,1)S(1)}, u32[]{:S(2)}, u32[]{:S(2)}) collective-permute-start(bf16[512,2048]{1,0:T(8,128)(2,1)S(1)} %convolution_convert_fusion.6), channel_id=1, source_target_pairs={{0,1},{1,0},{2,3},{3,2},{4,5},{5,4},{6,7},{7,6},{8,9},{9,8},{10,11... | collective-permute-start | bytes 6291464 | tf_op jit(solution)/shard_map/ppermute | solution.py:197
  160.2 47.4 %collective-permute-start.2 = (bf16[512,2048]{1,0:T(8,128)(2,1)S(1)}, bf16[512,2048]{1,0:T(8,128)(2,1)}, u32[]{:S(2)}, u32[]{:S(2)}) collective-permute-start(bf16[512,2048]{1,0:T(8,128)(2,1)S(1)} %fusion.35), channel_id=1, source_target_pairs={{0,1},{1,0},{2,3},{3,2},{4,5},{5,4},{6,7},{7,6},{8,9},{9,8},{10,11... | collective-permute-start | bytes 6291464 | tf_op jit(solution)/shard_map/ppermute | solution.py:185
  248.4 45.4 %collective-permute-start.3 = (bf16[512,2048]{1,0:T(8,128)(2,1)}, bf16[512,2048]{1,0:T(8,128)(2,1)}, u32[]{:S(2)}, u32[]{:S(2)}) collective-permute-start(bf16[512,2048]{1,0:T(8,128)(2,1)} %convolution_convert_fusion.7), channel_id=1, source_target_pairs={{0,1},{1,0},{2,3},{3,2},{4,5},{5,4},{6,7},{7,6},{8,9},{9,8},{10,11... | collective-permute-start | bytes 6291464 | tf_op jit(solution)/shard_map/ppermute | solution.py:197
  313.0 44.7 %collective-permute-start.7 = (bf16[512,2048]{1,0:T(8,128)(2,1)}, bf16[512,2048]{1,0:T(8,128)(2,1)}, u32[]{:S(2)}, u32[]{:S(2)}) collective-permute-start(bf16[512,2048]{1,0:T(8,128)(2,1)} %fusion.218), channel_id=1, source_target_pairs={{0,1},{1,0},{2,3},{3,2},{4,5},{5,4},{6,7},{7,6},{8,9},{9,8},{10,11... | collective-permute-start | bytes 6291464 | tf_op jit(solution)/shard_map/ppermute | solution.py:185
  369.2 45.3 %collective-permute-start.9 = (bf16[2816,512]{1,0:T(8,128)(2,1)}, bf16[2816,512]{1,0:T(8,128)(2,1)}, u32[]{:S(2)}, u32[]{:S(2)}) collective-permute-start(bf16[2816,512]{1,0:T(8,128)(2,1)} %convolution_convert_fusion.4), channel_id=1, source_target_pairs={{0,2},{2,0},{4,6},{6,4},{1,3},{3,1},{5,7},{7,5},{8,10},{10,8},{12,... | collective-permute-start | bytes 8650760 | tf_op jit(solution)/shard_map/ppermute | solution.py:236
  446.4 47.9 %collective-permute-start.10 = (bf16[512,2048]{1,0:T(8,128)(2,1)}, bf16[512,2048]{1,0:T(8,128)(2,1)}, u32[]{:S(2)}, u32[]{:S(2)}) collective-permute-start(bf16[512,2048]{1,0:T(8,128)(2,1)} %bitcast_convert_fusion.1), channel_id=1, source_target_pairs={{0,1},{1,0},{2,3},{3,2},{4,5},{5,4},{6,7},{7,6},{8,9},{9,8},{10,11... | collective-permute-start | bytes 6291464 | tf_op jit(solution)/shard_map/ppermute | solution.py:197
  459.9 57.2 %collective-permute-start.11 = (bf16[512,2816]{1,0:T(8,128)(2,1)}, bf16[512,2816]{1,0:T(8,128)(2,1)}, u32[]{:S(2)}, u32[]{:S(2)}) collective-permute-start(bf16[512,2816]{1,0:T(8,128)(2,1)} %convolution_convert_fusion.3), channel_id=1, source_target_pairs={{0,2},{2,0},{4,6},{6,4},{1,3},{3,1},{5,7},{7,5},{8,10},{10,8},{12,... | collective-permute-start | bytes 8650760 | tf_op jit(solution)/shard_map/ppermute | solution.py:235
  465.9 60.0 %collective-permute-start.12 = (bf16[512,2816]{1,0:T(8,128)(2,1)}, bf16[512,2816]{1,0:T(8,128)(2,1)}, u32[]{:S(2)}, u32[]{:S(2)}) collective-permute-start(bf16[512,2816]{1,0:T(8,128)(2,1)} %convolution_convert_fusion.2), channel_id=1, source_target_pairs={{0,2},{2,0},{4,6},{6,4},{1,3},{3,1},{5,7},{7,5},{8,10},{10,8},{12,... | collective-permute-start | bytes 8650760 | tf_op jit(solution)/shard_map/ppermute | solution.py:236
  472.3 73.8 %collective-permute-start.14 = (bf16[512,2816]{1,0:T(8,128)(2,1)}, bf16[512,2816]{1,0:T(8,128)(2,1)}, u32[]{:S(2)}, u32[]{:S(2)}) collective-permute-start(bf16[512,2816]{1,0:T(8,128)(2,1)} %convolution_convert_fusion.1), channel_id=1, source_target_pairs={{0,2},{2,0},{4,6},{6,4},{1,3},{3,1},{5,7},{7,5},{8,10},{10,8},{12,... | collective-permute-start | bytes 8650760 | tf_op jit(solution)/shard_map/ppermute | solution.py:235
  478.5 74.1 %collective-permute-start.15 = (bf16[512,2816]{1,0:T(8,128)(2,1)}, bf16[512,2816]{1,0:T(8,128)(2,1)}, u32[]{:S(2)}, u32[]{:S(2)}) collective-permute-start(bf16[512,2816]{1,0:T(8,128)(2,1)} %convolution_convert_fusion), channel_id=1, source_target_pairs={{0,2},{2,0},{4,6},{6,4},{1,3},{3,1},{5,7},{7,5},{8,10},{10,8},{12,... | collective-permute-start | bytes 8650760 | tf_op jit(solution)/shard_map/ppermute | solution.py:236
  494.3 65.7 %collective-permute-start.16 = (bf16[2816,512]{1,0:T(8,128)(2,1)}, bf16[2816,512]{1,0:T(8,128)(2,1)}, u32[]{:S(2)}, u32[]{:S(2)}) collective-permute-start(bf16[2816,512]{1,0:T(8,128)(2,1)} %add_convert_fusion.2), channel_id=1, source_target_pairs={{0,4},{4,0},{2,6},{6,2},{1,5},{5,1},{3,7},{7,3},{8,12},{12,8},{10,... | collective-permute-start | bytes 8650760 | tf_op jit(solution)/shard_map/ppermute | solution.py:242
  544.1 46.4 %collective-permute-start.13 = (bf16[512,2048]{1,0:T(8,128)(2,1)S(1)}, bf16[512,2048]{1,0:T(8,128)(2,1)S(1)}, u32[]{:S(2)}, u32[]{:S(2)}) collective-permute-start(bf16[512,2048]{1,0:T(8,128)(2,1)S(1)} %get-tuple-element.81), channel_id=1, source_target_pairs={{0,1},{1,0},{2,3},{3,2},{4,5},{5,4},{6,7},{7,6},{8,9},{9,8},{10,11... | collective-permute-start | bytes 6291464 | tf_op jit(solution)/shard_map/ppermute | solution.py:185
  545.6 76.2 %collective-permute-start.19 = (bf16[512,2816]{1,0:T(8,128)(2,1)}, bf16[512,2816]{1,0:T(8,128)(2,1)}, u32[]{:S(2)}, u32[]{:S(2)}) collective-permute-start(bf16[512,2816]{1,0:T(8,128)(2,1)} %add_convert_fusion.1), channel_id=1, source_target_pairs={{0,4},{4,0},{2,6},{6,2},{1,5},{5,1},{3,7},{7,3},{8,12},{12,8},{10,... | collective-permute-start | bytes 8650760 | tf_op jit(solution)/shard_map/ppermute | solution.py:242
  596.7 109.0 %collective-permute-start.21 = (bf16[512,2816]{1,0:T(8,128)(2,1)}, bf16[512,2816]{1,0:T(8,128)(2,1)}, u32[]{:S(2)}, u32[]{:S(2)}) collective-permute-start(bf16[512,2816]{1,0:T(8,128)(2,1)} %add_convert_fusion), channel_id=1, source_target_pairs={{0,4},{4,0},{2,6},{6,2},{1,5},{5,1},{3,7},{7,3},{8,12},{12,8},{10,... | collective-permute-start | bytes 8650760 | tf_op jit(solution)/shard_map/ppermute | solution.py:242
  630.4 77.9 %collective-permute-start.22 = (bf16[2,128,2816]{2,1,0:T(8,128)(2,1)}, bf16[2,128,2816]{2,1,0:T(8,128)(2,1)}, u32[]{:S(2)}, u32[]{:S(2)}) collective-permute-start(bf16[2,128,2816]{2,1,0:T(8,128)(2,1)} %pad_maximum_fusion.4), channel_id=1, source_target_pairs={{0,8},{8,0},{16,24},{24,16},{1,9},{9,1},{17,25},{25,17},{2,10},{10... | collective-permute-start | bytes 4325384 | tf_op jit(solution)/shard_map/ppermute | solution.py:257
  632.9 49.8 %collective-permute-start.23 = (bf16[2816,128]{1,0:T(8,128)(2,1)}, bf16[2816,128]{1,0:T(8,128)(2,1)}, u32[]{:S(2)}, u32[]{:S(2)}) collective-permute-start(bf16[2816,128]{1,0:T(8,128)(2,1)} %fusion.164), channel_id=1, source_target_pairs={{0,16},{16,0},{8,24},{24,8},{1,17},{17,1},{9,25},{25,9},{2,18},{18... | collective-permute-start | bytes 2162696 | tf_op jit(solution)/shard_map/ppermute | solution.py:262
  635.5 68.7 %collective-permute-start.33 = (bf16[1024,512]{1,0:T(8,128)(2,1)S(1)}, bf16[1024,512]{1,0:T(8,128)(2,1)}, u32[]{:S(2)}, u32[]{:S(2)}) collective-permute-start(bf16[1024,512]{1,0:T(8,128)(2,1)S(1)} %add_convert_fusion.7), channel_id=1, source_target_pairs={{0,4},{4,0},{2,6},{6,2},{1,5},{5,1},{3,7},{7,3},{8,12},{12,8},{10,... | collective-permute-start | bytes 3145736 | tf_op jit(solution)/shard_map/ppermute | solution.py:242
  736.5 62.5 %collective-permute-start.24 = (bf16[2,128,2816]{2,1,0:T(8,128)(2,1)S(1)}, bf16[2,128,2816]{2,1,0:T(8,128)(2,1)S(1)}, u32[]{:S(2)}, u32[]{:S(2)}) collective-permute-start(bf16[2,128,2816]{2,1,0:T(8,128)(2,1)S(1)} %pad_maximum_fusion.5), channel_id=1, source_target_pairs={{0,8},{8,0},{16,24},{24,16},{1,9},{9,1},{17,25},{25,17},{2,10},{10... | collective-permute-start | bytes 4325384 | tf_op jit(solution)/shard_map/ppermute | solution.py:257
  737.4 44.6 %collective-permute-start.25 = (bf16[128,2816]{1,0:T(8,128)(2,1)S(1)}, bf16[128,2816]{1,0:T(8,128)(2,1)S(1)}, u32[]{:S(2)}, u32[]{:S(2)}) collective-permute-start(bf16[128,2816]{1,0:T(8,128)(2,1)S(1)} %fusion.165), channel_id=1, source_target_pairs={{0,16},{16,0},{8,24},{24,8},{1,17},{17,1},{9,25},{25,9},{2,18},{18... | collective-permute-start | bytes 2162696 | tf_op jit(solution)/shard_map/ppermute | solution.py:262
  740.0 46.2 %collective-permute-start.28 = (bf16[512,1024]{1,0:T(8,128)(2,1)S(1)}, bf16[512,1024]{1,0:T(8,128)(2,1)S(1)}, u32[]{:S(2)}, u32[]{:S(2)}) collective-permute-start(bf16[512,1024]{1,0:T(8,128)(2,1)S(1)} %fusion.92), channel_id=1, source_target_pairs={{0,2},{2,0},{4,6},{6,4},{1,3},{3,1},{5,7},{7,5},{8,10},{10,8},{12,... | collective-permute-start | bytes 3145736 | tf_op jit(solution)/shard_map/ppermute | solution.py:236
  792.9 47.0 %collective-permute-start.35 = (bf16[512,1024]{1,0:T(8,128)(2,1)S(1)}, bf16[512,1024]{1,0:T(8,128)(2,1)S(1)}, u32[]{:S(2)}, u32[]{:S(2)}) collective-permute-start(bf16[512,1024]{1,0:T(8,128)(2,1)S(1)} %add_convert_fusion.5), channel_id=1, source_target_pairs={{0,4},{4,0},{2,6},{6,2},{1,5},{5,1},{3,7},{7,3},{8,12},{12,8},{10,... | collective-permute-start | bytes 3145736 | tf_op jit(solution)/shard_map/ppermute | solution.py:242
  793.5 68.5 %collective-permute-start.36 = (bf16[512,1024]{1,0:T(8,128)(2,1)S(1)}, bf16[512,1024]{1,0:T(8,128)(2,1)S(1)}, u32[]{:S(2)}, u32[]{:S(2)}) collective-permute-start(bf16[512,1024]{1,0:T(8,128)(2,1)S(1)} %add_convert_fusion.4), channel_id=1, source_target_pairs={{0,4},{4,0},{2,6},{6,2},{1,5},{5,1},{3,7},{7,3},{8,12},{12,8},{10,... | collective-permute-start | bytes 3145736 | tf_op jit(solution)/shard_map/ppermute | solution.py:242
  879.9 308.9 %all-gather.7.cloned.1.call-start = ((), (), s32[]{:S(2)}) async-start(), calls=%async_computation.1 | async-start | bytes 24510464 | tf_op jit(solution)/shard_map/all_gather | solution.py:267
  880.1 64.9 %collective-permute-start.50 = (bf16[128,2816]{1,0:T(8,128)(2,1)S(1)}, bf16[128,2816]{1,0:T(8,128)(2,1)S(1)}, u32[]{:S(2)}, u32[]{:S(2)}) collective-permute-start(bf16[128,2816]{1,0:T(8,128)(2,1)S(1)} %fusion.166), channel_id=1, source_target_pairs={{0,16},{16,0},{8,24},{24,8},{1,17},{17,1},{9,25},{25,9},{2,18},{18... | collective-permute-start | bytes 2162696 | tf_op jit(solution)/shard_map/ppermute | solution.py:262
  946.4 344.7 %all-gather.5.cloned.1.call-start = ((), (), s32[]{:S(2)}) async-start(), calls=%async_computation | async-start | bytes 13369344 | tf_op jit(solution)/shard_map/all_gather | solution.py:267
  947.9 46.8 %collective-permute-start.38 = (bf16[2,128,1024]{2,1,0:T(8,128)(2,1)S(1)}, bf16[2,128,1024]{2,1,0:T(8,128)(2,1)S(1)}, u32[]{:S(2)}, u32[]{:S(2)}) collective-permute-start(bf16[2,128,1024]{2,1,0:T(8,128)(2,1)S(1)} %pad_maximum_fusion.12), channel_id=1, source_target_pairs={{0,8},{8,0},{16,24},{24,16},{1,9},{9,1},{17,25},{25,17},{2,10},{10... | collective-permute-start | bytes 1572872 | tf_op jit(solution)/shard_map/ppermute | solution.py:257
  949.3 78.6 %collective-permute-start.40 = (bf16[2,128,1024]{2,1,0:T(8,128)(2,1)S(1)}, bf16[2,128,1024]{2,1,0:T(8,128)(2,1)S(1)}, u32[]{:S(2)}, u32[]{:S(2)}) collective-permute-start(bf16[2,128,1024]{2,1,0:T(8,128)(2,1)S(1)} %pad_maximum_fusion.13), channel_id=1, source_target_pairs={{0,8},{8,0},{16,24},{24,16},{1,9},{9,1},{17,25},{25,17},{2,10},{10... | collective-permute-start | bytes 1572872 | tf_op jit(solution)/shard_map/ppermute | solution.py:257
  953.1 105.5 %collective-permute-start.42 = (bf16[2,128,1024]{2,1,0:T(8,128)(2,1)S(1)}, bf16[2,128,1024]{2,1,0:T(8,128)(2,1)S(1)}, u32[]{:S(2)}, u32[]{:S(2)}) collective-permute-start(bf16[2,128,1024]{2,1,0:T(8,128)(2,1)S(1)} %pad_maximum_fusion.14), channel_id=1, source_target_pairs={{0,8},{8,0},{16,24},{24,16},{1,9},{9,1},{17,25},{25,17},{2,10},{10... | collective-permute-start | bytes 1572872 | tf_op jit(solution)/shard_map/ppermute | solution.py:257
  995.0 64.0 %collective-permute-start.39 = (bf16[128,1024]{1,0:T(8,128)(2,1)S(1)}, bf16[128,1024]{1,0:T(8,128)(2,1)S(1)}, u32[]{:S(2)}, u32[]{:S(2)}) collective-permute-start(bf16[128,1024]{1,0:T(8,128)(2,1)S(1)} %fusion.182), channel_id=1, source_target_pairs={{0,16},{16,0},{8,24},{24,8},{1,17},{17,1},{9,25},{25,9},{2,18},{18... | collective-permute-start | bytes 786440 | tf_op jit(solution)/shard_map/ppermute | solution.py:262
  1072.0 48.9 %collective-permute-start.26 = (bf16[512,2048]{1,0:T(8,128)(2,1)S(1)}, bf16[512,2048]{1,0:T(8,128)(2,1)}, u32[]{:S(2)}, u32[]{:S(2)}) collective-permute-start(bf16[512,2048]{1,0:T(8,128)(2,1)S(1)} %copy-done.56), channel_id=1, source_target_pairs={{0,1},{1,0},{2,3},{3,2},{4,5},{5,4},{6,7},{7,6},{8,9},{9,8},{10,11... | collective-permute-start | bytes 6291464 | tf_op jit(solution)/shard_map/ppermute | solution.py:197
  (89 other events, 1785.3 us)
Sparse Core Ops, SparseCore 0:
  880.0 180.2 all-gather.8
  1061.9 126.8 all-gather.6
  1191.1 99.9 all-gather.4

commit v4 on v3

--- a/solution.py
+++ b/solution.py
@@ -393,22 +393,26 @@
         return token_sum(columns(h_rows, q), d_gu[1])
 
     d_h = scatter_rows(feed_rows(d_gu_own), d_h_send)
-    d_h, (far_gate, near_gate) = tie((d_h, core_stage(make_gate, give_quarters(make_gate))))
+    d_h, (far_gate, near_gate), near_down = tie(
+        (d_h, core_stage(make_gate, give_quarters(make_gate)), near_down)
+    )
+    pair_down = z_near_stage(near_down, 1)
     near_gate = x_stage(far_gate, near_gate)
     d_z_one, d_gain_one, d_bias_one = norm_back(
         DEEP_ALPHA * d_z_two + d_h, zhat_one, scale_one, gain_one
     )
     d_attn_own = d_z_one.astype(BF16)
     d_attn_other = gather_rows(d_attn_own)
-    d_attn_other, (far_up, near_up), near_down = tie(
-        (d_attn_other, core_stage(make_up, give_quarters(make_up)), near_down)
+    d_attn_other, (far_up, near_up), near_gate, pair_down = tie(
+        (d_attn_other, core_stage(make_up, give_quarters(make_up)), near_gate, pair_down)
     )
     near_up = x_stage(far_up, near_up)
-    pair_down = z_near_stage(near_down, 1)
+    pair_gate = z_near_stage(near_gate, 0)
+    share_down = z_far_stage(pair_down)
     d_attn = jnp.concatenate([d_attn_own, d_attn_other], axis=0)
 
     def make_out(q):
-        return token_sum(mixed, columns(d_attn, q))
+        return token_sum(columns(d_attn, q), mixed)
 
     gives_out, d_attn_own, d_attn_other = tie((give_quarters(make_out), d_attn_own, d_attn_other))
 
@@ -418,14 +422,13 @@
         ).astype(BF16)
 
     d_mixed = jnp.concatenate([unmix(d_attn_own), unmix(d_attn_other)], axis=0)
-    d_mixed, (far_out, near_out), near_gate, pair_down = tie(
-        (d_mixed, core_stage(make_out, gives_out), near_gate, pair_down)
+    d_mixed, (far_out, near_out), share_down = tie(
+        (d_mixed, core_stage(make_out, gives_out), share_down)
     )
     near_out = x_stage(far_out, near_out)
-    pair_gate = z_near_stage(near_gate, 0)
-    share_down = z_far_stage(pair_down)
+    all_down = gather_columns_of(share_down)
     d_qkv = attend_back(info, qkv, d_mixed, cos_vals, sin_vals)
-    d_qkv, near_up, pair_gate, share_down = tie((d_qkv, near_up, pair_gate, share_down))
+    d_qkv, near_up, pair_gate = tie((d_qkv, near_up, pair_gate))
     pair_up = z_near_stage(near_up, 0)
     share_gate = z_far_stage(pair_gate)
     x_rows = jnp.concatenate([x_own, x_other], axis=0)
@@ -440,13 +443,14 @@
 
     parts_qkv = [core_stage(make_qkv(k), gives_qkv[k]) for k in range(3)]
     parts_qkv, near_out = tie((parts_qkv, near_out))
-    pair_out = z_near_stage(near_out, 1)
+    pair_out = z_near_stage(near_out, 0)
     near_qkv = [x_stage(far, near) for far, near in parts_qkv]
     d_x_send = unproject(d_qkv[:, share_len:]).astype(BF16)
     d_x_send, pair_up, share_gate = tie((d_x_send, pair_up, share_gate))
-    near_qkv, pair_up, pair_out = tie((near_qkv, pair_up, pair_out))
     share_up = z_far_stage(pair_up)
     share_out = z_far_stage(pair_out)
+    all_gate = gather_rows_of(share_gate)
+    near_qkv, share_up, share_out, all_down = tie((near_qkv, share_up, share_out, all_down))
     d_x = scatter_rows(unproject(d_qkv[:, :share_len]), d_x_send)
     input_grad = DEEP_ALPHA * d_z_one + d_x
 
@@ -456,16 +460,14 @@
     local = width // lax.axis_size("tp")
     norm_terms = lax.dynamic_slice_in_dim(norm_terms, tp_index * local, local, 1)
 
-    share_lanes = jnp.concatenate([share_down, share_out], axis=0)
-    share_gate_up = jnp.stack([share_gate, share_up], axis=1)
-    grad_lanes = gather_columns_of(share_lanes)
-    grad_gate_up = gather_rows_of(share_gate_up)
+    all_up_out = gather_rows_of(jnp.concatenate([share_up, share_out], axis=1))
     share_qkv = [z_far_stage(z_near_stage(near, 0)) for near in near_qkv]
-    share_qkv, grad_lanes = tie((share_qkv, grad_lanes))
+    share_qkv, all_gate, all_up_out = tie((share_qkv, all_gate, all_up_out))
     grad_qkv = gather_rows_of(jnp.stack(share_qkv, axis=1)).astype(F32)
-    grad_gate_up = grad_gate_up.astype(F32)
-    grad_down = widen(grad_lanes[:, :local_ff])
-    grad_out = widen(grad_lanes[:, local_ff:])
+    all_up, all_out = all_up_out[:, :local_ff], all_up_out[:, local_ff:]
+    grad_gate_up = tie(jnp.stack([all_gate, all_up], axis=1)).astype(F32)
+    grad_down = widen(all_down)
+    grad_out = all_out.T.astype(F32)
     return (
         outputs[None],
         input_grad[None],

time: 1320 us -> 1460 us (1.11)
  local copies, waits for them, and re-layouts: 104 us -> 223 us
    unnamed x166 -> x142, local copies, waits for them, and re-layouts: 86.1 us -> 200 us
    ppermute x7, waiting for transfers between devices: 127 us -> 171 us  [z_far_stage(): got = lax.ppermute(pair[1].astype(BF16), 'obj', Z_FAR)]
    ppermute x4, waiting for transfers between devices: 93.1 us -> 70.6 us  [gather_rows(): return lax.ppermute(own, 'tp', [(0, 1), (1, 0)])]
    all_gather x2 -> x3, waiting for transfers between devices: 58.6 us -> 37.4 us  [gather_rows_of(): return lax.all_gather(share, GROUP, axis=0, tiled=True)]
  transfers between devices with their start and end apart: 54 -> 55, of which waited for: 30 -> 30; matrix products, arithmetic and copies ran while one was open for 27% -> 36% of each run, Pallas kernels for 3% -> 3%
where the time goes in v4:
time: 1460 us; the launch traced here: 1450 us
  waiting for transfers between devices  645 us (44%)
  matrix products  309 us (21%)
  local copies, waits for them, and re-layouts  223 us (15%)
  other arithmetic  133 us (9%)
  Pallas kernels  70.5 us (5%)
  starting transfers between devices  49.7 us (3%)
  between operations  16.7 us (1%)
    unnamed x142, local copies, waits for them, and re-layouts  200 us
    ppermute x7, waiting for transfers between devices, z_far_stage(): got = lax.ppermute(pair[1].astype(BF16), 'obj', Z_FAR)  171 us
    ppermute x7, waiting for transfers between devices, z_near_stage(): got = lax.ppermute(pieces(obj_index ^ 1).astype(BF16), 'obj', Z_NEAR)  125 us
    dot_general x28, matrix products, token_sum(): lax.dot_general(left, right, (((0,), (0,)), ((), ())), preferred_element_...  113 us
    ppermute x8, waiting for transfers between devices, all_sum(): lax.ppermute(value, axis, [(i, i ^ step) for i in range(size)])  84 us
    ppermute x7, waiting for transfers between devices, x_stage(): return near + lax.ppermute(far, 'dp', X_SWAP).astype(F32)  81.6 us
    ppermute x4, waiting for transfers between devices, scatter_rows(): lax.ppermute(send_part, 'tp', [(0, 1), (1, 0)]).astype(F32)  74.4 us
    ppermute x4, waiting for transfers between devices, gather_rows(): return lax.ppermute(own, 'tp', [(0, 1), (1, 0)])  70.6 us
  transfers between devices with their start and end apart: 55, of which 30 were waited for; matrix products, arithmetic and copies ran while one was open for 36% of the time, Pallas kernels for 3%

profile of v4, /device:TPU:0, one launch (start us, length us, event | category | flops | bytes accessed | tf_op | source)
XLA Modules:
  0.0 1447.3 jit_solution(7768965493298672211)
XLA Ops:
  26.4 29.8 %collective-permute-done = bf16[512,2048]{1,0:T(8,128)(2,1)} collective-permute-done((bf16[512,2048]{1,0:T(8,128)(2,1)}, bf16[512,2048]{1,0:T(8,128)(2,1)}, u32[]{:S(2)}, u32[]{:S(2)}) %collective-permute-start) | collective-permute-done | bytes 2097184 | tf_op jit(solution)/shard_map/ppermute | solution.py:185
  66.3 27.5 %attend.1 = (bf16[1024,1024]{1,0:T(8,128)(2,1)}, bf16[3,1024,1024]{2,1,0:T(8,128)(2,1)}) custom-call(s32[2]{0:T(128)} %pad_add_fusion.info_ref, f32[3,512,1024]{2,1,0:T(8,128)} %convolution_bitcast_fusion.1.own_ref, f32[3,512,1024]{2,1,0:T(8,128)} %convolution_bitcast_fusion.other_ref, f32[1024,128]{1,0:T(8,128)} %get-tuple-element.197.cos_ref, ...), custom_call_target="tpu_custom_call" | custom-call | flops 8589934592 | bytes 20971520 | tf_op jit(solution)/shard_map/attend/pallas_call | solution.py:120
  100.6 45.1 %collective-permute-done.1 = bf16[512,2048]{1,0:T(8,128)(2,1)S(1)} collective-permute-done((bf16[512,2048]{1,0:T(8,128)(2,1)S(1)}, bf16[512,2048]{1,0:T(8,128)(2,1)S(1)}, u32[]{:S(2)}, u32[]{:S(2)}) %collective-permute-start.1) | collective-permute-done | bytes 2097184 | tf_op jit(solution)/shard_map/ppermute | solution.py:197
  159.6 36.5 %collective-permute-done.6 = f32[8,128]{1,0:T(8,128)S(1)} collective-permute-done((f32[8,128]{1,0:T(8,128)S(1)}, f32[8,128]{1,0:T(8,128)S(1)}, u32[]{:S(2)}, u32[]{:S(2)}) %collective-permute-start.6) | collective-permute-done | bytes 4128 | tf_op jit(solution)/shard_map/ppermute | solution.py:210
  197.3 21.4 %fusion.4 = f32[512,2,2816]{2,0,1:T(8,128)} fusion(bf16[2048,2,2816]{2,1,0:T(2,128)(2,1)} %param.20, bf16[512,2048]{1,0:T(8,128)(2,1)} %collective-permute-done.2), kind=kOutput, calls=%fused_computation.5 | convolution fusion | flops 11811160064 | bytes 36700160 | tf_op jit(solution)/shard_map/td,dke->tke/dot_general | solution.py:343
  239.4 20.9 %fusion.6 = f32[512,2,2816]{2,0,1:T(8,128)} fusion(bf16[2048,2,2816]{2,1,0:T(2,128)(2,1)} %param.20, bf16[512,2048]{1,0:T(8,128)(2,1)S(1)} %fusion.35), kind=kOutput, calls=%fused_computation.7 | convolution fusion | flops 11811160064 | bytes 36700160 | tf_op jit(solution)/shard_map/td,dke->tke/dot_general | solution.py:343
  268.6 15.0 %collective-permute-done.3 = bf16[512,2048]{1,0:T(8,128)(2,1)} collective-permute-done((bf16[512,2048]{1,0:T(8,128)(2,1)}, bf16[512,2048]{1,0:T(8,128)(2,1)}, u32[]{:S(2)}, u32[]{:S(2)}) %collective-permute-start.3) | collective-permute-done | bytes 2097184 | tf_op jit(solution)/shard_map/ppermute | solution.py:197
  306.8 40.8 %collective-permute-done.7 = bf16[512,2048]{1,0:T(8,128)(2,1)} collective-permute-done((bf16[512,2048]{1,0:T(8,128)(2,1)}, bf16[512,2048]{1,0:T(8,128)(2,1)}, u32[]{:S(2)}, u32[]{:S(2)}) %collective-permute-start.7) | collective-permute-done | bytes 2097184 | tf_op jit(solution)/shard_map/ppermute | solution.py:185
  359.6 15.1 %fusion.46 = (bf16[1,512,2816]{2,1,0:T(8,128)(2,1)}, bf16[1,512,2816]{2,1,0:T(8,128)(2,1)}) fusion(f32[512,2816]{1,0:T(8,128)} %get-tuple-element.75, f32[512,2816]{1,0:T(8,128)} %get-tuple-element.76, bf16[512,2048]{1,0:T(8,128)(2,1)} %collective-permute-done.7, bf16[2816,2048]{1,0:T(8,128)(2,1)} %param.21), kind=kOutput, calls=%fused_computation.128 | convolution fusion | flops 5911347200 | bytes 30932992 | tf_op jit(solution)/shard_map/dot_general | solution.py:368
  380.5 15.1 %fusion.44 = (bf16[1,512,2816]{2,1,0:T(8,128)(2,1)}, bf16[1,512,2816]{2,1,0:T(8,128)(2,1)}) fusion(f32[512,2816]{1,0:T(8,128)} %get-tuple-element.70, f32[512,2816]{1,0:T(8,128)} %get-tuple-element.71, bf16[512,2048]{1,0:T(8,128)(2,1)} %fusion.218, bf16[2816,2048]{1,0:T(8,128)(2,1)} %param.21), kind=kOutput, calls=%fused_computation.126 | convolution fusion | flops 5911347200 | bytes 30932992 | tf_op jit(solution)/shard_map/dot_general | solution.py:368
  413.8 22.1 %bitcast_convert_fusion.1 = bf16[512,2048]{1,0:T(8,128)(2,1)} fusion(bf16[2,512,2816]{2,1,0:T(8,128)(2,1)} %pad_maximum_fusion.2, bf16[2048,2,2816]{2,1,0:T(2,128)(2,1)} %param.20), kind=kOutput, calls=%fused_computation.106 | convolution fusion | flops 11812208640 | bytes 30932992 | tf_op jit(solution)/shard_map/kte,dke->td/dot_general | solution.py:382
  469.4 14.3 collective-permute-done.10
  483.8 22.4 %bitcast_add_fusion.1 = f32[512,2048]{1,0:T(8,128)} fusion(bf16[512,2048]{1,0:T(8,128)(2,1)} %collective-permute-done.10, bf16[2048,2,2816]{2,1,0:T(2,128)(2,1)} %param.20, bf16[1,512,2816]{2,1,0:T(8,128)(2,1)} %get-tuple-element.164, bf16[1,512,2816]{2,1,0:T(8,128)(2,1)} %get-tuple-element.163), kind=kOutput, calls=%fused_computation.107 | convolution fusion | flops 11816140800 | bytes 35127296 | tf_op jit(solution)/shard_map/kte,dke->td/dot_general | solution.py:382
  562.3 16.2 %collective-permute-done.18 = bf16[2,2816,128]{2,1,0:T(8,128)(2,1)S(1)} collective-permute-done((bf16[2,2816,128]{2,1,0:T(8,128)(2,1)S(1)}, bf16[2,2816,128]{2,1,0:T(8,128)(2,1)S(1)}, u32[]{:S(2)}, u32[]{:S(2)}) %collective-permute-start.18) | collective-permute-done | bytes 1441824 | tf_op jit(solution)/shard_map/ppermute | solution.py:257
  578.8 27.4 %collective-permute-done.17 = bf16[512,2816]{1,0:T(8,128)(2,1)} collective-permute-done((bf16[512,2816]{1,0:T(8,128)(2,1)}, bf16[512,2816]{1,0:T(8,128)(2,1)}, u32[]{:S(2)}, u32[]{:S(2)}) %collective-permute-start.17) | collective-permute-done | bytes 2883616 | tf_op jit(solution)/shard_map/ppermute | solution.py:242
  625.1 28.1 %collective-permute-done.21 = bf16[2816,128]{1,0:T(8,128)(2,1)S(1)} collective-permute-done((bf16[2816,128]{1,0:T(8,128)(2,1)S(1)}, bf16[2816,128]{1,0:T(8,128)(2,1)S(1)}, u32[]{:S(2)}, u32[]{:S(2)}) %collective-permute-start.21) | collective-permute-done | bytes 720928 | tf_op jit(solution)/shard_map/ppermute | solution.py:262
  669.9 43.0 %attend_back.1 = bf16[3,1024,1024]{2,1,0:T(8,128)(2,1)} custom-call(s32[2]{0:T(128)} %pad_add_fusion.info_ref, bf16[3,1024,1024]{2,1,0:T(8,128)(2,1)} %get-tuple-element.81.qkv_ref, bf16[1024,1024]{1,0:T(8,128)(2,1)} %pad_maximum_fusion.3.grad_ref, f32[1024,128]{1,0:T(8,128)} %get-tuple-element.197.cos_ref, f32[1024,128]{1,0:T(8,128)} %get-tuple-element.198.sin_ref), custom_call_target="tpu_custom_call" | custom-call | flops 21474836480 | bytes 14680064 | tf_op jit(solution)/shard_map/attend_back/pallas_call | solution.py:154
  727.8 14.6 %collective-permute-done.22 = bf16[512,2816]{1,0:T(8,128)(2,1)} collective-permute-done((bf16[512,2816]{1,0:T(8,128)(2,1)}, bf16[512,2816]{1,0:T(8,128)(2,1)}, u32[]{:S(2)}, u32[]{:S(2)}) %collective-permute-start.22) | collective-permute-done | bytes 2883616 | tf_op jit(solution)/shard_map/ppermute | solution.py:242
  763.7 55.2 %collective-permute-done.25 = bf16[128,2816]{1,0:T(8,128)(2,1)} collective-permute-done((bf16[128,2816]{1,0:T(8,128)(2,1)S(1)}, bf16[128,2816]{1,0:T(8,128)(2,1)}, u32[]{:S(2)}, u32[]{:S(2)}) %collective-permute-start.25) | collective-permute-done | bytes 720928 | tf_op jit(solution)/shard_map/ppermute | solution.py:262
  829.5 27.7 %collective-permute-done.33 = bf16[512,1024]{1,0:T(8,128)(2,1)S(1)} collective-permute-done((bf16[512,1024]{1,0:T(8,128)(2,1)}, bf16[512,1024]{1,0:T(8,128)(2,1)S(1)}, u32[]{:S(2)}, u32[]{:S(2)}) %collective-permute-start.33) | collective-permute-done | bytes 1048608 | tf_op jit(solution)/shard_map/ppermute | solution.py:242
  885.0 26.0 %collective-permute-done.38 = bf16[2,128,1024]{2,1,0:T(8,128)(2,1)S(1)} collective-permute-done((bf16[2,128,1024]{2,1,0:T(8,128)(2,1)S(1)}, bf16[2,128,1024]{2,1,0:T(8,128)(2,1)S(1)}, u32[]{:S(2)}, u32[]{:S(2)}) %collective-permute-start.38) | collective-permute-done | bytes 524320 | tf_op jit(solution)/shard_map/ppermute | solution.py:257
  914.3 41.3 %collective-permute-done.39 = bf16[128,1024]{1,0:T(8,128)(2,1)S(1)} collective-permute-done((bf16[128,1024]{1,0:T(8,128)(2,1)S(1)}, bf16[128,1024]{1,0:T(8,128)(2,1)S(1)}, u32[]{:S(2)}, u32[]{:S(2)}) %collective-permute-start.39) | collective-permute-done | bytes 262176 | tf_op jit(solution)/shard_map/ppermute | solution.py:262
  984.8 26.9 %collective-permute-done.40 = bf16[2,128,1024]{2,1,0:T(8,128)(2,1)S(1)} collective-permute-done((bf16[2,128,1024]{2,1,0:T(8,128)(2,1)S(1)}, bf16[2,128,1024]{2,1,0:T(8,128)(2,1)S(1)}, u32[]{:S(2)}, u32[]{:S(2)}) %collective-permute-start.40) | collective-permute-done | bytes 524320 | tf_op jit(solution)/shard_map/ppermute | solution.py:257
  1012.0 30.8 %collective-permute-done.42 = bf16[2,128,1024]{2,1,0:T(8,128)(2,1)S(1)} collective-permute-done((bf16[2,128,1024]{2,1,0:T(8,128)(2,1)S(1)}, bf16[2,128,1024]{2,1,0:T(8,128)(2,1)S(1)}, u32[]{:S(2)}, u32[]{:S(2)}) %collective-permute-start.42) | collective-permute-done | bytes 524320 | tf_op jit(solution)/shard_map/ppermute | solution.py:257
  1043.1 12.7 collective-permute-done.44
  1056.2 26.3 %collective-permute-done.43 = bf16[128,1024]{1,0:T(8,128)(2,1)S(1)} collective-permute-done((bf16[128,1024]{1,0:T(8,128)(2,1)S(1)}, bf16[128,1024]{1,0:T(8,128)(2,1)S(1)}, u32[]{:S(2)}, u32[]{:S(2)}) %collective-permute-start.43) | collective-permute-done | bytes 262176 | tf_op jit(solution)/shard_map/ppermute | solution.py:262
  1082.5 18.2 %collective-permute-done.45 = bf16[128,1024]{1,0:T(8,128)(2,1)S(1)} collective-permute-done((bf16[128,1024]{1,0:T(8,128)(2,1)S(1)}, bf16[128,1024]{1,0:T(8,128)(2,1)S(1)}, u32[]{:S(2)}, u32[]{:S(2)}) %collective-permute-start.45) | collective-permute-done | bytes 262176 | tf_op jit(solution)/shard_map/ppermute | solution.py:262
  1100.8 37.4 %all-gather.8.cloned.1.call-done = bf16[2048,3840]{1,0:T(8,128)(2,1)} async-done(((bf16[128,3840]{1,0:T(8,128)(2,1)}), bf16[2048,3840]{1,0:T(8,128)(2,1)}) %all-gather.8.cloned.1.call-update) | async-done | bytes 15728656 | tf_op jit(solution)/shard_map/all_gather | solution.py:267
  1157.2 30.5 %collective-permute-done.50 = f32[4,2048]{1,0:T(4,128)S(1)} collective-permute-done((f32[4,2048]{1,0:T(4,128)S(1)}, f32[4,2048]{1,0:T(4,128)S(1)}, u32[]{:S(2)}, u32[]{:S(2)}) %collective-permute-start.50) | collective-permute-done | bytes 32800 | tf_op jit(solution)/shard_map/ppermute | solution.py:210
  1188.3 14.6 %fusion.34 = f32[1,512,2048]{2,1,0:T(8,128)} fusion(bf16[512,2048]{1,0:T(8,128)(2,1)} %collective-permute-done.26, f32[512,2048]{1,0:T(8,128)} %get-tuple-element.141, bf16[2048,3,1024]{2,0,1:T(8,128)(2,1)} %param.16, bf16[3,1024,1024]{2,1,0:T(8,128)(2,1)} %attend_back.1), kind=kOutput, calls=%fused_computation.105 | convolution fusion | flops 6446645248 | bytes 26214400 | tf_op jit(solution)/shard_map/kte,dke->td/dot_general | solution.py:442
  1264.0 162.3 %copy.31 = f32[2048,2,2816]{2,1,0:T(2,128)} copy(bf16[2048,2,2816]{2,0,1:T(8,128)(2,1)S(1)} %pad_maximum_fusion) | data formatting | bytes 69206016
  1426.3 14.2 convert_element_type.412
  (372 shorter events, 451.1 us)
Async XLA Ops:
  7.2 968.6 %all-gather.12.cloned.1.call-start = ((), (), s32[]{:S(2)}) async-start(), calls=%async_computation.3 | async-start | bytes 12255232 | tf_op jit(solution)/shard_map/all_gather | solution.py:271
  7.2 49.0 %collective-permute-start = (bf16[512,2048]{1,0:T(8,128)(2,1)}, bf16[512,2048]{1,0:T(8,128)(2,1)}, u32[]{:S(2)}, u32[]{:S(2)}) collective-permute-start(bf16[512,2048]{1,0:T(8,128)(2,1)} %bitcast.375), channel_id=1, source_target_pairs={{0,1},{1,0},{2,3},{3,2},{4,5},{5,4},{6,7},{7,6},{8,9},{9,8},{10,11... | collective-permute-start | bytes 6291464 | tf_op jit(solution)/shard_map/ppermute | solution.py:185
  98.8 46.9 %collective-permute-start.1 = (bf16[512,2048]{1,0:T(8,128)(2,1)S(1)}, bf16[512,2048]{1,0:T(8,128)(2,1)S(1)}, u32[]{:S(2)}, u32[]{:S(2)}) collective-permute-start(bf16[512,2048]{1,0:T(8,128)(2,1)S(1)} %convolution_convert_fusion.6), channel_id=1, source_target_pairs={{0,1},{1,0},{2,3},{3,2},{4,5},{5,4},{6,7},{7,6},{8,9},{9,8},{10,11... | collective-permute-start | bytes 6291464 | tf_op jit(solution)/shard_map/ppermute | solution.py:197
  149.9 47.4 %collective-permute-start.2 = (bf16[512,2048]{1,0:T(8,128)(2,1)S(1)}, bf16[512,2048]{1,0:T(8,128)(2,1)}, u32[]{:S(2)}, u32[]{:S(2)}) collective-permute-start(bf16[512,2048]{1,0:T(8,128)(2,1)S(1)} %fusion.35), channel_id=1, source_target_pairs={{0,1},{1,0},{2,3},{3,2},{4,5},{5,4},{6,7},{7,6},{8,9},{9,8},{10,11... | collective-permute-start | bytes 6291464 | tf_op jit(solution)/shard_map/ppermute | solution.py:185
  238.2 45.4 %collective-permute-start.3 = (bf16[512,2048]{1,0:T(8,128)(2,1)}, bf16[512,2048]{1,0:T(8,128)(2,1)}, u32[]{:S(2)}, u32[]{:S(2)}) collective-permute-start(bf16[512,2048]{1,0:T(8,128)(2,1)} %convolution_convert_fusion.7), channel_id=1, source_target_pairs={{0,1},{1,0},{2,3},{3,2},{4,5},{5,4},{6,7},{7,6},{8,9},{9,8},{10,11... | collective-permute-start | bytes 6291464 | tf_op jit(solution)/shard_map/ppermute | solution.py:197
  302.9 44.6 %collective-permute-start.7 = (bf16[512,2048]{1,0:T(8,128)(2,1)}, bf16[512,2048]{1,0:T(8,128)(2,1)}, u32[]{:S(2)}, u32[]{:S(2)}) collective-permute-start(bf16[512,2048]{1,0:T(8,128)(2,1)} %fusion.218), channel_id=1, source_target_pairs={{0,1},{1,0},{2,3},{3,2},{4,5},{5,4},{6,7},{7,6},{8,9},{9,8},{10,11... | collective-permute-start | bytes 6291464 | tf_op jit(solution)/shard_map/ppermute | solution.py:185
  359.1 45.1 %collective-permute-start.9 = (bf16[2816,512]{1,0:T(8,128)(2,1)}, bf16[2816,512]{1,0:T(8,128)(2,1)}, u32[]{:S(2)}, u32[]{:S(2)}) collective-permute-start(bf16[2816,512]{1,0:T(8,128)(2,1)} %convolution_convert_fusion.4), channel_id=1, source_target_pairs={{0,2},{2,0},{4,6},{6,4},{1,3},{3,1},{5,7},{7,5},{8,10},{10,8},{12,... | collective-permute-start | bytes 8650760 | tf_op jit(solution)/shard_map/ppermute | solution.py:236
  435.9 47.9 %collective-permute-start.10 = (bf16[512,2048]{1,0:T(8,128)(2,1)}, bf16[512,2048]{1,0:T(8,128)(2,1)}, u32[]{:S(2)}, u32[]{:S(2)}) collective-permute-start(bf16[512,2048]{1,0:T(8,128)(2,1)} %bitcast_convert_fusion.1), channel_id=1, source_target_pairs={{0,1},{1,0},{2,3},{3,2},{4,5},{5,4},{6,7},{7,6},{8,9},{9,8},{10,11... | collective-permute-start | bytes 6291464 | tf_op jit(solution)/shard_map/ppermute | solution.py:197
  449.4 56.7 %collective-permute-start.11 = (bf16[512,2816]{1,0:T(8,128)(2,1)}, bf16[512,2816]{1,0:T(8,128)(2,1)}, u32[]{:S(2)}, u32[]{:S(2)}) collective-permute-start(bf16[512,2816]{1,0:T(8,128)(2,1)} %convolution_convert_fusion.3), channel_id=1, source_target_pairs={{0,2},{2,0},{4,6},{6,4},{1,3},{3,1},{5,7},{7,5},{8,10},{10,8},{12,... | collective-permute-start | bytes 8650760 | tf_op jit(solution)/shard_map/ppermute | solution.py:235
  455.3 59.5 %collective-permute-start.12 = (bf16[512,2816]{1,0:T(8,128)(2,1)}, bf16[512,2816]{1,0:T(8,128)(2,1)}, u32[]{:S(2)}, u32[]{:S(2)}) collective-permute-start(bf16[512,2816]{1,0:T(8,128)(2,1)} %convolution_convert_fusion.2), channel_id=1, source_target_pairs={{0,2},{2,0},{4,6},{6,4},{1,3},{3,1},{5,7},{7,5},{8,10},{10,8},{12,... | collective-permute-start | bytes 8650760 | tf_op jit(solution)/shard_map/ppermute | solution.py:236
  455.8 66.4 %collective-permute-start.13 = (bf16[2816,512]{1,0:T(8,128)(2,1)}, bf16[2816,512]{1,0:T(8,128)(2,1)}, u32[]{:S(2)}, u32[]{:S(2)}) collective-permute-start(bf16[2816,512]{1,0:T(8,128)(2,1)} %add_convert_fusion.2), channel_id=1, source_target_pairs={{0,4},{4,0},{2,6},{6,2},{1,5},{5,1},{3,7},{7,3},{8,12},{12,8},{10,... | collective-permute-start | bytes 8650760 | tf_op jit(solution)/shard_map/ppermute | solution.py:242
  463.3 83.4 %collective-permute-start.15 = (bf16[512,2816]{1,0:T(8,128)(2,1)}, bf16[512,2816]{1,0:T(8,128)(2,1)}, u32[]{:S(2)}, u32[]{:S(2)}) collective-permute-start(bf16[512,2816]{1,0:T(8,128)(2,1)} %convolution_convert_fusion.1), channel_id=1, source_target_pairs={{0,2},{2,0},{4,6},{6,4},{1,3},{3,1},{5,7},{7,5},{8,10},{10,8},{12,... | collective-permute-start | bytes 8650760 | tf_op jit(solution)/shard_map/ppermute | solution.py:235
  483.8 69.4 %collective-permute-start.16 = (bf16[512,2816]{1,0:T(8,128)(2,1)}, bf16[512,2816]{1,0:T(8,128)(2,1)}, u32[]{:S(2)}, u32[]{:S(2)}) collective-permute-start(bf16[512,2816]{1,0:T(8,128)(2,1)} %convolution_convert_fusion), channel_id=1, source_target_pairs={{0,2},{2,0},{4,6},{6,4},{1,3},{3,1},{5,7},{7,5},{8,10},{10,8},{12,... | collective-permute-start | bytes 8650760 | tf_op jit(solution)/shard_map/ppermute | solution.py:236
  540.8 70.4 %collective-permute-start.14 = (bf16[512,2048]{1,0:T(8,128)(2,1)S(1)}, bf16[512,2048]{1,0:T(8,128)(2,1)S(1)}, u32[]{:S(2)}, u32[]{:S(2)}) collective-permute-start(bf16[512,2048]{1,0:T(8,128)(2,1)S(1)} %get-tuple-element.86), channel_id=1, source_target_pairs={{0,1},{1,0},{2,3},{3,2},{4,5},{5,4},{6,7},{7,6},{8,9},{9,8},{10,11... | collective-permute-start | bytes 6291464 | tf_op jit(solution)/shard_map/ppermute | solution.py:185
  541.4 64.9 %collective-permute-start.17 = (bf16[512,2816]{1,0:T(8,128)(2,1)}, bf16[512,2816]{1,0:T(8,128)(2,1)}, u32[]{:S(2)}, u32[]{:S(2)}) collective-permute-start(bf16[512,2816]{1,0:T(8,128)(2,1)} %add_convert_fusion.1), channel_id=1, source_target_pairs={{0,4},{4,0},{2,6},{6,2},{1,5},{5,1},{3,7},{7,3},{8,12},{12,8},{10,... | collective-permute-start | bytes 8650760 | tf_op jit(solution)/shard_map/ppermute | solution.py:242
  662.4 438.3 %all-gather.6.cloned.1.call-start = ((), (), s32[]{:S(2)}) async-start(), calls=%async_computation | async-start | bytes 12255232 | tf_op jit(solution)/shard_map/all_gather | solution.py:267
  662.5 79.9 %collective-permute-start.22 = (bf16[512,2816]{1,0:T(8,128)(2,1)}, bf16[512,2816]{1,0:T(8,128)(2,1)}, u32[]{:S(2)}, u32[]{:S(2)}) collective-permute-start(bf16[512,2816]{1,0:T(8,128)(2,1)} %add_convert_fusion), channel_id=1, source_target_pairs={{0,4},{4,0},{2,6},{6,2},{1,5},{5,1},{3,7},{7,3},{8,12},{12,8},{10,... | collective-permute-start | bytes 8650760 | tf_op jit(solution)/shard_map/ppermute | solution.py:242
  669.3 56.3 %collective-permute-start.23 = (bf16[2,128,2816]{2,1,0:T(8,128)(2,1)}, bf16[2,128,2816]{2,1,0:T(8,128)(2,1)}, u32[]{:S(2)}, u32[]{:S(2)}) collective-permute-start(bf16[2,128,2816]{2,1,0:T(8,128)(2,1)} %pad_maximum_fusion.5), channel_id=1, source_target_pairs={{0,8},{8,0},{16,24},{24,16},{1,9},{9,1},{17,25},{25,17},{2,10},{10... | collective-permute-start | bytes 4325384 | tf_op jit(solution)/shard_map/ppermute | solution.py:257
  748.0 73.1 %collective-permute-start.24 = (bf16[2,128,2816]{2,1,0:T(8,128)(2,1)}, bf16[2,128,2816]{2,1,0:T(8,128)(2,1)S(1)}, u32[]{:S(2)}, u32[]{:S(2)}) collective-permute-start(bf16[2,128,2816]{2,1,0:T(8,128)(2,1)} %pad_maximum_fusion.6), channel_id=1, source_target_pairs={{0,8},{8,0},{16,24},{24,16},{1,9},{9,1},{17,25},{25,17},{2,10},{10... | collective-permute-start | bytes 4325384 | tf_op jit(solution)/shard_map/ppermute | solution.py:257
  748.2 70.7 %collective-permute-start.25 = (bf16[128,2816]{1,0:T(8,128)(2,1)S(1)}, bf16[128,2816]{1,0:T(8,128)(2,1)}, u32[]{:S(2)}, u32[]{:S(2)}) collective-permute-start(bf16[128,2816]{1,0:T(8,128)(2,1)S(1)} %fusion.164), channel_id=1, source_target_pairs={{0,16},{16,0},{8,24},{24,8},{1,17},{17,1},{9,25},{25,9},{2,18},{18... | collective-permute-start | bytes 2162696 | tf_op jit(solution)/shard_map/ppermute | solution.py:262
  824.6 313.5 %all-gather.8.cloned.1.call-start = ((), (), s32[]{:S(2)}) async-start(), calls=%async_computation.1 | async-start | bytes 16711680 | tf_op jit(solution)/shard_map/all_gather | solution.py:267
  881.4 74.3 %collective-permute-start.34 = (bf16[512,1024]{1,0:T(8,128)(2,1)S(1)}, bf16[512,1024]{1,0:T(8,128)(2,1)S(1)}, u32[]{:S(2)}, u32[]{:S(2)}) collective-permute-start(bf16[512,1024]{1,0:T(8,128)(2,1)S(1)} %add_convert_fusion.6), channel_id=1, source_target_pairs={{0,4},{4,0},{2,6},{6,2},{1,5},{5,1},{3,7},{7,3},{8,12},{12,8},{10,... | collective-permute-start | bytes 3145736 | tf_op jit(solution)/shard_map/ppermute | solution.py:242
  882.9 74.5 %collective-permute-start.35 = (bf16[512,1024]{1,0:T(8,128)(2,1)S(1)}, bf16[512,1024]{1,0:T(8,128)(2,1)S(1)}, u32[]{:S(2)}, u32[]{:S(2)}) collective-permute-start(bf16[512,1024]{1,0:T(8,128)(2,1)S(1)} %add_convert_fusion.5), channel_id=1, source_target_pairs={{0,4},{4,0},{2,6},{6,2},{1,5},{5,1},{3,7},{7,3},{8,12},{12,8},{10,... | collective-permute-start | bytes 3145736 | tf_op jit(solution)/shard_map/ppermute | solution.py:242
  883.4 87.4 %collective-permute-start.36 = (bf16[512,1024]{1,0:T(8,128)(2,1)S(1)}, bf16[512,1024]{1,0:T(8,128)(2,1)S(1)}, u32[]{:S(2)}, u32[]{:S(2)}) collective-permute-start(bf16[512,1024]{1,0:T(8,128)(2,1)S(1)} %add_convert_fusion.4), channel_id=1, source_target_pairs={{0,4},{4,0},{2,6},{6,2},{1,5},{5,1},{3,7},{7,3},{8,12},{12,8},{10,... | collective-permute-start | bytes 3145736 | tf_op jit(solution)/shard_map/ppermute | solution.py:242
  911.2 44.4 %collective-permute-start.39 = (bf16[128,1024]{1,0:T(8,128)(2,1)S(1)}, bf16[128,1024]{1,0:T(8,128)(2,1)S(1)}, u32[]{:S(2)}, u32[]{:S(2)}) collective-permute-start(bf16[128,1024]{1,0:T(8,128)(2,1)S(1)} %fusion.182), channel_id=1, source_target_pairs={{0,16},{16,0},{8,24},{24,8},{1,17},{17,1},{9,25},{25,9},{2,18},{18... | collective-permute-start | bytes 786440 | tf_op jit(solution)/shard_map/ppermute | solution.py:262
  911.8 63.0 %collective-permute-start.37 = (bf16[128,2816]{1,0:T(8,128)(2,1)S(1)}, bf16[128,2816]{1,0:T(8,128)(2,1)S(1)}, u32[]{:S(2)}, u32[]{:S(2)}) collective-permute-start(bf16[128,2816]{1,0:T(8,128)(2,1)S(1)} %fusion.165), channel_id=1, source_target_pairs={{0,16},{16,0},{8,24},{24,8},{1,17},{17,1},{9,25},{25,9},{2,18},{18... | collective-permute-start | bytes 2162696 | tf_op jit(solution)/shard_map/ppermute | solution.py:262
  977.9 448.4 %all-gather.10.cloned.1.call-start = ((), (), s32[]{:S(2)}) async-start(), calls=%async_computation.2 | async-start | bytes 13369344 | tf_op jit(solution)/shard_map/all_gather | solution.py:267
  980.9 61.9 %collective-permute-start.42 = (bf16[2,128,1024]{2,1,0:T(8,128)(2,1)S(1)}, bf16[2,128,1024]{2,1,0:T(8,128)(2,1)S(1)}, u32[]{:S(2)}, u32[]{:S(2)}) collective-permute-start(bf16[2,128,1024]{2,1,0:T(8,128)(2,1)S(1)} %pad_maximum_fusion.13), channel_id=1, source_target_pairs={{0,8},{8,0},{16,24},{24,16},{1,9},{9,1},{17,25},{25,17},{2,10},{10... | collective-permute-start | bytes 1572872 | tf_op jit(solution)/shard_map/ppermute | solution.py:257
  984.7 71.1 %collective-permute-start.44 = (bf16[2,128,1024]{2,1,0:T(8,128)(2,1)S(1)}, bf16[2,128,1024]{2,1,0:T(8,128)(2,1)S(1)}, u32[]{:S(2)}, u32[]{:S(2)}) collective-permute-start(bf16[2,128,1024]{2,1,0:T(8,128)(2,1)S(1)} %pad_maximum_fusion.14), channel_id=1, source_target_pairs={{0,8},{8,0},{16,24},{24,16},{1,9},{9,1},{17,25},{25,17},{2,10},{10... | collective-permute-start | bytes 1572872 | tf_op jit(solution)/shard_map/ppermute | solution.py:257
  1012.0 44.2 %collective-permute-start.41 = (bf16[128,1024]{1,0:T(8,128)(2,1)S(1)}, bf16[128,1024]{1,0:T(8,128)(2,1)S(1)}, u32[]{:S(2)}, u32[]{:S(2)}) collective-permute-start(bf16[128,1024]{1,0:T(8,128)(2,1)S(1)} %fusion.183), channel_id=1, source_target_pairs={{0,16},{16,0},{8,24},{24,8},{1,17},{17,1},{9,25},{25,9},{2,18},{18... | collective-permute-start | bytes 786440 | tf_op jit(solution)/shard_map/ppermute | solution.py:262
  1056.0 44.7 %collective-permute-start.45 = (bf16[128,1024]{1,0:T(8,128)(2,1)S(1)}, bf16[128,1024]{1,0:T(8,128)(2,1)S(1)}, u32[]{:S(2)}, u32[]{:S(2)}) collective-permute-start(bf16[128,1024]{1,0:T(8,128)(2,1)S(1)} %fusion.185), channel_id=1, source_target_pairs={{0,16},{16,0},{8,24},{24,8},{1,17},{17,1},{9,25},{25,9},{2,18},{18... | collective-permute-start | bytes 786440 | tf_op jit(solution)/shard_map/ppermute | solution.py:262
  1139.1 49.2 %collective-permute-start.26 = (bf16[512,2048]{1,0:T(8,128)(2,1)S(1)}, bf16[512,2048]{1,0:T(8,128)(2,1)}, u32[]{:S(2)}, u32[]{:S(2)}) collective-permute-start(bf16[512,2048]{1,0:T(8,128)(2,1)S(1)} %copy-done.51), channel_id=1, source_target_pairs={{0,1},{1,0},{2,3},{3,2},{4,5},{5,4},{6,7},{7,6},{8,9},{9,8},{10,11... | collective-permute-start | bytes 6291464 | tf_op jit(solution)/shard_map/ppermute | solution.py:197
  (85 other events, 2500.7 us)
Sparse Core Ops, SparseCore 0:
  662.6 142.2 all-gather.11
  824.7 140.6 all-gather.5
  978.1 160.0 all-gather.7
  1140.2 100.8 all-gather.9

commit v5 on v4

--- a/solution.py
+++ b/solution.py
@@ -422,13 +422,11 @@
         ).astype(BF16)
 
     d_mixed = jnp.concatenate([unmix(d_attn_own), unmix(d_attn_other)], axis=0)
-    d_mixed, (far_out, near_out), share_down = tie(
-        (d_mixed, core_stage(make_out, gives_out), share_down)
-    )
+    d_mixed, (far_out, near_out) = tie((d_mixed, core_stage(make_out, gives_out)))
     near_out = x_stage(far_out, near_out)
+    d_qkv = attend_back(info, qkv, d_mixed, cos_vals, sin_vals)
+    d_qkv, near_up, pair_gate, share_down = tie((d_qkv, near_up, pair_gate, share_down))
     all_down = gather_columns_of(share_down)
-    d_qkv = attend_back(info, qkv, d_mixed, cos_vals, sin_vals)
-    d_qkv, near_up, pair_gate = tie((d_qkv, near_up, pair_gate))
     pair_up = z_near_stage(near_up, 0)
     share_gate = z_far_stage(pair_gate)
     x_rows = jnp.concatenate([x_own, x_other], axis=0)
@@ -442,15 +440,15 @@
         return jnp.einsum("kte,dke->td", d_rows, w_qkv, preferred_element_type=F32)
 
     parts_qkv = [core_stage(make_qkv(k), gives_qkv[k]) for k in range(3)]
-    parts_qkv, near_out = tie((parts_qkv, near_out))
+    parts_qkv, near_out, pair_up = tie((parts_qkv, near_out, pair_up))
     pair_out = z_near_stage(near_out, 0)
     near_qkv = [x_stage(far, near) for far, near in parts_qkv]
     d_x_send = unproject(d_qkv[:, share_len:]).astype(BF16)
-    d_x_send, pair_up, share_gate = tie((d_x_send, pair_up, share_gate))
     share_up = z_far_stage(pair_up)
     share_out = z_far_stage(pair_out)
-    all_gate = gather_rows_of(share_gate)
-    near_qkv, share_up, share_out, all_down = tie((near_qkv, share_up, share_out, all_down))
+    near_qkv, share_gate, share_up, share_out, all_down = tie(
+        (near_qkv, share_gate, share_up, share_out, all_down)
+    )
     d_x = scatter_rows(unproject(d_qkv[:, :share_len]), d_x_send)
     input_grad = DEEP_ALPHA * d_z_one + d_x
 
@@ -460,14 +458,14 @@
     local = width // lax.axis_size("tp")
     norm_terms = lax.dynamic_slice_in_dim(norm_terms, tp_index * local, local, 1)
 
-    all_up_out = gather_rows_of(jnp.concatenate([share_up, share_out], axis=1))
-    share_qkv = [z_far_stage(z_near_stage(near, 0)) for near in near_qkv]
-    share_qkv, all_gate, all_up_out = tie((share_qkv, all_gate, all_up_out))
-    grad_qkv = gather_rows_of(jnp.stack(share_qkv, axis=1)).astype(F32)
-    all_up, all_out = all_up_out[:, :local_ff], all_up_out[:, local_ff:]
-    grad_gate_up = tie(jnp.stack([all_gate, all_up], axis=1)).astype(F32)
+    all_gate_up = gather_rows_of(jnp.stack([share_gate, share_up], axis=1))
+    share_last = [z_far_stage(z_near_stage(near, 0)) for near in near_qkv] + [share_out]
+    share_last, all_gate_up = tie((share_last, all_gate_up))
+    all_last = gather_rows_of(jnp.stack(share_last, axis=1))
+    grad_qkv = all_last[:, :3].astype(F32)
+    grad_out = all_last[:, 3].T.astype(F32)
+    grad_gate_up = all_gate_up.astype(F32)
     grad_down = widen(all_down)
-    grad_out = all_out.T.astype(F32)
     return (
         outputs[None],
         input_grad[None],

time: 1460 us -> 1410 us (0.966)
  waiting for transfers between devices: 645 us -> 628 us
    ppermute x7, waiting for transfers between devices: 171 us -> 56.6 us  [z_far_stage(): got = lax.ppermute(pair[1].astype(BF16), 'obj', Z_FAR)]
    all_gather x3 -> x2, waiting for transfers between devices: 37.4 us -> 89.5 us  [gather_rows_of(): return lax.all_gather(share, GROUP, axis=0, tiled=True)]
    ppermute x7, waiting for transfers between devices: 125 us -> 176 us  [z_near_stage(): got = lax.ppermute(pieces(obj_index ^ 1).astype(BF16), 'obj', Z_NEAR)]
    unnamed x142 -> x148, local copies, waits for them, and re-layouts: 200 us -> 201 us
  transfers between devices with their start and end apart: 55 -> 54, of which waited for: 30 -> 29; matrix products, arithmetic and copies ran while one was open for 36% -> 33% of each run, Pallas kernels for 3% -> 3%
where the time goes in v5:
time: 1410 us
  waiting for transfers between devices  628 us (45%)
  matrix products  310 us (22%)
  local copies, waits for them, and re-layouts  213 us (15%)
  other arithmetic  121 us (9%)
  Pallas kernels  70.6 us (5%)
  starting transfers between devices  47.1 us (3%)
  between operations  16.7 us (1%)
    unnamed x148, local copies, waits for them, and re-layouts  201 us
    ppermute x7, waiting for transfers between devices, z_near_stage(): got = lax.ppermute(pieces(obj_index ^ 1).astype(BF16), 'obj', Z_NEAR)  176 us
    dot_general x28, matrix products, token_sum(): lax.dot_general(left, right, (((0,), (0,)), ((), ())), preferred_element_...  112 us
    all_gather x2, waiting for transfers between devices, gather_rows_of(): return lax.all_gather(share, GROUP, axis=0, tiled=True)  89.5 us
    ppermute x7, waiting for transfers between devices, x_stage(): return near + lax.ppermute(far, 'dp', X_SWAP).astype(F32)  81.8 us
    ppermute x8, waiting for transfers between devices, all_sum(): lax.ppermute(value, axis, [(i, i ^ step) for i in range(size)])  79.3 us
    ppermute x4, waiting for transfers between devices, scatter_rows(): lax.ppermute(send_part, 'tp', [(0, 1), (1, 0)]).astype(F32)  74.4 us
    ppermute x4, waiting for transfers between devices, gather_rows(): return lax.ppermute(own, 'tp', [(0, 1), (1, 0)])  70.6 us
  transfers between devices with their start and end apart: 54, of which 29 were waited for; matrix products, arithmetic and copies ran while one was open for 33% of the time, Pallas kernels for 3%

profile of v5, /device:TPU:0, one launch (start us, length us, event | category | flops | bytes accessed | tf_op | source)
XLA Modules:
  0.0 1406.5 jit_solution(16618657938191958069)
XLA Ops:
  14.8 11.6 convolution_bitcast_fusion.1.own_ref
  26.4 29.8 %collective-permute-done = bf16[512,2048]{1,0:T(8,128)(2,1)} collective-permute-done((bf16[512,2048]{1,0:T(8,128)(2,1)}, bf16[512,2048]{1,0:T(8,128)(2,1)}, u32[]{:S(2)}, u32[]{:S(2)}) %collective-permute-start) | collective-permute-done | bytes 2097184 | tf_op jit(solution)/shard_map/ppermute | solution.py:185
  66.3 27.5 %attend.1 = (bf16[1024,1024]{1,0:T(8,128)(2,1)}, bf16[3,1024,1024]{2,1,0:T(8,128)(2,1)}) custom-call(s32[2]{0:T(128)} %pad_add_fusion.info_ref, f32[3,512,1024]{2,1,0:T(8,128)} %convolution_bitcast_fusion.1.own_ref, f32[3,512,1024]{2,1,0:T(8,128)} %convolution_bitcast_fusion.other_ref, f32[1024,128]{1,0:T(8,128)} %get-tuple-element.195.cos_ref, ...), custom_call_target="tpu_custom_call" | custom-call | flops 8589934592 | bytes 20971520 | tf_op jit(solution)/shard_map/attend/pallas_call | solution.py:120
  100.6 45.1 %collective-permute-done.1 = bf16[512,2048]{1,0:T(8,128)(2,1)S(1)} collective-permute-done((bf16[512,2048]{1,0:T(8,128)(2,1)S(1)}, bf16[512,2048]{1,0:T(8,128)(2,1)S(1)}, u32[]{:S(2)}, u32[]{:S(2)}) %collective-permute-start.1) | collective-permute-done | bytes 2097184 | tf_op jit(solution)/shard_map/ppermute | solution.py:197
  159.6 36.5 %collective-permute-done.6 = f32[8,128]{1,0:T(8,128)S(1)} collective-permute-done((f32[8,128]{1,0:T(8,128)S(1)}, f32[8,128]{1,0:T(8,128)S(1)}, u32[]{:S(2)}, u32[]{:S(2)}) %collective-permute-start.6) | collective-permute-done | bytes 4128 | tf_op jit(solution)/shard_map/ppermute | solution.py:210
  197.3 21.4 %fusion.4 = f32[512,2,2816]{2,0,1:T(8,128)} fusion(bf16[2048,2,2816]{2,1,0:T(2,128)(2,1)} %param.20, bf16[512,2048]{1,0:T(8,128)(2,1)} %collective-permute-done.2), kind=kOutput, calls=%fused_computation.4 | convolution fusion | flops 11811160064 | bytes 36700160 | tf_op jit(solution)/shard_map/td,dke->tke/dot_general | solution.py:343
  239.3 20.9 %fusion.6 = f32[512,2,2816]{2,0,1:T(8,128)} fusion(bf16[2048,2,2816]{2,1,0:T(2,128)(2,1)} %param.20, bf16[512,2048]{1,0:T(8,128)(2,1)S(1)} %fusion.35), kind=kOutput, calls=%fused_computation.6 | convolution fusion | flops 11811160064 | bytes 36700160 | tf_op jit(solution)/shard_map/td,dke->tke/dot_general | solution.py:343
  268.6 15.0 %collective-permute-done.3 = bf16[512,2048]{1,0:T(8,128)(2,1)} collective-permute-done((bf16[512,2048]{1,0:T(8,128)(2,1)}, bf16[512,2048]{1,0:T(8,128)(2,1)}, u32[]{:S(2)}, u32[]{:S(2)}) %collective-permute-start.3) | collective-permute-done | bytes 2097184 | tf_op jit(solution)/shard_map/ppermute | solution.py:197
  306.8 40.8 %collective-permute-done.7 = bf16[512,2048]{1,0:T(8,128)(2,1)} collective-permute-done((bf16[512,2048]{1,0:T(8,128)(2,1)}, bf16[512,2048]{1,0:T(8,128)(2,1)}, u32[]{:S(2)}, u32[]{:S(2)}) %collective-permute-start.7) | collective-permute-done | bytes 2097184 | tf_op jit(solution)/shard_map/ppermute | solution.py:185
  359.7 15.1 %fusion.46 = (bf16[1,512,2816]{2,1,0:T(8,128)(2,1)}, bf16[1,512,2816]{2,1,0:T(8,128)(2,1)}) fusion(f32[512,2816]{1,0:T(8,128)} %get-tuple-element.74, f32[512,2816]{1,0:T(8,128)} %get-tuple-element.75, bf16[512,2048]{1,0:T(8,128)(2,1)} %collective-permute-done.7, bf16[2816,2048]{1,0:T(8,128)(2,1)} %param.21), kind=kOutput, calls=%fused_computation.128 | convolution fusion | flops 5911347200 | bytes 30932992 | tf_op jit(solution)/shard_map/dot_general | solution.py:368
  380.5 15.1 %fusion.44 = (bf16[1,512,2816]{2,1,0:T(8,128)(2,1)}, bf16[1,512,2816]{2,1,0:T(8,128)(2,1)}) fusion(f32[512,2816]{1,0:T(8,128)} %get-tuple-element.69, f32[512,2816]{1,0:T(8,128)} %get-tuple-element.70, bf16[512,2048]{1,0:T(8,128)(2,1)} %fusion.218, bf16[2816,2048]{1,0:T(8,128)(2,1)} %param.21), kind=kOutput, calls=%fused_computation.126 | convolution fusion | flops 5911347200 | bytes 30932992 | tf_op jit(solution)/shard_map/dot_general | solution.py:368
  413.8 22.1 %bitcast_convert_fusion.1 = bf16[512,2048]{1,0:T(8,128)(2,1)} fusion(bf16[2,512,2816]{2,1,0:T(8,128)(2,1)} %pad_maximum_fusion.1, bf16[2048,2,2816]{2,1,0:T(2,128)(2,1)} %param.20), kind=kOutput, calls=%fused_computation.106 | convolution fusion | flops 11812208640 | bytes 30932992 | tf_op jit(solution)/shard_map/kte,dke->td/dot_general | solution.py:382
  469.4 14.3 %collective-permute-done.10 = bf16[512,2048]{1,0:T(8,128)(2,1)} collective-permute-done((bf16[512,2048]{1,0:T(8,128)(2,1)}, bf16[512,2048]{1,0:T(8,128)(2,1)}, u32[]{:S(2)}, u32[]{:S(2)}) %collective-permute-start.10) | collective-permute-done | bytes 2097184 | tf_op jit(solution)/shard_map/ppermute | solution.py:197
  483.8 22.4 %bitcast_add_fusion.1 = f32[512,2048]{1,0:T(8,128)} fusion(bf16[512,2048]{1,0:T(8,128)(2,1)} %collective-permute-done.10, bf16[2048,2,2816]{2,1,0:T(2,128)(2,1)} %param.20, bf16[1,512,2816]{2,1,0:T(8,128)(2,1)} %get-tuple-element.162, bf16[1,512,2816]{2,1,0:T(8,128)(2,1)} %get-tuple-element.161), kind=kOutput, calls=%fused_computation.107 | convolution fusion | flops 11816140800 | bytes 35127296 | tf_op jit(solution)/shard_map/kte,dke->td/dot_general | solution.py:382
  562.3 16.2 %collective-permute-done.18 = bf16[2,2816,128]{2,1,0:T(8,128)(2,1)S(1)} collective-permute-done((bf16[2,2816,128]{2,1,0:T(8,128)(2,1)S(1)}, bf16[2,2816,128]{2,1,0:T(8,128)(2,1)S(1)}, u32[]{:S(2)}, u32[]{:S(2)}) %collective-permute-start.18) | collective-permute-done | bytes 1441824 | tf_op jit(solution)/shard_map/ppermute | solution.py:257
  578.7 27.6 %collective-permute-done.17 = bf16[512,2816]{1,0:T(8,128)(2,1)} collective-permute-done((bf16[512,2816]{1,0:T(8,128)(2,1)}, bf16[512,2816]{1,0:T(8,128)(2,1)}, u32[]{:S(2)}, u32[]{:S(2)}) %collective-permute-start.17) | collective-permute-done | bytes 2883616 | tf_op jit(solution)/shard_map/ppermute | solution.py:242
  629.1 25.6 %collective-permute-done.23 = bf16[2816,128]{1,0:T(8,128)(2,1)S(1)} collective-permute-done((bf16[2816,128]{1,0:T(8,128)(2,1)S(1)}, bf16[2816,128]{1,0:T(8,128)(2,1)S(1)}, u32[]{:S(2)}, u32[]{:S(2)}) %collective-permute-start.23) | collective-permute-done | bytes 720928 | tf_op jit(solution)/shard_map/ppermute | solution.py:262
  664.2 43.1 %attend_back.1 = bf16[3,1024,1024]{2,1,0:T(8,128)(2,1)} custom-call(s32[2]{0:T(128)} %pad_add_fusion.info_ref, bf16[3,1024,1024]{2,1,0:T(8,128)(2,1)} %get-tuple-element.80.qkv_ref, bf16[1024,1024]{1,0:T(8,128)(2,1)} %pad_maximum_fusion.2.grad_ref, f32[1024,128]{1,0:T(8,128)} %get-tuple-element.195.cos_ref, f32[1024,128]{1,0:T(8,128)} %get-tuple-element.196.sin_ref), custom_call_target="tpu_custom_call" | custom-call | flops 21474836480 | bytes 14680064 | tf_op jit(solution)/shard_map/attend_back/pallas_call | solution.py:154
  720.8 28.7 %collective-permute-done.31 = bf16[512,1024]{1,0:T(8,128)(2,1)S(1)} collective-permute-done((bf16[512,1024]{1,0:T(8,128)(2,1)}, bf16[512,1024]{1,0:T(8,128)(2,1)S(1)}, u32[]{:S(2)}, u32[]{:S(2)}) %collective-permute-start.31) | collective-permute-done | bytes 1048608 | tf_op jit(solution)/shard_map/ppermute | solution.py:242
  773.2 81.8 %collective-permute-done.32 = bf16[2,128,2816]{2,1,0:T(8,128)(2,1)S(1)} collective-permute-done((bf16[2,128,2816]{2,1,0:T(8,128)(2,1)S(1)}, bf16[2,128,2816]{2,1,0:T(8,128)(2,1)S(1)}, u32[]{:S(2)}, u32[]{:S(2)}) %collective-permute-start.32) | collective-permute-done | bytes 1441824 | tf_op jit(solution)/shard_map/ppermute | solution.py:257
  863.2 19.6 %collective-permute-done.38 = bf16[2,128,1024]{2,1,0:T(8,128)(2,1)S(1)} collective-permute-done((bf16[2,128,1024]{2,1,0:T(8,128)(2,1)S(1)}, bf16[2,128,1024]{2,1,0:T(8,128)(2,1)S(1)}, u32[]{:S(2)}, u32[]{:S(2)}) %collective-permute-start.38) | collective-permute-done | bytes 524320 | tf_op jit(solution)/shard_map/ppermute | solution.py:257
  908.4 20.7 %collective-permute-done.35 = bf16[512,1024]{1,0:T(8,128)(2,1)S(1)} collective-permute-done((bf16[512,1024]{1,0:T(8,128)(2,1)S(1)}, bf16[512,1024]{1,0:T(8,128)(2,1)S(1)}, u32[]{:S(2)}, u32[]{:S(2)}) %collective-permute-start.35) | collective-permute-done | bytes 1048608 | tf_op jit(solution)/shard_map/ppermute | solution.py:242
  936.6 19.0 %collective-permute-done.40 = bf16[2,128,1024]{2,1,0:T(8,128)(2,1)S(1)} collective-permute-done((bf16[2,128,1024]{2,1,0:T(8,128)(2,1)S(1)}, bf16[2,128,1024]{2,1,0:T(8,128)(2,1)S(1)}, u32[]{:S(2)}, u32[]{:S(2)}) %collective-permute-start.40) | collective-permute-done | bytes 524320 | tf_op jit(solution)/shard_map/ppermute | solution.py:257
  955.9 22.2 %collective-permute-done.42 = bf16[2,128,1024]{2,1,0:T(8,128)(2,1)S(1)} collective-permute-done((bf16[2,128,1024]{2,1,0:T(8,128)(2,1)S(1)}, bf16[2,128,1024]{2,1,0:T(8,128)(2,1)S(1)}, u32[]{:S(2)}, u32[]{:S(2)}) %collective-permute-start.42) | collective-permute-done | bytes 524320 | tf_op jit(solution)/shard_map/ppermute | solution.py:257
  978.4 17.2 %collective-permute-done.44 = bf16[2,128,1024]{2,1,0:T(8,128)(2,1)S(1)} collective-permute-done((bf16[2,128,1024]{2,1,0:T(8,128)(2,1)S(1)}, bf16[2,128,1024]{2,1,0:T(8,128)(2,1)S(1)}, u32[]{:S(2)}, u32[]{:S(2)}) %collective-permute-start.44) | collective-permute-done | bytes 524320 | tf_op jit(solution)/shard_map/ppermute | solution.py:257
  1012.6 89.5 %all-gather.5.cloned.1.call-done = bf16[2048,2,2816]{2,0,1:T(8,128)(2,1)} async-done(((bf16[128,2,2816]{2,0,1:T(8,128)(2,1)}), bf16[2048,2,2816]{2,0,1:T(8,128)(2,1)}) %all-gather.5.cloned.1.call-update) | async-done | bytes 23068688 | tf_op jit(solution)/shard_map/all_gather | solution.py:267
  1103.2 11.6 bitcast_convert_fusion
  1136.9 20.4 %collective-permute-done.50 = f32[4,2048]{1,0:T(4,128)S(1)} collective-permute-done((f32[4,2048]{1,0:T(4,128)S(1)}, f32[4,2048]{1,0:T(4,128)S(1)}, u32[]{:S(2)}, u32[]{:S(2)}) %collective-permute-start.50) | collective-permute-done | bytes 32800 | tf_op jit(solution)/shard_map/ppermute | solution.py:210
  1157.9 14.2 %fusion.34 = f32[1,512,2048]{2,1,0:T(8,128)} fusion(bf16[512,2048]{1,0:T(8,128)(2,1)S(1)} %collective-permute-done.24, f32[512,2048]{1,0:T(8,128)} %get-tuple-element.139, bf16[2048,3,1024]{2,0,1:T(8,128)(2,1)} %param.16, bf16[3,1024,1024]{2,1,0:T(8,128)(2,1)} %attend_back.1), kind=kOutput, calls=%fused_computation.105 | convolution fusion | flops 6446645248 | bytes 26214400 | tf_op jit(solution)/shard_map/kte,dke->td/dot_general | solution.py:440
  1194.4 11.8 convert_element_type.420
  1207.5 162.3 %copy.31 = f32[2048,2,2816]{2,1,0:T(2,128)} copy(bf16[2048,2,2816]{2,0,1:T(8,128)(2,1)S(1)} %bitcast.360) | data formatting | bytes 69206016
  1385.5 14.2 %slice_convert_fusion = f32[2048,3,1024]{2,0,1:T(8,128)} fusion(bf16[2048,4,1024]{2,0,1:T(8,128)(2,1)} %all-gather.7.cloned.1.call-done), kind=kLoop, calls=%fused_computation.8 | loop fusion | flops 6291456 | bytes 37748736 | tf_op jit(solution)/shard_map/convert_element_type | solution.py:465
  (373 shorter events, 406.4 us)
Async XLA Ops:
  7.2 923.5 %all-gather.9.cloned.1.call-start = ((), (), s32[]{:S(2)}) async-start(), calls=%async_computation.2 | async-start | bytes 12255232 | tf_op jit(solution)/shard_map/all_gather | solution.py:271
  7.2 49.0 %collective-permute-start = (bf16[512,2048]{1,0:T(8,128)(2,1)}, bf16[512,2048]{1,0:T(8,128)(2,1)}, u32[]{:S(2)}, u32[]{:S(2)}) collective-permute-start(bf16[512,2048]{1,0:T(8,128)(2,1)} %bitcast.381), channel_id=1, source_target_pairs={{0,1},{1,0},{2,3},{3,2},{4,5},{5,4},{6,7},{7,6},{8,9},{9,8},{10,11... | collective-permute-start | bytes 6291464 | tf_op jit(solution)/shard_map/ppermute | solution.py:185
  98.8 46.9 %collective-permute-start.1 = (bf16[512,2048]{1,0:T(8,128)(2,1)S(1)}, bf16[512,2048]{1,0:T(8,128)(2,1)S(1)}, u32[]{:S(2)}, u32[]{:S(2)}) collective-permute-start(bf16[512,2048]{1,0:T(8,128)(2,1)S(1)} %convolution_convert_fusion.6), channel_id=1, source_target_pairs={{0,1},{1,0},{2,3},{3,2},{4,5},{5,4},{6,7},{7,6},{8,9},{9,8},{10,11... | collective-permute-start | bytes 6291464 | tf_op jit(solution)/shard_map/ppermute | solution.py:197
  149.9 47.4 %collective-permute-start.2 = (bf16[512,2048]{1,0:T(8,128)(2,1)S(1)}, bf16[512,2048]{1,0:T(8,128)(2,1)}, u32[]{:S(2)}, u32[]{:S(2)}) collective-permute-start(bf16[512,2048]{1,0:T(8,128)(2,1)S(1)} %fusion.35), channel_id=1, source_target_pairs={{0,1},{1,0},{2,3},{3,2},{4,5},{5,4},{6,7},{7,6},{8,9},{9,8},{10,11... | collective-permute-start | bytes 6291464 | tf_op jit(solution)/shard_map/ppermute | solution.py:185
  158.9 37.2 %collective-permute-start.6 = (f32[8,128]{1,0:T(8,128)S(1)}, f32[8,128]{1,0:T(8,128)S(1)}, u32[]{:S(2)}, u32[]{:S(2)}) collective-permute-start(f32[8,128]{1,0:T(8,128)S(1)} %fusion.265), channel_id=1, source_target_pairs={{0,1},{1,0},{2,3},{3,2},{4,5},{5,4},{6,7},{7,6},{8,9},{9,8},{10,11... | collective-permute-start | bytes 12296 | tf_op jit(solution)/shard_map/ppermute | solution.py:210
  238.2 45.4 %collective-permute-start.3 = (bf16[512,2048]{1,0:T(8,128)(2,1)}, bf16[512,2048]{1,0:T(8,128)(2,1)}, u32[]{:S(2)}, u32[]{:S(2)}) collective-permute-start(bf16[512,2048]{1,0:T(8,128)(2,1)} %convolution_convert_fusion.7), channel_id=1, source_target_pairs={{0,1},{1,0},{2,3},{3,2},{4,5},{5,4},{6,7},{7,6},{8,9},{9,8},{10,11... | collective-permute-start | bytes 6291464 | tf_op jit(solution)/shard_map/ppermute | solution.py:197
  302.9 44.6 %collective-permute-start.7 = (bf16[512,2048]{1,0:T(8,128)(2,1)}, bf16[512,2048]{1,0:T(8,128)(2,1)}, u32[]{:S(2)}, u32[]{:S(2)}) collective-permute-start(bf16[512,2048]{1,0:T(8,128)(2,1)} %fusion.218), channel_id=1, source_target_pairs={{0,1},{1,0},{2,3},{3,2},{4,5},{5,4},{6,7},{7,6},{8,9},{9,8},{10,11... | collective-permute-start | bytes 6291464 | tf_op jit(solution)/shard_map/ppermute | solution.py:185
  359.1 45.1 %collective-permute-start.9 = (bf16[2816,512]{1,0:T(8,128)(2,1)}, bf16[2816,512]{1,0:T(8,128)(2,1)}, u32[]{:S(2)}, u32[]{:S(2)}) collective-permute-start(bf16[2816,512]{1,0:T(8,128)(2,1)} %convolution_convert_fusion.4), channel_id=1, source_target_pairs={{0,2},{2,0},{4,6},{6,4},{1,3},{3,1},{5,7},{7,5},{8,10},{10,8},{12,... | collective-permute-start | bytes 8650760 | tf_op jit(solution)/shard_map/ppermute | solution.py:236
  435.9 47.9 %collective-permute-start.10 = (bf16[512,2048]{1,0:T(8,128)(2,1)}, bf16[512,2048]{1,0:T(8,128)(2,1)}, u32[]{:S(2)}, u32[]{:S(2)}) collective-permute-start(bf16[512,2048]{1,0:T(8,128)(2,1)} %bitcast_convert_fusion.1), channel_id=1, source_target_pairs={{0,1},{1,0},{2,3},{3,2},{4,5},{5,4},{6,7},{7,6},{8,9},{9,8},{10,11... | collective-permute-start | bytes 6291464 | tf_op jit(solution)/shard_map/ppermute | solution.py:197
  449.5 56.7 %collective-permute-start.11 = (bf16[512,2816]{1,0:T(8,128)(2,1)}, bf16[512,2816]{1,0:T(8,128)(2,1)}, u32[]{:S(2)}, u32[]{:S(2)}) collective-permute-start(bf16[512,2816]{1,0:T(8,128)(2,1)} %convolution_convert_fusion.3), channel_id=1, source_target_pairs={{0,2},{2,0},{4,6},{6,4},{1,3},{3,1},{5,7},{7,5},{8,10},{10,8},{12,... | collective-permute-start | bytes 8650760 | tf_op jit(solution)/shard_map/ppermute | solution.py:235
  455.3 59.5 %collective-permute-start.12 = (bf16[512,2816]{1,0:T(8,128)(2,1)}, bf16[512,2816]{1,0:T(8,128)(2,1)}, u32[]{:S(2)}, u32[]{:S(2)}) collective-permute-start(bf16[512,2816]{1,0:T(8,128)(2,1)} %convolution_convert_fusion.2), channel_id=1, source_target_pairs={{0,2},{2,0},{4,6},{6,4},{1,3},{3,1},{5,7},{7,5},{8,10},{10,8},{12,... | collective-permute-start | bytes 8650760 | tf_op jit(solution)/shard_map/ppermute | solution.py:236
  455.9 66.3 %collective-permute-start.13 = (bf16[2816,512]{1,0:T(8,128)(2,1)}, bf16[2816,512]{1,0:T(8,128)(2,1)}, u32[]{:S(2)}, u32[]{:S(2)}) collective-permute-start(bf16[2816,512]{1,0:T(8,128)(2,1)} %add_convert_fusion.2), channel_id=1, source_target_pairs={{0,4},{4,0},{2,6},{6,2},{1,5},{5,1},{3,7},{7,3},{8,12},{12,8},{10,... | collective-permute-start | bytes 8650760 | tf_op jit(solution)/shard_map/ppermute | solution.py:242
  463.3 83.4 %collective-permute-start.15 = (bf16[512,2816]{1,0:T(8,128)(2,1)}, bf16[512,2816]{1,0:T(8,128)(2,1)}, u32[]{:S(2)}, u32[]{:S(2)}) collective-permute-start(bf16[512,2816]{1,0:T(8,128)(2,1)} %convolution_convert_fusion.1), channel_id=1, source_target_pairs={{0,2},{2,0},{4,6},{6,4},{1,3},{3,1},{5,7},{7,5},{8,10},{10,8},{12,... | collective-permute-start | bytes 8650760 | tf_op jit(solution)/shard_map/ppermute | solution.py:235
  483.8 69.5 %collective-permute-start.16 = (bf16[512,2816]{1,0:T(8,128)(2,1)}, bf16[512,2816]{1,0:T(8,128)(2,1)}, u32[]{:S(2)}, u32[]{:S(2)}) collective-permute-start(bf16[512,2816]{1,0:T(8,128)(2,1)} %convolution_convert_fusion), channel_id=1, source_target_pairs={{0,2},{2,0},{4,6},{6,4},{1,3},{3,1},{5,7},{7,5},{8,10},{10,8},{12,... | collective-permute-start | bytes 8650760 | tf_op jit(solution)/shard_map/ppermute | solution.py:236
  540.8 67.9 %collective-permute-start.14 = (bf16[512,2048]{1,0:T(8,128)(2,1)S(1)}, bf16[512,2048]{1,0:T(8,128)(2,1)S(1)}, u32[]{:S(2)}, u32[]{:S(2)}) collective-permute-start(bf16[512,2048]{1,0:T(8,128)(2,1)S(1)} %get-tuple-element.85), channel_id=1, source_target_pairs={{0,1},{1,0},{2,3},{3,2},{4,5},{5,4},{6,7},{7,6},{8,9},{9,8},{10,11... | collective-permute-start | bytes 6291464 | tf_op jit(solution)/shard_map/ppermute | solution.py:185
  541.4 64.9 %collective-permute-start.17 = (bf16[512,2816]{1,0:T(8,128)(2,1)}, bf16[512,2816]{1,0:T(8,128)(2,1)}, u32[]{:S(2)}, u32[]{:S(2)}) collective-permute-start(bf16[512,2816]{1,0:T(8,128)(2,1)} %add_convert_fusion.1), channel_id=1, source_target_pairs={{0,4},{4,0},{2,6},{6,2},{1,5},{5,1},{3,7},{7,3},{8,12},{12,8},{10,... | collective-permute-start | bytes 8650760 | tf_op jit(solution)/shard_map/ppermute | solution.py:242
  618.1 37.6 %collective-permute-start.19 = (bf16[512,1024]{1,0:T(8,128)(2,1)}, bf16[512,1024]{1,0:T(8,128)(2,1)}, u32[]{:S(2)}, u32[]{:S(2)}) collective-permute-start(bf16[512,1024]{1,0:T(8,128)(2,1)} %convolution_convert_fusion.9), channel_id=1, source_target_pairs={{0,2},{2,0},{4,6},{6,4},{1,3},{3,1},{5,7},{7,5},{8,10},{10,8},{12,... | collective-permute-start | bytes 3145736 | tf_op jit(solution)/shard_map/ppermute | solution.py:235
  618.2 42.0 %collective-permute-start.20 = (bf16[512,1024]{1,0:T(8,128)(2,1)}, bf16[512,1024]{1,0:T(8,128)(2,1)}, u32[]{:S(2)}, u32[]{:S(2)}) collective-permute-start(bf16[512,1024]{1,0:T(8,128)(2,1)} %convolution_convert_fusion.8), channel_id=1, source_target_pairs={{0,2},{2,0},{4,6},{6,4},{1,3},{3,1},{5,7},{7,5},{8,10},{10,8},{12,... | collective-permute-start | bytes 3145736 | tf_op jit(solution)/shard_map/ppermute | solution.py:236
  618.7 92.1 %collective-permute-start.21 = (bf16[512,2816]{1,0:T(8,128)(2,1)}, bf16[512,2816]{1,0:T(8,128)(2,1)}, u32[]{:S(2)}, u32[]{:S(2)}) collective-permute-start(bf16[512,2816]{1,0:T(8,128)(2,1)} %add_convert_fusion), channel_id=1, source_target_pairs={{0,4},{4,0},{2,6},{6,2},{1,5},{5,1},{3,7},{7,3},{8,12},{12,8},{10,... | collective-permute-start | bytes 8650760 | tf_op jit(solution)/shard_map/ppermute | solution.py:242
  624.3 83.0 %collective-permute-start.22 = (bf16[2,128,2816]{2,1,0:T(8,128)(2,1)}, bf16[2,128,2816]{2,1,0:T(8,128)(2,1)S(1)}, u32[]{:S(2)}, u32[]{:S(2)}) collective-permute-start(bf16[2,128,2816]{2,1,0:T(8,128)(2,1)} %pad_maximum_fusion.4), channel_id=1, source_target_pairs={{0,8},{8,0},{16,24},{24,16},{1,9},{9,1},{17,25},{25,17},{2,10},{10... | collective-permute-start | bytes 4325384 | tf_op jit(solution)/shard_map/ppermute | solution.py:257
  717.4 384.6 %all-gather.5.cloned.1.call-start = ((), (), s32[]{:S(2)}) async-start(), calls=%async_computation | async-start | bytes 24510464 | tf_op jit(solution)/shard_map/all_gather | solution.py:267
  761.3 93.7 %collective-permute-start.32 = (bf16[2,128,2816]{2,1,0:T(8,128)(2,1)S(1)}, bf16[2,128,2816]{2,1,0:T(8,128)(2,1)S(1)}, u32[]{:S(2)}, u32[]{:S(2)}) collective-permute-start(bf16[2,128,2816]{2,1,0:T(8,128)(2,1)S(1)} %pad_maximum_fusion.5), channel_id=1, source_target_pairs={{0,8},{8,0},{16,24},{24,16},{1,9},{9,1},{17,25},{25,17},{2,10},{10... | collective-permute-start | bytes 4325384 | tf_op jit(solution)/shard_map/ppermute | solution.py:257
  764.4 94.2 %collective-permute-start.36 = (bf16[128,2816]{1,0:T(8,128)(2,1)S(1)}, bf16[128,2816]{1,0:T(8,128)(2,1)S(1)}, u32[]{:S(2)}, u32[]{:S(2)}) collective-permute-start(bf16[128,2816]{1,0:T(8,128)(2,1)S(1)} %fusion.164), channel_id=1, source_target_pairs={{0,16},{16,0},{8,24},{24,8},{1,17},{17,1},{9,25},{25,9},{2,18},{18... | collective-permute-start | bytes 2162696 | tf_op jit(solution)/shard_map/ppermute | solution.py:262
  855.4 39.9 %collective-permute-start.37 = (bf16[128,2816]{1,0:T(8,128)(2,1)S(1)}, bf16[128,2816]{1,0:T(8,128)(2,1)S(1)}, u32[]{:S(2)}, u32[]{:S(2)}) collective-permute-start(bf16[128,2816]{1,0:T(8,128)(2,1)S(1)} %fusion.165), channel_id=1, source_target_pairs={{0,16},{16,0},{8,24},{24,8},{1,17},{17,1},{9,25},{25,9},{2,18},{18... | collective-permute-start | bytes 2162696 | tf_op jit(solution)/shard_map/ppermute | solution.py:262
  859.6 42.0 %collective-permute-start.33 = (bf16[512,1024]{1,0:T(8,128)(2,1)S(1)}, bf16[512,1024]{1,0:T(8,128)(2,1)S(1)}, u32[]{:S(2)}, u32[]{:S(2)}) collective-permute-start(bf16[512,1024]{1,0:T(8,128)(2,1)S(1)} %add_convert_fusion.6), channel_id=1, source_target_pairs={{0,4},{4,0},{2,6},{6,2},{1,5},{5,1},{3,7},{7,3},{8,12},{12,8},{10,... | collective-permute-start | bytes 3145736 | tf_op jit(solution)/shard_map/ppermute | solution.py:242
  861.1 47.0 %collective-permute-start.34 = (bf16[512,1024]{1,0:T(8,128)(2,1)S(1)}, bf16[512,1024]{1,0:T(8,128)(2,1)S(1)}, u32[]{:S(2)}, u32[]{:S(2)}) collective-permute-start(bf16[512,1024]{1,0:T(8,128)(2,1)S(1)} %add_convert_fusion.5), channel_id=1, source_target_pairs={{0,4},{4,0},{2,6},{6,2},{1,5},{5,1},{3,7},{7,3},{8,12},{12,8},{10,... | collective-permute-start | bytes 3145736 | tf_op jit(solution)/shard_map/ppermute | solution.py:242
  861.6 67.5 %collective-permute-start.35 = (bf16[512,1024]{1,0:T(8,128)(2,1)S(1)}, bf16[512,1024]{1,0:T(8,128)(2,1)S(1)}, u32[]{:S(2)}, u32[]{:S(2)}) collective-permute-start(bf16[512,1024]{1,0:T(8,128)(2,1)S(1)} %add_convert_fusion.4), channel_id=1, source_target_pairs={{0,4},{4,0},{2,6},{6,2},{1,5},{5,1},{3,7},{7,3},{8,12},{12,8},{10,... | collective-permute-start | bytes 3145736 | tf_op jit(solution)/shard_map/ppermute | solution.py:242
  932.0 437.8 %all-gather.7.cloned.1.call-start = ((), (), s32[]{:S(2)}) async-start(), calls=%async_computation.1 | async-start | bytes 17825792 | tf_op jit(solution)/shard_map/all_gather | solution.py:267
  934.0 44.0 %collective-permute-start.42 = (bf16[2,128,1024]{2,1,0:T(8,128)(2,1)S(1)}, bf16[2,128,1024]{2,1,0:T(8,128)(2,1)S(1)}, u32[]{:S(2)}, u32[]{:S(2)}) collective-permute-start(bf16[2,128,1024]{2,1,0:T(8,128)(2,1)S(1)} %pad_maximum_fusion.12), channel_id=1, source_target_pairs={{0,8},{8,0},{16,24},{24,16},{1,9},{9,1},{17,25},{25,17},{2,10},{10... | collective-permute-start | bytes 1572872 | tf_op jit(solution)/shard_map/ppermute | solution.py:257
  936.3 59.3 %collective-permute-start.44 = (bf16[2,128,1024]{2,1,0:T(8,128)(2,1)S(1)}, bf16[2,128,1024]{2,1,0:T(8,128)(2,1)S(1)}, u32[]{:S(2)}, u32[]{:S(2)}) collective-permute-start(bf16[2,128,1024]{2,1,0:T(8,128)(2,1)S(1)} %pad_maximum_fusion.13), channel_id=1, source_target_pairs={{0,8},{8,0},{16,24},{24,16},{1,9},{9,1},{17,25},{25,17},{2,10},{10... | collective-permute-start | bytes 1572872 | tf_op jit(solution)/shard_map/ppermute | solution.py:257
  955.8 40.0 %collective-permute-start.41 = (bf16[128,1024]{1,0:T(8,128)(2,1)S(1)}, bf16[128,1024]{1,0:T(8,128)(2,1)S(1)}, u32[]{:S(2)}, u32[]{:S(2)}) collective-permute-start(bf16[128,1024]{1,0:T(8,128)(2,1)S(1)} %fusion.183), channel_id=1, source_target_pairs={{0,16},{16,0},{8,24},{24,8},{1,17},{17,1},{9,25},{25,9},{2,18},{18... | collective-permute-start | bytes 786440 | tf_op jit(solution)/shard_map/ppermute | solution.py:262
  1114.8 43.1 %collective-permute-start.24 = (bf16[512,2048]{1,0:T(8,128)(2,1)}, bf16[512,2048]{1,0:T(8,128)(2,1)S(1)}, u32[]{:S(2)}, u32[]{:S(2)}) collective-permute-start(bf16[512,2048]{1,0:T(8,128)(2,1)} %bitcast_convert_fusion), channel_id=1, source_target_pairs={{0,1},{1,0},{2,3},{3,2},{4,5},{5,4},{6,7},{7,6},{8,9},{9,8},{10,11... | collective-permute-start | bytes 6291464 | tf_op jit(solution)/shard_map/ppermute | solution.py:197
  (87 other events, 2233.4 us)
Sparse Core Ops, SparseCore 0:
  717.5 133.3 all-gather.8
  932.1 169.9 all-gather.4
  1104.9 126.6 all-gather.6

commit v6 on v5

--- a/solution.py
+++ b/solution.py
@@ -446,9 +446,7 @@
     d_x_send = unproject(d_qkv[:, share_len:]).astype(BF16)
     share_up = z_far_stage(pair_up)
     share_out = z_far_stage(pair_out)
-    near_qkv, share_gate, share_up, share_out, all_down = tie(
-        (near_qkv, share_gate, share_up, share_out, all_down)
-    )
+    near_qkv, share_gate, share_up, share_out = tie((near_qkv, share_gate, share_up, share_out))
     d_x = scatter_rows(unproject(d_qkv[:, :share_len]), d_x_send)
     input_grad = DEEP_ALPHA * d_z_one + d_x
 
@@ -460,7 +458,7 @@
 
     all_gate_up = gather_rows_of(jnp.stack([share_gate, share_up], axis=1))
     share_last = [z_far_stage(z_near_stage(near, 0)) for near in near_qkv] + [share_out]
-    share_last, all_gate_up = tie((share_last, all_gate_up))
+    share_last, all_down = tie((share_last, all_down))
     all_last = gather_rows_of(jnp.stack(share_last, axis=1))
     grad_qkv = all_last[:, :3].astype(F32)
     grad_out = all_last[:, 3].T.astype(F32)

time: 1410 us -> 1280 us (0.908)
  local copies, waits for them, and re-layouts: 213 us -> 94.1 us
  waiting for transfers between devices: 628 us -> 603 us
    unnamed x148 -> x132, local copies, waits for them, and re-layouts: 201 us -> 82.1 us
    all_gather x2, waiting for transfers between devices: 89.5 us -> 68.5 us  [gather_rows_of(): return lax.all_gather(share, GROUP, axis=0, tiled=True)]
  transfers between devices with their start and end apart: 54 -> 54, of which waited for: 29 -> 29; matrix products, arithmetic and copies ran while one was open for 33% -> 28% of each run, Pallas kernels for 3% -> 3%
where the time goes in v6:
time: 1280 us; the launch traced here: 1270 us
  waiting for transfers between devices  603 us (47%)
  matrix products  319 us (25%)
  other arithmetic  116 us (9%)
  local copies, waits for them, and re-layouts  94.1 us (7%)
  Pallas kernels  70.5 us (6%)
  starting transfers between devices  48.5 us (4%)
  between operations  16.6 us (1%)
    ppermute x7, waiting for transfers between devices, z_near_stage(): got = lax.ppermute(pieces(obj_index ^ 1).astype(BF16), 'obj', Z_NEAR)  177 us
    dot_general x28, matrix products, token_sum(): lax.dot_general(left, right, (((0,), (0,)), ((), ())), preferred_element_...  112 us
    unnamed x132, local copies, waits for them, and re-layouts  82.1 us
    ppermute x8, waiting for transfers between devices, all_sum(): lax.ppermute(value, axis, [(i, i ^ step) for i in range(size)])  82.1 us
    ppermute x7, waiting for transfers between devices, x_stage(): return near + lax.ppermute(far, 'dp', X_SWAP).astype(F32)  81.7 us
    ppermute x4, waiting for transfers between devices, gather_rows(): return lax.ppermute(own, 'tp', [(0, 1), (1, 0)])  70.6 us
    all_gather x2, waiting for transfers between devices, gather_rows_of(): return lax.all_gather(share, GROUP, axis=0, tiled=True)  68.5 us
    ppermute x4, waiting for transfers between devices, scatter_rows(): lax.ppermute(send_part, 'tp', [(0, 1), (1, 0)]).astype(F32)  66.2 us
  transfers between devices with their start and end apart: 54, of which 29 were waited for; matrix products, arithmetic and copies ran while one was open for 28% of the time, Pallas kernels for 3%

profile of v6, /device:TPU:0, one launch (start us, length us, event | category | flops | bytes accessed | tf_op | source)
XLA Modules:
  0.0 1267.3 jit_solution(15638204973984733330)
XLA Ops:
  14.9 11.6 convolution_bitcast_fusion.1.own_ref
  26.5 29.8 %collective-permute-done = bf16[512,2048]{1,0:T(8,128)(2,1)} collective-permute-done((bf16[512,2048]{1,0:T(8,128)(2,1)}, bf16[512,2048]{1,0:T(8,128)(2,1)}, u32[]{:S(2)}, u32[]{:S(2)}) %collective-permute-start) | collective-permute-done | bytes 2097184 | tf_op jit(solution)/shard_map/ppermute | solution.py:185
  66.3 27.4 %attend.1 = (bf16[1024,1024]{1,0:T(8,128)(2,1)}, bf16[3,1024,1024]{2,1,0:T(8,128)(2,1)}) custom-call(s32[2]{0:T(128)} %pad_add_fusion.info_ref, f32[3,512,1024]{2,1,0:T(8,128)} %convolution_bitcast_fusion.1.own_ref, f32[3,512,1024]{2,1,0:T(8,128)} %convolution_bitcast_fusion.other_ref, f32[1024,128]{1,0:T(8,128)} %get-tuple-element.193.cos_ref, ...), custom_call_target="tpu_custom_call" | custom-call | flops 8589934592 | bytes 20971520 | tf_op jit(solution)/shard_map/attend/pallas_call | solution.py:120
  100.5 45.1 %collective-permute-done.1 = bf16[512,2048]{1,0:T(8,128)(2,1)S(1)} collective-permute-done((bf16[512,2048]{1,0:T(8,128)(2,1)S(1)}, bf16[512,2048]{1,0:T(8,128)(2,1)S(1)}, u32[]{:S(2)}, u32[]{:S(2)}) %collective-permute-start.1) | collective-permute-done | bytes 2097184 | tf_op jit(solution)/shard_map/ppermute | solution.py:197
  159.4 36.5 %collective-permute-done.6 = f32[8,128]{1,0:T(8,128)S(1)} collective-permute-done((f32[8,128]{1,0:T(8,128)S(1)}, f32[8,128]{1,0:T(8,128)S(1)}, u32[]{:S(2)}, u32[]{:S(2)}) %collective-permute-start.6) | collective-permute-done | bytes 4128 | tf_op jit(solution)/shard_map/ppermute | solution.py:210
  197.2 21.4 %fusion.4 = f32[512,2,2816]{2,0,1:T(8,128)} fusion(bf16[2048,2,2816]{2,1,0:T(2,128)(2,1)} %param.20, bf16[512,2048]{1,0:T(8,128)(2,1)} %collective-permute-done.2), kind=kOutput, calls=%fused_computation.4 | convolution fusion | flops 11811160064 | bytes 36700160 | tf_op jit(solution)/shard_map/td,dke->tke/dot_general | solution.py:343
  227.0 11.0 convolution_convert_fusion.7
  239.2 29.2 %fusion.6 = f32[512,2,2816]{2,0,1:T(8,128)} fusion(bf16[2048,2,2816]{2,1,0:T(2,128)(2,1)} %param.20, bf16[512,2048]{1,0:T(8,128)(2,1)S(1)} %fusion.35), kind=kOutput, calls=%fused_computation.6 | convolution fusion | flops 11811160064 | bytes 36700160 | tf_op jit(solution)/shard_map/td,dke->tke/dot_general | solution.py:343
  306.6 40.8 %collective-permute-done.7 = bf16[512,2048]{1,0:T(8,128)(2,1)} collective-permute-done((bf16[512,2048]{1,0:T(8,128)(2,1)}, bf16[512,2048]{1,0:T(8,128)(2,1)}, u32[]{:S(2)}, u32[]{:S(2)}) %collective-permute-start.7) | collective-permute-done | bytes 2097184 | tf_op jit(solution)/shard_map/ppermute | solution.py:185
  359.5 15.1 %fusion.46 = (bf16[1,512,2816]{2,1,0:T(8,128)(2,1)}, bf16[1,512,2816]{2,1,0:T(8,128)(2,1)}) fusion(f32[512,2816]{1,0:T(8,128)} %get-tuple-element.73, f32[512,2816]{1,0:T(8,128)} %get-tuple-element.74, bf16[512,2048]{1,0:T(8,128)(2,1)} %collective-permute-done.7, bf16[2816,2048]{1,0:T(8,128)(2,1)} %param.21), kind=kOutput, calls=%fused_computation.128 | convolution fusion | flops 5911347200 | bytes 30932992 | tf_op jit(solution)/shard_map/dot_general | solution.py:368
  380.4 15.1 %fusion.44 = (bf16[1,512,2816]{2,1,0:T(8,128)(2,1)}, bf16[1,512,2816]{2,1,0:T(8,128)(2,1)}) fusion(f32[512,2816]{1,0:T(8,128)} %get-tuple-element.68, f32[512,2816]{1,0:T(8,128)} %get-tuple-element.69, bf16[512,2048]{1,0:T(8,128)(2,1)} %fusion.218, bf16[2816,2048]{1,0:T(8,128)(2,1)} %param.21), kind=kOutput, calls=%fused_computation.126 | convolution fusion | flops 5911347200 | bytes 30932992 | tf_op jit(solution)/shard_map/dot_general | solution.py:368
  413.6 22.1 %bitcast_convert_fusion.1 = bf16[512,2048]{1,0:T(8,128)(2,1)} fusion(bf16[2,512,2816]{2,1,0:T(8,128)(2,1)} %pad_maximum_fusion.1, bf16[2048,2,2816]{2,1,0:T(2,128)(2,1)} %param.20), kind=kOutput, calls=%fused_computation.106 | convolution fusion | flops 11812208640 | bytes 30932992 | tf_op jit(solution)/shard_map/kte,dke->td/dot_general | solution.py:382
  469.2 14.4 %collective-permute-done.10 = bf16[512,2048]{1,0:T(8,128)(2,1)} collective-permute-done((bf16[512,2048]{1,0:T(8,128)(2,1)}, bf16[512,2048]{1,0:T(8,128)(2,1)}, u32[]{:S(2)}, u32[]{:S(2)}) %collective-permute-start.10) | collective-permute-done | bytes 2097184 | tf_op jit(solution)/shard_map/ppermute | solution.py:197
  483.6 22.4 %bitcast_add_fusion.1 = f32[512,2048]{1,0:T(8,128)} fusion(bf16[512,2048]{1,0:T(8,128)(2,1)} %collective-permute-done.10, bf16[2048,2,2816]{2,1,0:T(2,128)(2,1)} %param.20, bf16[1,512,2816]{2,1,0:T(8,128)(2,1)} %get-tuple-element.160, bf16[1,512,2816]{2,1,0:T(8,128)(2,1)} %get-tuple-element.159), kind=kOutput, calls=%fused_computation.107 | convolution fusion | flops 11816140800 | bytes 35127296 | tf_op jit(solution)/shard_map/kte,dke->td/dot_general | solution.py:382
  562.2 16.1 %collective-permute-done.18 = bf16[2,2816,128]{2,1,0:T(8,128)(2,1)S(1)} collective-permute-done((bf16[2,2816,128]{2,1,0:T(8,128)(2,1)S(1)}, bf16[2,2816,128]{2,1,0:T(8,128)(2,1)S(1)}, u32[]{:S(2)}, u32[]{:S(2)}) %collective-permute-start.18) | collective-permute-done | bytes 1441824 | tf_op jit(solution)/shard_map/ppermute | solution.py:257
  578.6 27.5 %collective-permute-done.17 = bf16[512,2816]{1,0:T(8,128)(2,1)} collective-permute-done((bf16[512,2816]{1,0:T(8,128)(2,1)}, bf16[512,2816]{1,0:T(8,128)(2,1)}, u32[]{:S(2)}, u32[]{:S(2)}) %collective-permute-start.17) | collective-permute-done | bytes 2883616 | tf_op jit(solution)/shard_map/ppermute | solution.py:242
  628.9 25.6 %collective-permute-done.23 = bf16[2816,128]{1,0:T(8,128)(2,1)S(1)} collective-permute-done((bf16[2816,128]{1,0:T(8,128)(2,1)S(1)}, bf16[2816,128]{1,0:T(8,128)(2,1)S(1)}, u32[]{:S(2)}, u32[]{:S(2)}) %collective-permute-start.23) | collective-permute-done | bytes 720928 | tf_op jit(solution)/shard_map/ppermute | solution.py:262
  664.0 43.1 %attend_back.1 = bf16[3,1024,1024]{2,1,0:T(8,128)(2,1)} custom-call(s32[2]{0:T(128)} %pad_add_fusion.info_ref, bf16[3,1024,1024]{2,1,0:T(8,128)(2,1)} %get-tuple-element.79.qkv_ref, bf16[1024,1024]{1,0:T(8,128)(2,1)} %pad_maximum_fusion.2.grad_ref, f32[1024,128]{1,0:T(8,128)} %get-tuple-element.193.cos_ref, f32[1024,128]{1,0:T(8,128)} %get-tuple-element.194.sin_ref), custom_call_target="tpu_custom_call" | custom-call | flops 21474836480 | bytes 14680064 | tf_op jit(solution)/shard_map/attend_back/pallas_call | solution.py:154
  720.5 28.8 %collective-permute-done.31 = bf16[512,1024]{1,0:T(8,128)(2,1)S(1)} collective-permute-done((bf16[512,1024]{1,0:T(8,128)(2,1)}, bf16[512,1024]{1,0:T(8,128)(2,1)S(1)}, u32[]{:S(2)}, u32[]{:S(2)}) %collective-permute-start.31) | collective-permute-done | bytes 1048608 | tf_op jit(solution)/shard_map/ppermute | solution.py:242
  773.0 81.9 %collective-permute-done.32 = bf16[2,128,2816]{2,1,0:T(8,128)(2,1)S(1)} collective-permute-done((bf16[2,128,2816]{2,1,0:T(8,128)(2,1)S(1)}, bf16[2,128,2816]{2,1,0:T(8,128)(2,1)S(1)}, u32[]{:S(2)}, u32[]{:S(2)}) %collective-permute-start.32) | collective-permute-done | bytes 1441824 | tf_op jit(solution)/shard_map/ppermute | solution.py:257
  862.2 20.4 %collective-permute-done.38 = bf16[2,128,1024]{2,1,0:T(8,128)(2,1)S(1)} collective-permute-done((bf16[2,128,1024]{2,1,0:T(8,128)(2,1)S(1)}, bf16[2,128,1024]{2,1,0:T(8,128)(2,1)S(1)}, u32[]{:S(2)}, u32[]{:S(2)}) %collective-permute-start.38) | collective-permute-done | bytes 524320 | tf_op jit(solution)/shard_map/ppermute | solution.py:257
  907.4 20.7 %collective-permute-done.35 = bf16[512,1024]{1,0:T(8,128)(2,1)S(1)} collective-permute-done((bf16[512,1024]{1,0:T(8,128)(2,1)S(1)}, bf16[512,1024]{1,0:T(8,128)(2,1)S(1)}, u32[]{:S(2)}, u32[]{:S(2)}) %collective-permute-start.35) | collective-permute-done | bytes 1048608 | tf_op jit(solution)/shard_map/ppermute | solution.py:242
  935.6 19.0 %collective-permute-done.40 = bf16[2,128,1024]{2,1,0:T(8,128)(2,1)S(1)} collective-permute-done((bf16[2,128,1024]{2,1,0:T(8,128)(2,1)S(1)}, bf16[2,128,1024]{2,1,0:T(8,128)(2,1)S(1)}, u32[]{:S(2)}, u32[]{:S(2)}) %collective-permute-start.40) | collective-permute-done | bytes 524320 | tf_op jit(solution)/shard_map/ppermute | solution.py:257
  954.9 22.2 %collective-permute-done.42 = bf16[2,128,1024]{2,1,0:T(8,128)(2,1)S(1)} collective-permute-done((bf16[2,128,1024]{2,1,0:T(8,128)(2,1)S(1)}, bf16[2,128,1024]{2,1,0:T(8,128)(2,1)S(1)}, u32[]{:S(2)}, u32[]{:S(2)}) %collective-permute-start.42) | collective-permute-done | bytes 524320 | tf_op jit(solution)/shard_map/ppermute | solution.py:257
  977.4 17.2 %collective-permute-done.44 = bf16[2,128,1024]{2,1,0:T(8,128)(2,1)S(1)} collective-permute-done((bf16[2,128,1024]{2,1,0:T(8,128)(2,1)S(1)}, bf16[2,128,1024]{2,1,0:T(8,128)(2,1)S(1)}, u32[]{:S(2)}, u32[]{:S(2)}) %collective-permute-start.44) | collective-permute-done | bytes 524320 | tf_op jit(solution)/shard_map/ppermute | solution.py:257
  1000.1 11.4 collective-permute-done.45
  1012.8 11.8 bitcast_convert_fusion
  1042.3 28.9 %collective-permute-done.50 = f32[4,2048]{1,0:T(4,128)S(1)} collective-permute-done((f32[4,2048]{1,0:T(4,128)S(1)}, f32[4,2048]{1,0:T(4,128)S(1)}, u32[]{:S(2)}, u32[]{:S(2)}) %collective-permute-start.50) | collective-permute-done | bytes 32800 | tf_op jit(solution)/shard_map/ppermute | solution.py:210
  1071.8 14.4 %fusion.34 = f32[1,512,2048]{2,1,0:T(8,128)} fusion(bf16[512,2048]{1,0:T(8,128)(2,1)S(1)} %collective-permute-done.24, f32[512,2048]{1,0:T(8,128)} %get-tuple-element.137, bf16[2048,3,1024]{2,0,1:T(8,128)(2,1)} %param.16, bf16[3,1024,1024]{2,1,0:T(8,128)(2,1)} %attend_back.1), kind=kOutput, calls=%fused_computation.105 | convolution fusion | flops 6446645248 | bytes 26214400 | tf_op jit(solution)/shard_map/kte,dke->td/dot_general | solution.py:440
  1116.9 45.2 %copy.31 = f32[2048,2,2816]{2,1,0:T(2,128)} copy(bf16[2048,2,2816]{2,0,1:T(8,128)(2,1)} %all-gather.7.cloned.1.call-done) | data formatting | bytes 69206016
  1162.1 68.5 %all-gather.5.cloned.1.call-done = bf16[2048,4,1024]{2,0,1:T(8,128)(2,1)} async-done(((bf16[128,4,1024]{2,0,1:T(8,128)(2,1)}), bf16[2048,4,1024]{2,0,1:T(8,128)(2,1)}) %all-gather.5.cloned.1.call-update) | async-done | bytes 16777232 | tf_op jit(solution)/shard_map/all_gather | solution.py:267
  1246.4 14.2 %slice_convert_fusion = f32[2048,3,1024]{2,0,1:T(8,128)} fusion(bf16[2048,4,1024]{2,0,1:T(8,128)(2,1)} %all-gather.5.cloned.1.call-done), kind=kLoop, calls=%fused_computation.8 | loop fusion | flops 6291456 | bytes 37748736 | tf_op jit(solution)/shard_map/convert_element_type | solution.py:463
  (356 shorter events, 391.9 us)
Async XLA Ops:
  7.2 1004.4 %all-gather.9.cloned.1.call-start = ((), (), s32[]{:S(2)}) async-start(), calls=%async_computation.2 | async-start | bytes 12255232 | tf_op jit(solution)/shard_map/all_gather | solution.py:271
  7.2 49.0 %collective-permute-start = (bf16[512,2048]{1,0:T(8,128)(2,1)}, bf16[512,2048]{1,0:T(8,128)(2,1)}, u32[]{:S(2)}, u32[]{:S(2)}) collective-permute-start(bf16[512,2048]{1,0:T(8,128)(2,1)} %bitcast.379), channel_id=1, source_target_pairs={{0,1},{1,0},{2,3},{3,2},{4,5},{5,4},{6,7},{7,6},{8,9},{9,8},{10,11... | collective-permute-start | bytes 6291464 | tf_op jit(solution)/shard_map/ppermute | solution.py:185
  98.7 46.9 %collective-permute-start.1 = (bf16[512,2048]{1,0:T(8,128)(2,1)S(1)}, bf16[512,2048]{1,0:T(8,128)(2,1)S(1)}, u32[]{:S(2)}, u32[]{:S(2)}) collective-permute-start(bf16[512,2048]{1,0:T(8,128)(2,1)S(1)} %convolution_convert_fusion.6), channel_id=1, source_target_pairs={{0,1},{1,0},{2,3},{3,2},{4,5},{5,4},{6,7},{7,6},{8,9},{9,8},{10,11... | collective-permute-start | bytes 6291464 | tf_op jit(solution)/shard_map/ppermute | solution.py:197
  149.8 47.4 %collective-permute-start.2 = (bf16[512,2048]{1,0:T(8,128)(2,1)S(1)}, bf16[512,2048]{1,0:T(8,128)(2,1)}, u32[]{:S(2)}, u32[]{:S(2)}) collective-permute-start(bf16[512,2048]{1,0:T(8,128)(2,1)S(1)} %fusion.35), channel_id=1, source_target_pairs={{0,1},{1,0},{2,3},{3,2},{4,5},{5,4},{6,7},{7,6},{8,9},{9,8},{10,11... | collective-permute-start | bytes 6291464 | tf_op jit(solution)/shard_map/ppermute | solution.py:185
  158.8 37.2 %collective-permute-start.6 = (f32[8,128]{1,0:T(8,128)S(1)}, f32[8,128]{1,0:T(8,128)S(1)}, u32[]{:S(2)}, u32[]{:S(2)}) collective-permute-start(f32[8,128]{1,0:T(8,128)S(1)} %fusion.265), channel_id=1, source_target_pairs={{0,1},{1,0},{2,3},{3,2},{4,5},{5,4},{6,7},{7,6},{8,9},{9,8},{10,11... | collective-permute-start | bytes 12296 | tf_op jit(solution)/shard_map/ppermute | solution.py:210
  238.0 45.4 %collective-permute-start.3 = (bf16[512,2048]{1,0:T(8,128)(2,1)}, bf16[512,2048]{1,0:T(8,128)(2,1)}, u32[]{:S(2)}, u32[]{:S(2)}) collective-permute-start(bf16[512,2048]{1,0:T(8,128)(2,1)} %convolution_convert_fusion.7), channel_id=1, source_target_pairs={{0,1},{1,0},{2,3},{3,2},{4,5},{5,4},{6,7},{7,6},{8,9},{9,8},{10,11... | collective-permute-start | bytes 6291464 | tf_op jit(solution)/shard_map/ppermute | solution.py:197
  302.8 44.6 %collective-permute-start.7 = (bf16[512,2048]{1,0:T(8,128)(2,1)}, bf16[512,2048]{1,0:T(8,128)(2,1)}, u32[]{:S(2)}, u32[]{:S(2)}) collective-permute-start(bf16[512,2048]{1,0:T(8,128)(2,1)} %fusion.218), channel_id=1, source_target_pairs={{0,1},{1,0},{2,3},{3,2},{4,5},{5,4},{6,7},{7,6},{8,9},{9,8},{10,11... | collective-permute-start | bytes 6291464 | tf_op jit(solution)/shard_map/ppermute | solution.py:185
  359.0 45.1 %collective-permute-start.9 = (bf16[2816,512]{1,0:T(8,128)(2,1)}, bf16[2816,512]{1,0:T(8,128)(2,1)}, u32[]{:S(2)}, u32[]{:S(2)}) collective-permute-start(bf16[2816,512]{1,0:T(8,128)(2,1)} %convolution_convert_fusion.4), channel_id=1, source_target_pairs={{0,2},{2,0},{4,6},{6,4},{1,3},{3,1},{5,7},{7,5},{8,10},{10,8},{12,... | collective-permute-start | bytes 8650760 | tf_op jit(solution)/shard_map/ppermute | solution.py:236
  435.8 47.8 %collective-permute-start.10 = (bf16[512,2048]{1,0:T(8,128)(2,1)}, bf16[512,2048]{1,0:T(8,128)(2,1)}, u32[]{:S(2)}, u32[]{:S(2)}) collective-permute-start(bf16[512,2048]{1,0:T(8,128)(2,1)} %bitcast_convert_fusion.1), channel_id=1, source_target_pairs={{0,1},{1,0},{2,3},{3,2},{4,5},{5,4},{6,7},{7,6},{8,9},{9,8},{10,11... | collective-permute-start | bytes 6291464 | tf_op jit(solution)/shard_map/ppermute | solution.py:197
  449.3 56.8 %collective-permute-start.11 = (bf16[512,2816]{1,0:T(8,128)(2,1)}, bf16[512,2816]{1,0:T(8,128)(2,1)}, u32[]{:S(2)}, u32[]{:S(2)}) collective-permute-start(bf16[512,2816]{1,0:T(8,128)(2,1)} %convolution_convert_fusion.3), channel_id=1, source_target_pairs={{0,2},{2,0},{4,6},{6,4},{1,3},{3,1},{5,7},{7,5},{8,10},{10,8},{12,... | collective-permute-start | bytes 8650760 | tf_op jit(solution)/shard_map/ppermute | solution.py:235
  455.2 59.5 %collective-permute-start.12 = (bf16[512,2816]{1,0:T(8,128)(2,1)}, bf16[512,2816]{1,0:T(8,128)(2,1)}, u32[]{:S(2)}, u32[]{:S(2)}) collective-permute-start(bf16[512,2816]{1,0:T(8,128)(2,1)} %convolution_convert_fusion.2), channel_id=1, source_target_pairs={{0,2},{2,0},{4,6},{6,4},{1,3},{3,1},{5,7},{7,5},{8,10},{10,8},{12,... | collective-permute-start | bytes 8650760 | tf_op jit(solution)/shard_map/ppermute | solution.py:236
  455.7 66.4 %collective-permute-start.13 = (bf16[2816,512]{1,0:T(8,128)(2,1)}, bf16[2816,512]{1,0:T(8,128)(2,1)}, u32[]{:S(2)}, u32[]{:S(2)}) collective-permute-start(bf16[2816,512]{1,0:T(8,128)(2,1)} %add_convert_fusion.2), channel_id=1, source_target_pairs={{0,4},{4,0},{2,6},{6,2},{1,5},{5,1},{3,7},{7,3},{8,12},{12,8},{10,... | collective-permute-start | bytes 8650760 | tf_op jit(solution)/shard_map/ppermute | solution.py:242
  463.1 83.4 %collective-permute-start.15 = (bf16[512,2816]{1,0:T(8,128)(2,1)}, bf16[512,2816]{1,0:T(8,128)(2,1)}, u32[]{:S(2)}, u32[]{:S(2)}) collective-permute-start(bf16[512,2816]{1,0:T(8,128)(2,1)} %convolution_convert_fusion.1), channel_id=1, source_target_pairs={{0,2},{2,0},{4,6},{6,4},{1,3},{3,1},{5,7},{7,5},{8,10},{10,8},{12,... | collective-permute-start | bytes 8650760 | tf_op jit(solution)/shard_map/ppermute | solution.py:235
  483.6 69.5 %collective-permute-start.16 = (bf16[512,2816]{1,0:T(8,128)(2,1)}, bf16[512,2816]{1,0:T(8,128)(2,1)}, u32[]{:S(2)}, u32[]{:S(2)}) collective-permute-start(bf16[512,2816]{1,0:T(8,128)(2,1)} %convolution_convert_fusion), channel_id=1, source_target_pairs={{0,2},{2,0},{4,6},{6,4},{1,3},{3,1},{5,7},{7,5},{8,10},{10,8},{12,... | collective-permute-start | bytes 8650760 | tf_op jit(solution)/shard_map/ppermute | solution.py:236
  540.6 67.9 %collective-permute-start.14 = (bf16[512,2048]{1,0:T(8,128)(2,1)S(1)}, bf16[512,2048]{1,0:T(8,128)(2,1)S(1)}, u32[]{:S(2)}, u32[]{:S(2)}) collective-permute-start(bf16[512,2048]{1,0:T(8,128)(2,1)S(1)} %get-tuple-element.84), channel_id=1, source_target_pairs={{0,1},{1,0},{2,3},{3,2},{4,5},{5,4},{6,7},{7,6},{8,9},{9,8},{10,11... | collective-permute-start | bytes 6291464 | tf_op jit(solution)/shard_map/ppermute | solution.py:185
  541.2 64.9 %collective-permute-start.17 = (bf16[512,2816]{1,0:T(8,128)(2,1)}, bf16[512,2816]{1,0:T(8,128)(2,1)}, u32[]{:S(2)}, u32[]{:S(2)}) collective-permute-start(bf16[512,2816]{1,0:T(8,128)(2,1)} %add_convert_fusion.1), channel_id=1, source_target_pairs={{0,4},{4,0},{2,6},{6,2},{1,5},{5,1},{3,7},{7,3},{8,12},{12,8},{10,... | collective-permute-start | bytes 8650760 | tf_op jit(solution)/shard_map/ppermute | solution.py:242
  617.9 37.8 %collective-permute-start.19 = (bf16[512,1024]{1,0:T(8,128)(2,1)}, bf16[512,1024]{1,0:T(8,128)(2,1)}, u32[]{:S(2)}, u32[]{:S(2)}) collective-permute-start(bf16[512,1024]{1,0:T(8,128)(2,1)} %convolution_convert_fusion.9), channel_id=1, source_target_pairs={{0,2},{2,0},{4,6},{6,4},{1,3},{3,1},{5,7},{7,5},{8,10},{10,8},{12,... | collective-permute-start | bytes 3145736 | tf_op jit(solution)/shard_map/ppermute | solution.py:235
  617.9 42.1 %collective-permute-start.20 = (bf16[512,1024]{1,0:T(8,128)(2,1)}, bf16[512,1024]{1,0:T(8,128)(2,1)}, u32[]{:S(2)}, u32[]{:S(2)}) collective-permute-start(bf16[512,1024]{1,0:T(8,128)(2,1)} %convolution_convert_fusion.8), channel_id=1, source_target_pairs={{0,2},{2,0},{4,6},{6,4},{1,3},{3,1},{5,7},{7,5},{8,10},{10,8},{12,... | collective-permute-start | bytes 3145736 | tf_op jit(solution)/shard_map/ppermute | solution.py:236
  618.4 92.2 %collective-permute-start.21 = (bf16[512,2816]{1,0:T(8,128)(2,1)}, bf16[512,2816]{1,0:T(8,128)(2,1)}, u32[]{:S(2)}, u32[]{:S(2)}) collective-permute-start(bf16[512,2816]{1,0:T(8,128)(2,1)} %add_convert_fusion), channel_id=1, source_target_pairs={{0,4},{4,0},{2,6},{6,2},{1,5},{5,1},{3,7},{7,3},{8,12},{12,8},{10,... | collective-permute-start | bytes 8650760 | tf_op jit(solution)/shard_map/ppermute | solution.py:242
  624.0 83.1 %collective-permute-start.22 = (bf16[2,128,2816]{2,1,0:T(8,128)(2,1)}, bf16[2,128,2816]{2,1,0:T(8,128)(2,1)S(1)}, u32[]{:S(2)}, u32[]{:S(2)}) collective-permute-start(bf16[2,128,2816]{2,1,0:T(8,128)(2,1)} %pad_maximum_fusion.4), channel_id=1, source_target_pairs={{0,8},{8,0},{16,24},{24,16},{1,9},{9,1},{17,25},{25,17},{2,10},{10... | collective-permute-start | bytes 4325384 | tf_op jit(solution)/shard_map/ppermute | solution.py:257
  717.3 399.6 %all-gather.7.cloned.1.call-start = ((), (), s32[]{:S(2)}) async-start(), calls=%async_computation.1 | async-start | bytes 24510464 | tf_op jit(solution)/shard_map/all_gather | solution.py:267
  761.2 93.6 %collective-permute-start.32 = (bf16[2,128,2816]{2,1,0:T(8,128)(2,1)S(1)}, bf16[2,128,2816]{2,1,0:T(8,128)(2,1)S(1)}, u32[]{:S(2)}, u32[]{:S(2)}) collective-permute-start(bf16[2,128,2816]{2,1,0:T(8,128)(2,1)S(1)} %pad_maximum_fusion.5), channel_id=1, source_target_pairs={{0,8},{8,0},{16,24},{24,16},{1,9},{9,1},{17,25},{25,17},{2,10},{10... | collective-permute-start | bytes 4325384 | tf_op jit(solution)/shard_map/ppermute | solution.py:257
  764.2 94.2 %collective-permute-start.36 = (bf16[128,2816]{1,0:T(8,128)(2,1)S(1)}, bf16[128,2816]{1,0:T(8,128)(2,1)S(1)}, u32[]{:S(2)}, u32[]{:S(2)}) collective-permute-start(bf16[128,2816]{1,0:T(8,128)(2,1)S(1)} %fusion.164), channel_id=1, source_target_pairs={{0,16},{16,0},{8,24},{24,8},{1,17},{17,1},{9,25},{25,9},{2,18},{18... | collective-permute-start | bytes 2162696 | tf_op jit(solution)/shard_map/ppermute | solution.py:262
  855.2 39.9 %collective-permute-start.37 = (bf16[128,2816]{1,0:T(8,128)(2,1)S(1)}, bf16[128,2816]{1,0:T(8,128)(2,1)S(1)}, u32[]{:S(2)}, u32[]{:S(2)}) collective-permute-start(bf16[128,2816]{1,0:T(8,128)(2,1)S(1)} %fusion.165), channel_id=1, source_target_pairs={{0,16},{16,0},{8,24},{24,8},{1,17},{17,1},{9,25},{25,9},{2,18},{18... | collective-permute-start | bytes 2162696 | tf_op jit(solution)/shard_map/ppermute | solution.py:262
  858.6 42.2 %collective-permute-start.33 = (bf16[512,1024]{1,0:T(8,128)(2,1)S(1)}, bf16[512,1024]{1,0:T(8,128)(2,1)S(1)}, u32[]{:S(2)}, u32[]{:S(2)}) collective-permute-start(bf16[512,1024]{1,0:T(8,128)(2,1)S(1)} %add_convert_fusion.6), channel_id=1, source_target_pairs={{0,4},{4,0},{2,6},{6,2},{1,5},{5,1},{3,7},{7,3},{8,12},{12,8},{10,... | collective-permute-start | bytes 3145736 | tf_op jit(solution)/shard_map/ppermute | solution.py:242
  860.1 47.0 %collective-permute-start.34 = (bf16[512,1024]{1,0:T(8,128)(2,1)S(1)}, bf16[512,1024]{1,0:T(8,128)(2,1)S(1)}, u32[]{:S(2)}, u32[]{:S(2)}) collective-permute-start(bf16[512,1024]{1,0:T(8,128)(2,1)S(1)} %add_convert_fusion.5), channel_id=1, source_target_pairs={{0,4},{4,0},{2,6},{6,2},{1,5},{5,1},{3,7},{7,3},{8,12},{12,8},{10,... | collective-permute-start | bytes 3145736 | tf_op jit(solution)/shard_map/ppermute | solution.py:242
  860.6 67.5 %collective-permute-start.35 = (bf16[512,1024]{1,0:T(8,128)(2,1)S(1)}, bf16[512,1024]{1,0:T(8,128)(2,1)S(1)}, u32[]{:S(2)}, u32[]{:S(2)}) collective-permute-start(bf16[512,1024]{1,0:T(8,128)(2,1)S(1)} %add_convert_fusion.4), channel_id=1, source_target_pairs={{0,4},{4,0},{2,6},{6,2},{1,5},{5,1},{3,7},{7,3},{8,12},{12,8},{10,... | collective-permute-start | bytes 3145736 | tf_op jit(solution)/shard_map/ppermute | solution.py:242
  931.0 299.6 %all-gather.5.cloned.1.call-start = ((), (), s32[]{:S(2)}) async-start(), calls=%async_computation | async-start | bytes 17825792 | tf_op jit(solution)/shard_map/all_gather | solution.py:267
  933.0 44.0 %collective-permute-start.42 = (bf16[2,128,1024]{2,1,0:T(8,128)(2,1)S(1)}, bf16[2,128,1024]{2,1,0:T(8,128)(2,1)S(1)}, u32[]{:S(2)}, u32[]{:S(2)}) collective-permute-start(bf16[2,128,1024]{2,1,0:T(8,128)(2,1)S(1)} %pad_maximum_fusion.12), channel_id=1, source_target_pairs={{0,8},{8,0},{16,24},{24,16},{1,9},{9,1},{17,25},{25,17},{2,10},{10... | collective-permute-start | bytes 1572872 | tf_op jit(solution)/shard_map/ppermute | solution.py:257
  935.3 59.3 %collective-permute-start.44 = (bf16[2,128,1024]{2,1,0:T(8,128)(2,1)S(1)}, bf16[2,128,1024]{2,1,0:T(8,128)(2,1)S(1)}, u32[]{:S(2)}, u32[]{:S(2)}) collective-permute-start(bf16[2,128,1024]{2,1,0:T(8,128)(2,1)S(1)} %pad_maximum_fusion.13), channel_id=1, source_target_pairs={{0,8},{8,0},{16,24},{24,16},{1,9},{9,1},{17,25},{25,17},{2,10},{10... | collective-permute-start | bytes 1572872 | tf_op jit(solution)/shard_map/ppermute | solution.py:257
  954.8 40.0 %collective-permute-start.41 = (bf16[128,1024]{1,0:T(8,128)(2,1)S(1)}, bf16[128,1024]{1,0:T(8,128)(2,1)S(1)}, u32[]{:S(2)}, u32[]{:S(2)}) collective-permute-start(bf16[128,1024]{1,0:T(8,128)(2,1)S(1)} %fusion.183), channel_id=1, source_target_pairs={{0,16},{16,0},{8,24},{24,8},{1,17},{17,1},{9,25},{25,9},{2,18},{18... | collective-permute-start | bytes 786440 | tf_op jit(solution)/shard_map/ppermute | solution.py:262
  1024.5 47.2 %collective-permute-start.24 = (bf16[512,2048]{1,0:T(8,128)(2,1)}, bf16[512,2048]{1,0:T(8,128)(2,1)S(1)}, u32[]{:S(2)}, u32[]{:S(2)}) collective-permute-start(bf16[512,2048]{1,0:T(8,128)(2,1)} %bitcast_convert_fusion), channel_id=1, source_target_pairs={{0,1},{1,0},{2,3},{3,2},{4,5},{5,4},{6,7},{7,6},{8,9},{9,8},{10,11... | collective-permute-start | bytes 6291464 | tf_op jit(solution)/shard_map/ppermute | solution.py:197
  (79 other events, 1989.7 us)
Sparse Core Ops, SparseCore 0:
  717.4 133.2 all-gather.8
  931.1 171.3 all-gather.6
  1105.3 125.2 all-gather.4
